TPU v7x, 32 devices: a whole 2x2x4 slice. The times are simulated.
32 devices in a mesh: dp: 16 (over z, y, x), mp: 2 (over core).
Axes of the slice: x: 2, y: 2, z: 4, core: 2. Of those that a mesh axis runs over, the one named last changes fastest.
Arguments:
- tokens: bfloat16 [16384, 768], P('dp'), may hold values from -6 to 6
- cotangent: bfloat16 [16384, 768], P('dp'), may hold values from -6 to 6
- lengths: int32 [16, 16], P('dp'), may hold values from 0 to 900, as said below
- ln1_gain: float32 [768], replicated, may hold values from 0.5 to 1.5
- ln1_bias: float32 [768], replicated, may hold values from -1.5 to 1.5
- qkv_weight: bfloat16 [768, 3, 768], P(None, None, 'mp'), may hold values from -0.21875 to 0.21875
- qv_bias: float32 [2, 768], P(None, 'mp'), may hold values from -2.5 to 2.5
- out_weight: bfloat16 [768, 768], P('mp'), may hold values from -0.875 to 0.875
- out_bias: float32 [768], replicated, may hold values from -1.5 to 1.5
- ln2_gain: float32 [768], replicated, may hold values from 0.5 to 1.5
- ln2_bias: float32 [768], replicated, may hold values from -1.5 to 1.5
- up_weight: bfloat16 [768, 3072], P(None, 'mp'), may hold values from -0.21875 to 0.21875
- up_bias: float32 [3072], P('mp'), may hold values from -2.5 to 2.5
- down_weight: bfloat16 [3072, 768], P('mp'), may hold values from -0.109375 to 0.109375
- down_bias: float32 [768], replicated, may hold values from -1.5 to 1.5
Outputs:
- output: bfloat16 [16384, 768], P('dp')
- tokens_grad: float32 [16384, 768], P('dp')
- ln1_gain_grad: float32 [768], replicated
- ln1_bias_grad: float32 [768], replicated
- qkv_weight_grad: float32 [768, 3, 768], P('dp', None, 'mp')
- qv_bias_grad: float32 [2, 768], P(None, 'mp')
- out_weight_grad: float32 [768, 768], P('mp', 'dp')
- out_bias_grad: float32 [768], replicated
- ln2_gain_grad: float32 [768], replicated
- ln2_bias_grad: float32 [768], replicated
- up_weight_grad: float32 [768, 3072], P('dp', 'mp')
- up_bias_grad: float32 [3072], P('mp')
- down_weight_grad: float32 [3072, 768], P('mp', 'dp')
- down_bias_grad: float32 [768], replicated
Inputs may be any that keep to these rules, and one draw needn't show every extreme that they name: Each length is 0 or the square of one of 30, 15, 10, 6, 5. The lengths of one index of dp sum to at most 1024; its images lie one after another from its row 0 in slot order, and its remaining rows are padding.
All inputs are finite; a program needn't handle non-finite values.
Results may differ from a plain program's by a relative error of at most 0.012.
The roundings to bfloat16 on the way count: a program that leaves them out, or rounds other values in their place, can miss the bound.
Values may be sent and summed in bfloat16 or wider, within the bound.
No kernel may reach another device: no remote copies, remote signals or barrier semaphores. Data moves between devices by JAX's collectives and lax.ppermute only.
A program may use at most 192 MiB of HBM per device.

v0:
```python
import functools

import jax
import jax.numpy as jnp
from jax import lax
from jax.experimental import pallas as pl
from jax.experimental.pallas import tpu as pltpu
from jax.sharding import PartitionSpec as P

HEAD_DIM = 64
EPSILON = 1e-06
MASKED = 1e30
LANES = 128
TOTALS_AT = 32
bf16 = jnp.bfloat16
f32 = jnp.float32


class Given:
    def __init__(self, array, kind, pieces=1, columns=None):
        self.array, self.kind, self.pieces, self.columns = array, kind, pieces, columns

    @property
    def shape(self):
        if self.columns is None:
            return self.array.shape
        return (self.array.shape[0], self.columns[1])


class Made:
    def __init__(self, shape, dtype, kind, pieces=1, source=None):
        self.shape, self.dtype, self.kind, self.pieces, self.source = shape, dtype, kind, pieces, source


def piece_span(piece, rows):
    if isinstance(piece, int):
        return pl.ds(piece * rows, rows)
    return pl.ds(pl.multiple_of(piece * rows, rows), rows)


class Arriving:
    def __init__(self, ref, source=None, semaphores=None, pieces=1, columns=None):
        self.ref, self.source, self.semaphores, self.pieces = ref, source, semaphores, pieces
        self.pending, self.columns = source is not None, columns

    def copy(self, piece):
        span = piece_span(piece, self.ref.shape[0] // self.pieces)
        source = self.source.at[span]
        if self.columns is not None:
            source = self.source.at[span, pl.ds(*self.columns)]
        return pltpu.make_async_copy(source, self.ref.at[span], self.semaphores.at[piece])

    def ready(self, piece):
        if self.source is not None:
            self.pending = False
            self.copy(piece).wait()
        return self.ref

    def __call__(self):
        if self.pending:
            for piece in range(self.pieces):
                self.copy(piece).wait()
            self.pending = False
        return self.ref


class Leaving:
    def __init__(self, ref, target, semaphores, pieces):
        self.ref, self.target, self.semaphores, self.pieces = ref, target, semaphores, pieces
        self.started = False

    def copy(self, piece):
        span = piece_span(piece, self.ref.shape[0] // self.pieces)
        return pltpu.make_async_copy(
            self.ref.at[span], self.target.at[span], self.semaphores.at[piece]
        )

    def send(self, piece=0):
        self.started = True
        self.copy(piece).start()

    def finish(self):
        if not self.started:
            for piece in range(self.pieces):
                self.send(piece)

    def wait(self):
        for piece in range(self.pieces):
            self.copy(piece).wait()


class Staying:
    def __init__(self, ref):
        self.ref = ref

    def send(self, piece=0):
        pass


pins = {"v": pltpu.VMEM, "h": pltpu.HBM, "c": pltpu.HBM, "p": pltpu.VMEM, "q": pltpu.HBM}


def pinned(given):
    if given.kind in "sw":
        return given.array
    return pltpu.with_memory_space_constraint(given.array, pins[given.kind])


class Chain:
    last = None


def call(chain, kernel, name, outs, args, scratch=(), limit=9, covers=True):
    if chain.last is not None and all(g.array is not chain.last for g in args):
        args = [*args, Given(chain.last, "w")]
    ahead = [m for m in outs if m.kind == "p"]
    kernel_args = len(args)
    args = [*args, *(Given(m.source, "q") for m in ahead)]
    near = [g for g in args if g.kind == "h"]
    far = [m for m in outs if m.kind == "h"]
    copied = [m for m in outs if m.kind in "hc"]
    scratches = [pltpu.VMEM(g.shape, g.array.dtype) for g in near]
    scratches += [pltpu.VMEM(m.shape, m.dtype) for m in far]
    scratches += [pltpu.SemaphoreType.DMA((g.pieces,)) for g in near]
    scratches += [pltpu.SemaphoreType.DMA((m.pieces,)) for m in copied]
    scratches += [pltpu.SemaphoreType.DMA(()) for _ in ahead]

    def body(*refs):
        refs = list(refs)

        def take(count):
            taken = refs[:count]
            del refs[:count]
            return taken

        ins, results = take(len(args)), take(len(outs))
        arrivals, departures = take(len(near)), take(len(far))
        ready, gone = take(len(near)), take(len(copied))
        fetched = take(len(ahead))
        given, made, fetches = [], [], []
        for m, result in zip(outs, results):
            if m.kind == "p":
                source = ins[kernel_args + len(fetches)]
                fetches.append(pltpu.make_async_copy(source, result, fetched[len(fetches)]))
        for g, ref in zip(args, ins):
            if g.kind == "h":
                given.append(Arriving(arrivals.pop(0), ref, ready.pop(0), g.pieces, g.columns))
            elif g.kind not in "wq":
                given.append(ref if g.kind == "s" else Arriving(ref))
        waiting = [one for one in given if isinstance(one, Arriving) and one.pending]
        small = [one for one in waiting if len(one.ref.shape) == 1]
        pieced = [one for one in waiting if one.pieces > 1]
        order = [(one, 0) for one in small]
        for piece in range(max((one.pieces for one in pieced), default=0)):
            order += [(one, piece) for one in pieced if piece < one.pieces]
        order += [(one, 0) for one in waiting if one not in small and one not in pieced]
        for one, piece in order:
            one.copy(piece).start()
        for copy in fetches:
            copy.start()
        for m, ref in zip(outs, results):
            if m.kind == "h":
                made.append(Leaving(departures.pop(0), ref, gone.pop(0), m.pieces))
            elif m.kind == "p":
                continue
            elif m.kind == "c":
                made[-1] = Leaving(made[-1].ref, ref, gone.pop(0), m.pieces)
            else:
                made.append(Staying(ref))
        kernel(given, made, *refs)
        for one in waiting:
            one()
        leaving = [one for one in made if isinstance(one, Leaving)]
        for one in leaving:
            one.finish()
        for one in leaving:
            one.wait()
        for copy in fetches:
            copy.wait()

    spaces = {"s": pltpu.SMEM, "v": pltpu.VMEM, "h": pltpu.HBM, "c": pltpu.HBM, "w": pl.ANY, "p": pltpu.VMEM, "q": pltpu.HBM}
    results = pl.pallas_call(
        body,
        name=name,
        out_shape=tuple(pins[m.kind](m.shape, m.dtype) for m in outs),
        in_specs=[pl.BlockSpec(memory_space=spaces[g.kind]) for g in args],
        out_specs=tuple(pl.BlockSpec(memory_space=spaces[m.kind]) for m in outs),
        scratch_shapes=[*scratches, *scratch],
        compiler_params=pltpu.CompilerParams(vmem_limit_bytes=limit << 20),
        cost_estimate=pl.CostEstimate(flops=2 * 10**10 * covers, bytes_accessed=1, transcendentals=0),
    )(*(pinned(g) for g in args))
    chain.last = min(results, key=lambda result: result.size * result.dtype.itemsize)
    return results


def dot(a, b):
    return jnp.dot(a, b, preferred_element_type=f32)


def dot_t(a, b):
    return lax.dot_general(a, b, (((1,), (1,)), ((), ())), preferred_element_type=f32)


def lane_of(shape):
    return lax.broadcasted_iota(jnp.int32, shape, 1)


def head_half(values, half):
    return jnp.where(lane_of(values.shape) // HEAD_DIM == half, values, jnp.zeros_like(values))


def normalize(values):
    centered = values - jnp.mean(values, axis=-1, keepdims=True)
    variance = jnp.mean(centered * centered, axis=-1, keepdims=True)
    inverse = lax.rsqrt(variance + EPSILON)
    return centered * inverse, inverse


def norm_back(grad_out, normed, inverse, gain):
    scaled = grad_out * gain
    return inverse * (
        scaled
        - jnp.mean(scaled, axis=-1, keepdims=True)
        - normed * jnp.mean(scaled * normed, axis=-1, keepdims=True)
    )


def column_sum(values):
    return jnp.sum(values, axis=0, keepdims=True)


def rows_used(lengths):
    used = jnp.int32(0)
    for slot in range(lengths.shape[1]):
        used = used + lengths[0, slot]
    return used


def row_span(index, size):
    return pl.ds(pl.multiple_of(index * size, size), size)


def vector(ref):
    return ref[...][None, :]


def log_total_lanes(feature, head, log_total):
    lane = lane_of(feature.shape)
    rest = -log_total
    for piece in range(3):
        part_of = rest.astype(bf16).astype(f32)
        rest = rest - part_of
        feature = jnp.where(lane == TOTALS_AT + 3 * head + piece, part_of, feature)
    return feature


def attend(queries, keys, values, id_k, mixed, features, block):
    lane = lane_of((block, LANES))

    @pl.loop(0, queries.shape[0] // block)
    def _(index):
        span = row_span(index, block)
        ids = features[span, :]
        feature = ids.astype(f32)
        for pair in range(queries.shape[1] // LANES):
            cols = slice(pair * LANES, (pair + 1) * LANES)
            wide_keys = jnp.concatenate([keys[:, cols], id_k[...]], axis=1)
            query, value = queries[span, cols], values[:, cols]
            total = None
            inverses = []
            for half in range(2):
                wide_query = jnp.concatenate([head_half(query, half), ids], axis=1)
                exponent = jnp.exp(dot_t(wide_query, wide_keys))
                totals = jnp.sum(exponent, axis=1, keepdims=True)
                term = dot(exponent.astype(bf16), head_half(value, half))
                total = term if total is None else total + term
                inverses.append(1.0 / totals)
                feature = log_total_lanes(feature, 2 * pair + half, jnp.log(totals))
            mixed[span, cols] = (
                total * jnp.where(lane < HEAD_DIM, inverses[0], inverses[1])
            ).astype(bf16)
        features[span, :] = feature.astype(bf16)


def attend_shifted(queries, keys, values, id_k, mixed, features, block):
    @pl.loop(0, queries.shape[0] // block)
    def _(index):
        span = row_span(index, block)
        ids = jnp.where(lane_of((block, LANES)) < TOTALS_AT, features[span, :], jnp.zeros((), bf16))

        @pl.loop(0, queries.shape[1] // LANES)
        def _(pair):
            cols = row_span(pair, LANES)
            total = None
            for half in range(2):
                wide_query = jnp.concatenate([head_half(queries[span, cols], half), ids], axis=1)
                scores = dot_t(wide_query, jnp.concatenate([keys[:, cols], id_k[...]], axis=1))
                largest = jnp.max(scores, axis=1, keepdims=True)
                exponent = jnp.exp(scores - largest)
                totals = jnp.sum(exponent, axis=1, keepdims=True)
                term = dot(exponent.astype(bf16), head_half(values[:, cols], half)) / totals
                total = term if total is None else total + term
                features[span, :] = log_total_lanes(
                    features[span, :].astype(f32), 2 * pair + half, largest + jnp.log(totals)
                ).astype(bf16)
            mixed[span, cols] = total.astype(bf16)


def largest_norms(array):
    found = jnp.zeros((1, 1), f32)
    for start in range(0, array.shape[1], LANES):
        values = array[:, start : start + LANES].astype(f32)
        squares = values * values
        both = jnp.sum(squares, axis=1, keepdims=True)
        one = jnp.sum(head_half(squares, 0), axis=1, keepdims=True)
        found = jnp.maximum(found, jnp.max(jnp.maximum(one, both - one), axis=0, keepdims=True))
    return jnp.max(found)


def qkv_kernel(given, made):
    lengths, gain, bias, tokens, weight, qv_bias, out_weight = given
    hidden, queries, keys, values, id_k, mixed, features, part = made[:8]
    rows = tokens.ref.shape[0]
    slots = lengths.shape[1]
    lane = lane_of((1, LANES))
    starts = jnp.where(lane == 0, 0, rows)
    ends = jnp.full((1, LANES), rows, jnp.int32)
    running = jnp.int32(0)
    for slot in range(slots):
        running = running + lengths[0, slot]
        ends = jnp.where(lane == slot, running, ends)
        starts = jnp.where(lane == slot + 1, running, starts)
    scale = HEAD_DIM**-0.5
    block = rows // tokens.pieces
    gain, bias = gain(), bias()

    @pl.loop(0, tokens.pieces)
    def _(index):
        span = row_span(index, block)
        row = index * block + lax.broadcasted_iota(jnp.int32, (block, LANES), 0)
        same = (row >= starts) & (row < ends)
        features.ref[span, :] = same.astype(f32).astype(bf16)
        id_k.ref[span, :] = jnp.where(same | (lane > slots), 0.0, -MASKED).astype(bf16)
        normed, _ = normalize(tokens.ready(index)[span, :].astype(f32))
        hidden.ref[span, :] = (normed * vector(gain) + vector(bias)).astype(bf16)
        hidden.send(index)
        id_k.send(index)

    weight, qv_bias = weight(), qv_bias()

    @pl.loop(0, tokens.pieces)
    def _(index):
        span = row_span(index, block)
        low = hidden.ref[span, :]
        raised = (dot(low, weight[0]) + qv_bias[0:1, :]).astype(bf16)
        queries.ref[span, :] = (raised.astype(f32) * scale).astype(bf16)
        keys.ref[span, :] = dot(low, weight[1]).astype(bf16)
        values.ref[span, :] = (dot(low, weight[2]) + qv_bias[1:2, :]).astype(bf16)
        for one in (queries, keys, values):
            one.send(index)

    bounded = largest_norms(queries.ref) * largest_norms(keys.ref) <= 4000.0
    operands = [one.ref for one in (queries, keys, values, id_k, mixed, features)]

    @pl.when(bounded)
    def _():
        attend(*operands, rows // 2)

    @pl.when(jnp.logical_not(bounded))
    def _():
        attend_shifted(*operands, LANES)

    mixed.send()
    features.send()
    out_weight = out_weight()

    @pl.loop(0, 4)
    def _(index):
        span = row_span(index, rows // 4)
        part.ref[span, :] = dot(mixed.ref[span, :], out_weight[...]).astype(bf16)
        part.send(index)


def mlp_kernel(blocks, given, made, ordered, grad_mlp):
    lengths, place, out_bias, gain, bias, tokens, mine, other, up_bias, up, down, cotangent = given
    hidden, normed_two, inverse_two, active_out, grad_pre, part, down_bias_grad, keep, send = made
    rows = hidden.ref.shape[0]
    used = rows_used(lengths)
    block, tile = rows // 4, 512
    down_bias_grad.ref[...] = jnp.zeros_like(down_bias_grad.ref)
    out_bias, gain, bias = out_bias(), gain(), bias()

    @pl.loop(0, rows // block)
    def _(index):
        span = row_span(index, block)
        for one in (tokens, mine, other):
            one.ready(index)
        after = tokens.ref[span, :].astype(f32) + (
            mine.ref[span, :].astype(f32) + other.ref[span, :].astype(f32) + vector(out_bias)
        )
        normed, inverse = normalize(after)
        normed_two.ref[span, :] = normed.astype(bf16)
        inverse_two.ref[span, :] = jnp.broadcast_to(inverse, (block, LANES))
        hidden.ref[span, :] = (normed * vector(gain) + vector(bias)).astype(bf16)
        row = index * block + lax.broadcasted_iota(jnp.int32, (block, 1), 0)
        grad = jnp.where(row < used, cotangent.ready(index)[span, :].astype(f32), 0.0)
        down_bias_grad.ref[...] += column_sum(grad)
        grad_mlp[span, :] = grad.astype(bf16)
        for one in (normed_two, inverse_two):
            one.send(index)

    up_bias, up, down = up_bias(), up(), down()

    block = rows // 2

    @pl.loop(0, rows // block)
    def _(index):
        span = row_span(index, block)
        low, grad = hidden.ref[span, :], grad_mlp[span, :]
        total = None
        for start in range(0, up.shape[1], tile):
            cols = slice(start, start + tile)
            pre = dot(low, up[:, cols]) + up_bias[cols][None, :]
            square = pre * pre
            inner = pre * (0.7978845608028654 + (0.7978845608028654 * 0.044715) * square)
            share = 0.5 + 0.5 * jnp.tanh(inner)
            active = pre * share
            active_out.ref[span, cols] = active.astype(bf16)
            slope = share + (active * (1.0 - share)) * (
                (2 * 0.7978845608028654) + (6 * 0.7978845608028654 * 0.044715) * square
            )
            grad_low = (dot_t(grad, down[cols, :]) * slope).astype(bf16)
            grad_pre.ref[span, cols] = grad_low
            term = dot_t(grad_low, up[:, cols])
            total = term if total is None else total + term
        active_out.send(index)
        part.ref[span, :] = total.astype(bf16)

    order_columns(grad_mlp[...], place, ordered, blocks)
    weight_grad(ordered, active_out.ref, keep, send)


def down_kernel(given, made):
    weight, activated = given
    part = made[0]
    rows = activated.ref.shape[0] // 4
    weight = weight()
    activated = activated()

    @pl.loop(0, 4)
    def _(index):
        span = row_span(index, rows)
        part.ref[span, :] = dot(activated[span, :], weight[...]).astype(bf16)


def order_columns(values, place, ordered, blocks):
    turned = values.T
    width = turned.shape[0]
    size = width // blocks
    if size % 16:
        ordered[:width, :] = turned
    else:
        for index in range(blocks):
            at = pl.multiple_of(place[index] * size, size)
            ordered[pl.ds(at, size), :] = turned[index * size : (index + 1) * size]
    ordered[width:, :] = jnp.ones((16, turned.shape[1]), bf16)


def weight_grad(ordered, right, keep, send, sums=None, at=0):
    width = ordered.shape[0] - 16
    middle, columns = width // 2, right.shape[1]
    tile = 512 if columns % 512 == 0 else columns

    def one(start):
        source = pl.ds(start, tile)
        target = pl.ds(at + start, tile)
        result = dot(ordered[...], right[:, source])
        send.ref[:, target] = result[middle:width].astype(bf16)
        keep.ref[:, target] = result[:middle].astype(bf16)
        if sums is not None:
            sums.ref[:, source] = result[width : width + 8]

    if tile == columns:
        one(0)
    else:

        @pl.loop(0, columns // tile)
        def _(index):
            one(pl.multiple_of(index * tile, tile))


def weight_kernel(blocks, given, made, ordered):
    place, left, right = given
    order_columns(left()[...], place, ordered, blocks)
    weight_grad(ordered, right(), *made)


def middle_kernel(blocks, given, made, normed_back, ordered):
    lengths, place, gain, norm_mine, norm_other, normed_two, inverse_two, cotangent, weight, mixed = given
    used = rows_used(lengths)
    resid, grad_mixed, sums, keep, send = made
    rows = norm_mine.ref.shape[0]
    block = 256
    sums.ref[...] = jnp.zeros_like(sums.ref)
    gain = gain()

    @pl.loop(0, rows // block)
    def _(index):
        span = row_span(index, block)
        for one in (normed_two, inverse_two, cotangent):
            one.ready(index)
        normed = normed_two.ref[span, :].astype(f32)
        grad_norm = norm_mine.ready(index)[span, :].astype(f32) + norm_other.ready(index)[
            span, :
        ].astype(f32)
        inverse = inverse_two.ref[span, 0:1]
        row = index * block + lax.broadcasted_iota(jnp.int32, (block, 1), 0)
        grad = jnp.where(row < used, cotangent.ref[span, :].astype(f32), 0.0)
        grad = grad + norm_back(grad_norm, normed, inverse, vector(gain))
        resid.ref[span, :] = grad
        resid.send(index)
        low = grad.astype(bf16)
        normed_back[span, :] = low
        sums.ref[0:1, :] += column_sum(grad_norm * normed)
        sums.ref[1:2, :] += column_sum(grad_norm)
        sums.ref[2:3, :] += column_sum(low.astype(f32))

    grad_mixed.ref[...] = dot_t(normed_back[...], weight()[...]).astype(bf16)
    order_columns(normed_back[...], place, ordered, blocks)
    weight_grad(ordered, mixed(), keep, send)


def attention_back_kernel(pair, blocks, given, made, wide_keys, turned, key_total, value_total):
    given, before = given[:8], given[8:]
    place, keys, queries, values, id_k, features, grad_mixed, hidden = given
    if pair == 0:
        *made, ordered = made
        ordered = ordered.ref
    queries, keys, values, id_k, features, grad_mixed = (
        one() for one in (queries, keys, values, id_k, features, grad_mixed)
    )
    grads, sums, keep, send = made
    rows = queries.shape[0]
    cols = slice(pair * LANES, (pair + 1) * LANES)
    lane = lane_of((1, LANES))
    key = keys[:, cols]
    turned[...] = key.T
    for half in range(2):
        at = TOTALS_AT + 3 * (2 * pair + half)
        wide_keys[half, :, :LANES] = key
        wide_keys[half, :, LANES:] = id_k[...] + ((lane >= at) & (lane < at + 3)).astype(f32).astype(bf16)
    block = rows // 2
    key_total[...] = jnp.zeros_like(key_total)
    value_total[...] = jnp.zeros_like(value_total)

    @pl.loop(0, 2)
    def _(index):
        span = row_span(index, block)
        query, grad, feature = queries[span, cols], grad_mixed[span, cols], features[span, :]
        value = values[:, cols]
        key_term = value_term = None
        turned_grads = []
        for half in range(2):
            one_query, one_grad = head_half(query, half), head_half(grad, half)
            probs = jnp.exp(dot_t(wide_keys[half], jnp.concatenate([one_query, feature], axis=1)))
            grad_probs = dot_t(value, one_grad)
            centre = jnp.sum(probs * grad_probs, axis=0, keepdims=True)
            grad_scores = (probs * (grad_probs - centre)).astype(bf16)
            value_one = dot(probs.astype(bf16), one_grad)
            key_one = dot(grad_scores, one_query)
            value_term = value_one if half == 0 else value_term + value_one
            key_term = key_one if half == 0 else key_term + key_one
            turned_grads.append(dot(turned[half * HEAD_DIM : (half + 1) * HEAD_DIM, :], grad_scores))
        key_total[...] += key_term
        value_total[...] += value_term
        grads.ref[span, :LANES] = (jnp.concatenate(turned_grads, axis=0).T * HEAD_DIM**-0.5).astype(bf16)

    grads.ref[:, LANES : 2 * LANES] = key_total[...].astype(bf16)
    grads.ref[:, 2 * LANES :] = value_total[...].astype(bf16)
    if pair == 0:
        order_columns(hidden()[...], place, ordered, blocks)
    else:
        ordered = hidden()
    at = 0
    for index in range(0, len(before), 2):
        columns = before[index].ref.shape[1]
        for target, source in zip((keep, send), before[index : index + 2]):
            target.ref[:, at : at + columns] = source()[...]
        at += columns
    weight_grad(ordered, grads.ref, keep, send, sums, at)


def first_kernel(given, made):
    *grads, weight = given
    weight, part = weight(), made[0]
    rows = part.ref.shape[0] // 4
    grads = [one() for one in grads]
    @pl.loop(0, 4)
    def _(index):
        span = row_span(index, rows)
        operand = jnp.concatenate(
            [one[span, kind * LANES : (kind + 1) * LANES] for kind in range(3) for one in grads], axis=1
        )
        full = jnp.concatenate([weight[kind] for kind in range(3)], axis=1)
        part.ref[span, :] = dot_t(operand, full).astype(bf16)


def last_kernel(given, made):
    gain, tokens, mine, other, resid, *sums = given
    out, vectors = made
    middle_sums, down_sums, up_sums, *pair_sums = (one()[...] for one in sums)
    block = tokens.ref.shape[0] // 4
    width = tokens.ref.shape[1]
    vectors.ref[...] = jnp.zeros_like(vectors.ref)
    gain, tokens, mine, other, resid = gain(), tokens(), mine(), other(), resid()

    @pl.loop(0, 4)
    def _(index):
        span = row_span(index, block)
        normed, inverse = normalize(tokens[span, :].astype(f32))
        grad_first = mine[span, :].astype(f32) + other[span, :].astype(f32)
        out.ref[span, :] = resid[span, :] + norm_back(grad_first, normed, inverse, vector(gain))
        out.send(index)
        vectors.ref[0:1, :] += column_sum(grad_first * normed)
        vectors.ref[1:2, :] += column_sum(grad_first)

    pairs = len(pair_sums)
    for pair, one in enumerate(pair_sums):
        for kind, start in ((0, 0), (2, pairs * LANES)):
            at = start + pair * LANES
            vectors.ref[2:3, at : at + LANES] = one[0:1, kind * LANES : (kind + 1) * LANES]
    vectors.ref[3:6, :] = middle_sums[0:3, :]
    vectors.ref[6:7, :] = down_sums
    for index in range(up_sums.shape[1] // width):
        vectors.ref[7 + index : 8 + index, :] = up_sums[0:1, index * width : (index + 1) * width]


def fold_kernel(joined, folded, given, made):
    at = 0
    for index in range(len(given) // 2):
        keep, came = given[2 * index](), given[2 * index + 1]()
        stays, sent = made[:2] if joined else made[2 * index : 2 * index + 2]
        cols = slice(at, at + keep.shape[1])
        at += keep.shape[1] if joined else 0
        if index < folded:
            stays.ref[:, cols] = keep[...]
            sent.ref[:, cols] = came[...]
            continue
        middle = keep.shape[0] // 2
        sent.ref[:, cols] = (keep[middle:].astype(f32) + came[middle:].astype(f32)).astype(bf16)
        stays.ref[:, cols] = keep[:middle].astype(f32) + came[:middle].astype(f32)


def add_kernel(given, made):
    made[0].ref[...] = given[0]()[...] + given[1]()[...]


def output_kernel(given, made):
    out_bias, down_bias, tokens, part, other, down_part, down_other = given
    out = made[0]
    out_bias, down_bias, down_part, down_other = out_bias(), down_bias(), down_part(), down_other()
    block = out.ref.shape[0] // out.pieces

    @pl.loop(0, out.pieces)
    def _(index):
        span = row_span(index, block)
        for one in (tokens, part, other):
            one.ready(index)
        after = tokens.ref[span, :].astype(f32) + (
            part.ref[span, :].astype(f32) + other.ref[span, :].astype(f32) + vector(out_bias)
        )
        branch = down_part[span, :].astype(f32) + down_other[span, :].astype(f32) + vector(down_bias)
        out.ref[span, :] = (after + branch).astype(bf16)
        out.send(index)


def final_kernel(given, made):
    for index, one in enumerate(made):
        one.ref[...] = given[2 * index]()[...] + given[2 * index + 1]()[...].astype(f32)
        one.send()


def final_qkv_kernel(given, made):
    qkv, out = made
    keep, came = given
    total = keep()[...] + came()[...].astype(f32)
    local = out.ref.shape[1]
    out.ref[...] = total[:, :local]
    for pair in range(local // LANES):
        for kind in range(3):
            at = local + (3 * pair + kind) * LANES
            qkv.ref[kind, :, pair * LANES : (pair + 1) * LANES] = total[:, at : at + LANES]


def swap(values, axis, bit, size):
    return lax.ppermute(values, axis, [(i, i ^ (1 << bit)) for i in range(size)])


class Flow:
    def __init__(self, orders, size, keep, send):
        self.orders, self.size, self.keep, self.send, self.step = orders, size, keep, send, 0

    def exchange(self):
        pairs = [
            (2 * index + core, 2 * (index ^ (1 << order[self.step])) + core)
            for index in range(self.size)
            for core, order in enumerate(self.orders)
        ]
        self.came = lax.ppermute(self.send, ("dp", "mp"), pairs)
        self.step += 1


def fold(chain, flows, ready=()):
    halved = [(flow.keep.shape[0] // 2, flow.keep.shape[1]) for flow in flows]
    if ready:
        columns = sum(flow.keep.shape[1] for flow in (*ready, *flows))
        halved = [(halved[0][0], columns)]
    outs = []
    for rows, columns in halved:
        outs += [Made((rows, columns), f32, "h" if rows <= 48 else "v"), Made((rows, columns), bf16, "v")]
    pairs = [(flow.keep, flow.send) for flow in ready] + [(flow.keep, flow.came) for flow in flows]
    results = call(
        chain,
        functools.partial(fold_kernel, bool(ready), len(ready)),
        "fold",
        outs,
        [Given(array, "v") for pair in pairs for array in pair],
        limit=8,
    )
    for index in range(len(halved)):
        flows[index].keep, flows[index].send = results[2 * index : 2 * index + 2]


def finish(chain, flows, kernel, shapes, covers=True):
    return call(
        chain,
        kernel,
        "final",
        [Made(shape, f32, "h") for shape in shapes],
        [Given(array, kind) for flow in flows for array, kind in ((flow.keep, "h"), (flow.came, "v"))],
        limit=8,
        covers=covers,
    )


def places(orders, size, me, core):
    source = jnp.arange(size, dtype=jnp.int32) ^ me
    found = []
    for order in orders:
        place = jnp.zeros((size,), jnp.int32)
        for step, bit in enumerate(order):
            place = place + (((source >> bit) & 1) << (size.bit_length() - 2 - step))
        found.append(place)
    return jnp.where(core == 0, *found)


def arranged(halves, place, size):
    keep, send = halves
    rows, columns = keep.shape
    if (2 * rows // size) % 16 == 0:
        return halves
    spots = jnp.zeros((size,), jnp.int32).at[place].set(jnp.arange(size, dtype=jnp.int32))
    both = jnp.concatenate(halves, axis=0).reshape(size, 2 * rows // size, columns)[spots]
    both = both.reshape(2 * rows, columns)
    return both[:rows], both[rows:]


def per_device(
    n_dp, tokens, cotangent, lengths, ln1_gain, ln1_bias, qkv_weight, qv_bias, out_weight, out_bias,
    ln2_gain, ln2_bias, up_weight, up_bias, down_weight, down_bias,
):
    chain = Chain()
    rows, width = tokens.shape
    local = qkv_weight.shape[2]
    units = up_weight.shape[1]
    pairs = local // LANES
    me, core = lax.axis_index("dp"), lax.axis_index("mp")
    bits = list(range(n_dp.bit_length() - 1))
    rest = bits[3:]
    near_orders = [[0, 1, 2, *rest], [1, 0, 2, *rest]]
    long_orders = [[2, 0, 1, *rest], [2, 1, 0, *rest]]
    near_place, long_place = (places(orders, n_dp, me, core) for orders in (near_orders, long_orders))
    weight = jnp.transpose(qkv_weight, (1, 0, 2))
    scalars = Given(lengths, "s")
    near = lambda array: Given(array, "v")
    far = lambda array, pieces=1: Given(array, "h", pieces)
    fetch = lambda array: Made(array.shape, array.dtype, "p", source=array)
    halves = lambda columns: [Made((width // 2, columns), bf16, "v")] * 2
    turned = pltpu.VMEM((width + 16, rows), bf16)

    hidden_one, queries, keys, values, id_k, mixed, features, part = call(
        chain,
        qkv_kernel,
        "qkv_attention",
        [
            Made((rows, width), bf16, "h", 4),
            *[Made((rows, local), bf16, "h", 4)] * 3,
            Made((rows, LANES), bf16, "h", 4),
            Made((rows, local), bf16, "h"),
            Made((rows, LANES), bf16, "h"),
            Made((rows, width), bf16, "v", 4),
        ],
        [
            scalars, far(ln1_gain), far(ln1_bias), far(tokens, 4), far(weight), far(qv_bias), far(out_weight)
        ],
        limit=28,
    )
    other = swap(part, "mp", 0, 2)
    (
        hidden_two, normed_two, inverse_two, activated, grad_pre, norm_part, down_sums,
        down_keep, down_send,
    ) = call(
        chain,
        functools.partial(mlp_kernel, n_dp),
        "mlp",
        [
            Made((rows, width), bf16, "v"),
            Made((rows, width), bf16, "h", 4),
            Made((rows, LANES), f32, "h", 4),
            Made((rows, units), bf16, "h", 2),
            Made((rows, units), bf16, "v"),
            Made((rows, width), bf16, "v"),
            Made((1, width), f32, "v"),
            *halves(units),
        ],
        [
            scalars,
            Given(near_place, "s"),
            *map(far, (out_bias, ln2_gain, ln2_bias)),
            far(tokens, 4),
            near(part),
            near(other),
            *map(far, (up_bias, up_weight, down_weight)),
            far(cotangent, 4),
        ],
        scratch=[turned, pltpu.VMEM((rows, width), bf16)],
        limit=30,
    )
    norm_other = swap(norm_part, "mp", 0, 2)

    def weights(name, left, right, place, with_sums=False):
        return call(
        chain,
            functools.partial(weight_kernel, n_dp),
            name,
            [*halves(units), *[Made((8, units), f32, "v")] * with_sums],
            [Given(place, "s"), near(left), near(right)],
            scratch=[turned],
            limit=10,
        )

    flow_down = Flow(near_orders, n_dp, *arranged((down_keep, down_send), near_place, n_dp))
    flow_down.exchange()
    up_keep, up_send, up_sums = weights("up_grad", hidden_two, grad_pre, long_place, True)
    flow_up = Flow(long_orders, n_dp, *arranged((up_keep, up_send), long_place, n_dp))
    flow_up.exchange()
    resid, grad_mixed, middle_sums, out_keep, out_send = call(
        chain,
        functools.partial(middle_kernel, n_dp),
        "middle",
        [
            Made((rows, width), f32, "h", 4),
            Made((rows, local), bf16, "v"),
            Made((8, width), f32, "v"),
            *halves(local),
        ],
        [
            scalars,
            Given(near_place, "s"),
            far(ln2_gain),
            near(norm_part),
            near(norm_other),
            *map(near, (normed_two, inverse_two, cotangent)),
            near(out_weight),
            near(mixed),
        ],
        scratch=[pltpu.VMEM((rows, width), bf16), turned],
        limit=16,
    )
    grads, sums, halves_qkv = [], [], []
    hiddens = [hidden_one]

    def attention_back(pair, before=()):
        columns = 3 * LANES + sum(keep.shape[1] for keep, _ in before)
        three, sums_one, keep, send, *order = call(
            chain,
            functools.partial(attention_back_kernel, pair, n_dp),
            "attention_back%d" % pair,
            [
                Made((rows, 3 * LANES), bf16, "v"),
                Made((8, 3 * LANES), f32, "v"),
                *halves(columns),
                *[Made((width + 16, rows), bf16, "h")] * (pair == 0),
            ],
            [
                Given(near_place, "s"),
                *map(near, (keys, queries, values, id_k, features, grad_mixed)),
                near(hiddens[-1]),
                *(near(array) for pieces in before for array in pieces),
            ],
            scratch=[
                pltpu.VMEM((2, rows, 2 * LANES), bf16),
                pltpu.VMEM((LANES, rows), bf16),
                pltpu.VMEM((rows, LANES), f32),
                pltpu.VMEM((rows, LANES), f32),
            ],
            limit=18,
        )
        hiddens.extend(order)
        grads.append(three)
        sums.append(sums_one)
        halves_qkv.append((keep, send))

    def exchange(*flows):
        for flow in flows:
            flow.exchange()

    def flow_of(pieces):
        return Flow(near_orders, n_dp, *arranged(pieces, near_place, n_dp))

    flow_out = flow_of((out_keep, out_send))
    exchange(flow_out)
    attention_back(0)
    flow_first = flow_of(halves_qkv[0])
    fold(chain, [flow_down, flow_out])
    exchange(flow_down, flow_first)
    for pair in range(1, pairs - 1):
        attention_back(pair)
    flows_next = [flow_of(pieces) for pieces in halves_qkv[1:]]
    fold(chain, [flow_down, flow_up, flow_first])
    exchange(flow_down, flow_up, *flows_next)
    attention_back(pairs - 1)
    flow_qkv = flow_of(halves_qkv[-1])
    exchange(flow_qkv)
    fold(chain, [flow_down, flow_up, *flows_next])
    (first_part,) = call(
        chain,
        first_kernel,
        "first",
        [Made((rows, width), bf16, "v", 4)],
        [*map(near, grads), near(weight)],
        limit=10,
    )
    first_other = swap(first_part, "mp", 0, 2)
    fold(chain, [flow_qkv], [flow_out, flow_first, *flows_next])
    exchange(flow_qkv, flow_up)
    last_step = len(rest) == 1
    if last_step:
        exchange(flow_down)
    (down_part,) = call(
        chain,
        down_kernel,
        "down",
        [Made((rows, width), bf16, "v", 4)],
        [near(down_weight), near(activated)],
        limit=10,
    )
    down_other = swap(down_part, "mp", 0, 2)
    tokens_grad, vectors = call(
        chain,
        last_kernel,
        "last",
        [Made((rows, width), f32, "h", 4), Made((16, width), f32, "v")],
        [
            far(ln1_gain),
            *map(near, (tokens, first_part, first_other, resid, middle_sums, down_sums, up_sums, *sums)),
        ],
        limit=14,
        covers=False,
    )
    shape = (width // n_dp, units)
    if last_step:
        (down_total,) = finish(chain, [flow_down], final_kernel, [shape], False)
    fold(chain, [flow_qkv, flow_up])
    exchange(flow_qkv, flow_up)
    if not last_step:
        exchange(flow_down)

    def all_sum_step(bit):
        nonlocal vectors
        other = swap(vectors, "dp", bit, n_dp)
        (vectors,) = call(
            chain, add_kernel, "add", [Made((16, width), f32, "v")], [near(vectors), near(other)], limit=4
        )

    (output,) = call(
        chain,
        output_kernel,
        "output",
        [Made((rows, width), bf16, "h", 4)],
        [
            far(out_bias), far(down_bias), *(far(array, 4) for array in (tokens, part, other)), near(down_part),
            near(down_other),
        ],
        limit=16,
    )
    all_sum_step(bits[0])
    fold(chain, [flow_qkv])
    exchange(flow_qkv)
    all_sum_step(bits[1])
    if last_step:
        (up_total,) = finish(chain, [flow_up], final_kernel, [shape])
    for bit in bits[2:-1]:
        all_sum_step(bit)
    flows = [flow_qkv, flow_up, flow_down]
    for step in range(1, len(rest)):
        fold(chain, flows)
        exchange(*flows)
    if not last_step:
        down_total, up_total = finish(chain, [flow_down, flow_up], final_kernel, [shape] * 2)
    mine = width // n_dp
    qkv_total, out_total = finish(
        chain, [flow_qkv], final_qkv_kernel, [(3, mine, local), (mine, local)]
    )
    all_sum_step(bits[-1])
    ups = units // width
    return (
        output,
        tokens_grad,
        vectors[0],
        vectors[1],
        jnp.transpose(qkv_total, (1, 0, 2)),
        vectors[2].reshape(2, local),
        out_total.T,
        vectors[5],
        vectors[3],
        vectors[4],
        up_total,
        vectors[7 : 7 + ups].reshape(-1),
        down_total.T,
        vectors[6],
    )


def solution(mesh):
    return jax.shard_map(
        functools.partial(per_device, mesh.shape["dp"]),
        mesh=mesh,
        in_specs=(
            P("dp", None),
            P("dp", None),
            P("dp", None),
            P(),
            P(),
            P(None, None, "mp"),
            P(None, "mp"),
            P("mp", None),
            P(),
            P(),
            P(),
            P(None, "mp"),
            P("mp"),
            P("mp", None),
            P(),
        ),
        out_specs=(
            P("dp", None),
            P("dp", None),
            P(),
            P(),
            P("dp", None, "mp"),
            P(None, "mp"),
            P("mp", "dp"),
            P(),
            P(),
            P(),
            P("dp", "mp"),
            P("mp"),
            P("mp", "dp"),
            P(),
        ),
        check_vma=False,
    )
```

profile of v0, /device:TPU:0, one launch (start us, length us, event | category | flops | bytes accessed | tf_op | source)
XLA Modules:
  0.0 140.7 jit_solution(3501242212912020644)
XLA Ops:
  1.3 18.8 %qkv_attention.1 = (bf16[1024,768]{1,0:T(8,128)(2,1)}, bf16[1024,384]{1,0:T(8,128)(2,1)}, bf16[1024,384]{1,0:T(8,128)(2,1)}, bf16[1024,384]{1,0:T(8,128)(2,1)}, ...) custom-call(s32[1,16]{1,0:T(1,128)S(1)} %copy-done.13, ...), custom_call_target="tpu_custom_call" | custom-call | flops 20000000000 | bytes 1 | tf_op jit(solution)/shard_map/qkv_attention/pallas_call | solution.py:182
  20.6 3.0 %collective-permute-done.refs_7_.refs_4_ = bf16[1024,768]{1,0:T(8,128)(2,1)S(1)} collective-permute-done((bf16[1024,768]{1,0:T(8,128)(2,1)S(1)}, bf16[1024,768]{1,0:T(8,128)(2,1)S(1)}, u32[]{:S(2)}, u32[]{:S(2)}) %collective-permute-start) | collective-permute-done | bytes 1572896 | tf_op jit(solution)/shard_map/ppermute | solution.py:696
  23.7 1.1 copy-done.27
  24.8 16.8 %mlp.1 = (bf16[1024,768]{1,0:T(8,128)(2,1)S(1)}, bf16[1024,768]{1,0:T(8,128)(2,1)}, f32[1024,128]{1,0:T(8,128)}, bf16[1024,1536]{1,0:T(8,128)(2,1)}, bf16[1024,1...) custom-call(s32[1,16]{1,0:T(1,128)S(1)} %copy-done.14, ...), custom_call_target="tpu_custom_call" | custom-call | flops 20000000000 | bytes 1 | tf_op jit(solution)/shard_map/mlp/pallas_call | solution.py:182
  42.0 2.6 %collective-permute-start.1 = (bf16[384,1536]{1,0:T(8,128)(2,1)S(1)}, bf16[384,1536]{1,0:T(8,128)(2,1)S(1)}, u32[]{:S(2)}, u32[]{:S(2)}) collective-permute-start(bf16[384,1536]{1,0:T(8,128)(2,1)S(1)} %get-tuple-element.84), channel_id=1, source_target_pairs={{0,2},{1,5},{2,0},{3,7},{4,6},{5,1},{6,4},{7,3},{8,10},{9,13},{10,... | collective-permute-start | bytes 3538952 | tf_op jit(solution)/shard_map/ppermute | solution.py:709
  44.7 4.0 %up_grad.1 = (bf16[384,1536]{1,0:T(8,128)(2,1)S(1)}, bf16[384,1536]{1,0:T(8,128)(2,1)S(1)}, f32[8,1536]{1,0:T(8,128)S(1)}) custom-call(s32[16]{0:T(128)S(1)} %get-tuple-element.153.refs_0_, bf16[1024,768]{1,0:T(8,128)(2,1)S(1)} %get-tuple-element.89.refs_1_, bf16[1024,1536]{1,0:T(8,128)(2,1)S(1)} %get-tuple-element.90.refs_2_, ...), custom_call_target="tpu_custom_call" | custom-call | flops 20000000000 | bytes 1 | tf_op jit(solution)/shard_map/up_grad/pallas_call | solution.py:182
  48.7 1.6 %collective-permute-start.5 = (bf16[384,1536]{1,0:T(8,128)(2,1)S(1)}, bf16[384,1536]{1,0:T(8,128)(2,1)S(1)}, u32[]{:S(2)}, u32[]{:S(2)}) collective-permute-start(bf16[384,1536]{1,0:T(8,128)(2,1)S(1)} %get-tuple-element.108), channel_id=1, source_target_pairs={{0,8},{1,9},{2,10},{3,11},{4,12},{5,13},{6,14},{7,15},{8,0},{9,1},... | collective-permute-start | bytes 3538952 | tf_op jit(solution)/shard_map/ppermute | solution.py:709
  50.5 6.4 %middle.1 = (f32[1024,768]{1,0:T(8,128)}, bf16[1024,384]{1,0:T(8,128)(2,1)S(1)}, f32[8,768]{1,0:T(8,128)S(1)}, bf16[384,384]{1,0:T(8,128)(2,1)S(1)}, bf16[384,384]{1,0:T(8,128)(2,1)S(1)}) custom-call(s32[1,16]{1,0:T(1,128)S(1)} %copy-done.14, s32[16]{0:T(128)S(1)} %get-tuple-element.154.refs_1_.refs_0_, f32[768]{0:T(1024)} %refs_2_.6, ...), custom_call_target="tpu_custom_call" | custom-call | flops 20000000000 | bytes 1 | tf_op jit(solution)/shard_map/middle/pallas_call | solution.py:182
  57.5 9.7 %attention_back0.1 = (bf16[1024,384]{1,0:T(8,128)(2,1)S(1)}, f32[8,384]{1,0:T(8,128)S(1)}, bf16[384,384]{1,0:T(8,128)(2,1)S(1)}, bf16[384,384]{1,0:T(8,128)(2,1)S(1)}, bf16[784,1024]{1,0:T(8,128)(2,1)}) custom-call(s32[16]{0:T(128)S(1)} %get-tuple-element.154.refs_1_.refs_0_, bf16[1024,384]{1,0:T(8,128)(2,1)S(1)} %copy-done.24, ...), custom_call_target="tpu_custom_call" | custom-call | flops 20000000000 | bytes 1 | tf_op jit(solution)/shard_map/attention_back0/pallas_call | solution.py:182
  67.2 1.5 %collective-permute-start.6 = (bf16[384,384]{1,0:T(8,128)(2,1)S(1)}, bf16[384,384]{1,0:T(8,128)(2,1)S(1)}, u32[]{:S(2)}, u32[]{:S(2)}) collective-permute-start(bf16[384,384]{1,0:T(8,128)(2,1)S(1)} %get-tuple-element.110), channel_id=1, source_target_pairs={{0,2},{1,5},{2,0},{3,7},{4,6},{5,1},{6,4},{7,3},{8,10},{9,13},{10,... | collective-permute-start | bytes 884744 | tf_op jit(solution)/shard_map/ppermute | solution.py:709
  69.1 1.6 %collective-permute-start.4 = (bf16[192,1536]{1,0:T(8,128)(2,1)S(1)}, bf16[192,1536]{1,0:T(8,128)(2,1)S(1)}, u32[]{:S(2)}, u32[]{:S(2)}) collective-permute-start(bf16[192,1536]{1,0:T(8,128)(2,1)S(1)} %get-tuple-element.106), channel_id=1, source_target_pairs={{0,4},{1,3},{2,6},{3,1},{4,0},{5,7},{6,2},{7,5},{8,12},{9,11},{10,... | collective-permute-start | bytes 1769480 | tf_op jit(solution)/shard_map/ppermute | solution.py:709
  70.7 8.7 %attention_back1.1 = (bf16[1024,384]{1,0:T(8,128)(2,1)S(1)}, f32[8,384]{1,0:T(8,128)S(1)}, bf16[384,384]{1,0:T(8,128)(2,1)S(1)}, bf16[384,384]{1,0:T(8,128)(2,1)S(1)}) custom-call(s32[16]{0:T(128)S(1)} %get-tuple-element.154.refs_1_.refs_0_, bf16[1024,384]{1,0:T(8,128)(2,1)S(1)} %copy-done.24, bf16[1024,384]{1,0:T(8,128)(2,1)S(1)} %copy-done.23, ...), custom_call_target="tpu_custom_call" | custom-call | flops 20000000000 | bytes 1 | tf_op jit(solution)/shard_map/attention_back1/pallas_call | solution.py:182
  80.5 1.6 %collective-permute-start.8 = (bf16[192,1536]{1,0:T(8,128)(2,1)S(1)}, bf16[192,1536]{1,0:T(8,128)(2,1)S(1)}, u32[]{:S(2)}, u32[]{:S(2)}) collective-permute-start(bf16[192,1536]{1,0:T(8,128)(2,1)S(1)} %get-tuple-element.118), channel_id=1, source_target_pairs={{0,2},{1,5},{2,0},{3,7},{4,6},{5,1},{6,4},{7,3},{8,10},{9,13},{10,... | collective-permute-start | bytes 1769480 | tf_op jit(solution)/shard_map/ppermute | solution.py:709
  82.6 9.0 %attention_back2.1 = (bf16[1024,384]{1,0:T(8,128)(2,1)S(1)}, f32[8,384]{1,0:T(8,128)S(1)}, bf16[384,384]{1,0:T(8,128)(2,1)S(1)}, bf16[384,384]{1,0:T(8,128)(2,1)S(1)}) custom-call(s32[16]{0:T(128)S(1)} %get-tuple-element.154.refs_1_.refs_0_, bf16[1024,384]{1,0:T(8,128)(2,1)S(1)} %copy-done.24, bf16[1024,384]{1,0:T(8,128)(2,1)S(1)} %copy-done.23, ...), custom_call_target="tpu_custom_call" | custom-call | flops 20000000000 | bytes 1 | tf_op jit(solution)/shard_map/attention_back2/pallas_call | solution.py:182
  93.4 2.6 %collective-permute-start.14 = (bf16[48,1536]{1,0:T(8,128)(2,1)S(1)}, bf16[48,1536]{1,0:T(8,128)(2,1)S(1)}, u32[]{:S(2)}, u32[]{:S(2)}) collective-permute-start(bf16[48,1536]{1,0:T(8,128)(2,1)S(1)} %get-tuple-element.129.refs_4_), channel_id=1, source_target_pairs={{0,16},{1,17},{2,18},{3,19},{4,20},{5,21},{6,22},{7,23},{8,24},{9,... | collective-permute-start | bytes 442376 | tf_op jit(solution)/shard_map/ppermute | solution.py:709
  96.1 2.9 %first.1.refs_8_.refs_2_ = bf16[1024,768]{1,0:T(8,128)(2,1)S(1)} custom-call(bf16[1024,384]{1,0:T(8,128)(2,1)S(1)} %get-tuple-element.126.refs_0_, bf16[1024,384]{1,0:T(8,128)(2,1)S(1)} %get-tuple-element.127.refs_1_, bf16[1024,384]{1,0:T(8,128)(2,1)S(1)} %get-tuple-element.128.refs_2_, bf16[3,768,384]{2,1,0:T(8,128)(2,1)S(1)} %bitcast.6, ...), custom_call_target="tpu_custom_call" | custom-call | flops 20000000000 | bytes 1 | tf_op jit(solution)/shard_map/first/pallas_call | solution.py:182
  99.3 1.0 collective-permute-start.12
  100.3 1.1 collective-permute-start.13
  101.7 3.1 %down.1.refs_11_.refs_5_ = bf16[1024,768]{1,0:T(8,128)(2,1)S(1)} custom-call(bf16[1536,768]{1,0:T(8,128)(2,1)S(1)} %copy-done.7, bf16[1024,1536]{1,0:T(8,128)(2,1)S(1)} %copy-done.18, bf16[192,1536]{1,0:T(8,128)(2,1)S(1)} %get-tuple-element.130.refs_2_), custom_call_target="tpu_custom_call" | custom-call | flops 20000000000 | bytes 1 | tf_op jit(solution)/shard_map/down/pallas_call | solution.py:182
  105.4 4.2 %last.1 = (f32[1024,768]{1,0:T(8,128)}, f32[16,768]{1,0:T(8,128)S(1)}) custom-call(f32[768]{0:T(1024)} %refs_0_.10, bf16[1024,768]{1,0:T(8,128)(2,1)S(1)} %copy-done.1, bf16[1024,768]{1,0:T(8,128)(2,1)S(1)} %first.1.refs_8_.refs_2_, bf16[1024,768]{1,0:T(8,128)(2,1)S(1)} %collective-permute-done.15.refs_3_, f32[1024,768]{1,0:T(8,128)S(1)} %copy-done, ...), custom_call_target="tpu_custom_call" | custom-call | bytes 1 | tf_op jit(solution)/shard_map/last/pallas_call | solution.py:182
  109.6 1.1 collective-permute-start.16
  110.8 1.7 %final.3.refs_4_ = f32[48,1536]{1,0:T(8,128)} custom-call(f32[48,1536]{1,0:T(8,128)} %get-tuple-element.134.refs_0_, bf16[48,1536]{1,0:T(8,128)(2,1)S(1)} %collective-permute-done.14.refs_1_, f32[16,768]{1,0:T(8,128)S(1)} %get-tuple-element.136.refs_2_.refs_0_), custom_call_target="tpu_custom_call" | custom-call | bytes 1 | tf_op jit(solution)/shard_map/final/pallas_call | solution.py:182
  114.2 1.6 %collective-permute-start.18 = (bf16[96,1536]{1,0:T(8,128)(2,1)S(1)}, bf16[96,1536]{1,0:T(8,128)(2,1)S(1)}, u32[]{:S(2)}, u32[]{:S(2)}) collective-permute-start(bf16[96,1536]{1,0:T(8,128)(2,1)S(1)} %get-tuple-element.140), channel_id=1, source_target_pairs={{0,8},{1,9},{2,10},{3,11},{4,12},{5,13},{6,14},{7,15},{8,0},{9,1},... | collective-permute-start | bytes 884744 | tf_op jit(solution)/shard_map/ppermute | solution.py:709
  115.9 1.7 %collective-permute-start.20 = (bf16[48,1536]{1,0:T(8,128)(2,1)S(1)}, bf16[48,1536]{1,0:T(8,128)(2,1)S(1)}, u32[]{:S(2)}, u32[]{:S(2)}) collective-permute-start(bf16[48,1536]{1,0:T(8,128)(2,1)S(1)} %get-tuple-element.137.refs_7_), channel_id=1, source_target_pairs={{0,16},{1,17},{2,18},{3,19},{4,20},{5,21},{6,22},{7,23},{8,24},{9,... | collective-permute-start | bytes 442376 | tf_op jit(solution)/shard_map/ppermute | solution.py:709
  117.6 3.9 %output.1.refs_2_ = bf16[1024,768]{1,0:T(8,128)(2,1)} custom-call(f32[768]{0:T(1024)} %refs_0_.11, f32[768]{0:T(1024)} %refs_1_.5, bf16[1024,768]{1,0:T(8,128)(2,1)} %refs_2_.7, bf16[1024,768]{1,0:T(8,128)(2,1)} %copy-done.10, bf16[1024,768]{1,0:T(8,128)(2,1)} %copy-done.11, bf16[1024,768]{1,0:T(8,128)(2,1)S(1)} %down.1.refs_11_.refs_5_, ...), custom_call_target="tpu_custom_call" | custom-call | flops 20000000000 | bytes 1 | tf_op jit(solution)/shard_map/output/pallas_call | solution.py:182
  121.5 1.4 copy-done.15
  122.9 1.0 collective-permute-start.17
  123.9 2.3 %collective-permute-done.18.refs_1_ = bf16[96,1536]{1,0:T(8,128)(2,1)S(1)} collective-permute-done((bf16[96,1536]{1,0:T(8,128)(2,1)S(1)}, bf16[96,1536]{1,0:T(8,128)(2,1)S(1)}, u32[]{:S(2)}, u32[]{:S(2)}) %collective-permute-start.18) | collective-permute-done | bytes 294944 | tf_op jit(solution)/shard_map/ppermute | solution.py:709
  127.3 2.5 %collective-permute-start.19 = (f32[16,768]{1,0:T(8,128)S(1)}, f32[16,768]{1,0:T(8,128)S(1)}, u32[]{:S(2)}, u32[]{:S(2)}) collective-permute-start(f32[16,768]{1,0:T(8,128)S(1)} %add.72.refs_2_.refs_0_), channel_id=1, source_target_pairs={{0,8},{2,10},{4,12},{6,14},{8,0},{10,2},{12,4},{14,6},{16,24},{18,... | collective-permute-start | bytes 147464 | tf_op jit(solution)/shard_map/ppermute | solution.py:696
  129.9 1.7 %final.4.refs_2_ = f32[48,1536]{1,0:T(8,128)} custom-call(f32[48,1536]{1,0:T(8,128)} %get-tuple-element.142.refs_0_, bf16[48,1536]{1,0:T(8,128)(2,1)S(1)} %collective-permute-done.20.refs_1_, f32[16,768]{1,0:T(8,128)S(1)} %add.72.refs_2_.refs_0_), custom_call_target="tpu_custom_call" | custom-call | flops 20000000000 | bytes 1 | tf_op jit(solution)/shard_map/final/pallas_call | solution.py:182
  132.9 2.1 %collective-permute-start.21 = (f32[16,768]{1,0:T(8,128)S(1)}, f32[16,768]{1,0:T(8,128)S(1)}, u32[]{:S(2)}, u32[]{:S(2)}) collective-permute-start(f32[16,768]{1,0:T(8,128)S(1)} %add.73.refs_2_.refs_0_), channel_id=1, source_target_pairs={{0,16},{2,18},{4,20},{6,22},{8,24},{10,26},{12,28},{14,30},{16,0},... | collective-permute-start | bytes 147464 | tf_op jit(solution)/shard_map/ppermute | solution.py:696
  135.8 1.7 %final.5 = (f32[3,48,384]{2,1,0:T(8,128)}, f32[48,384]{1,0:T(8,128)}) custom-call(f32[48,1536]{1,0:T(8,128)} %get-tuple-element.143.refs_0_, bf16[48,1536]{1,0:T(8,128)(2,1)S(1)} %collective-permute-done.22.refs_1_, f32[16,768]{1,0:T(8,128)S(1)} %add.73.refs_2_.refs_0_), custom_call_target="tpu_custom_call" | custom-call | flops 20000000000 | bytes 1 | tf_op jit(solution)/shard_map/final/pallas_call | solution.py:182
  (103 shorter events, 15.3 us)
Async XLA Ops:
  1.3 22.4 %copy-start.14 = (s32[1,16]{1,0:T(1,128)S(1)}, s32[1,16]{1,0:T(1,128)}, u32[]{:S(2)}) copy-start(s32[1,16]{1,0:T(1,128)} %refs_0_.8) | copy-start | bytes 196
  20.1 21.5 %copy-start.10 = (bf16[1024,768]{1,0:T(8,128)(2,1)}, bf16[1024,768]{1,0:T(8,128)(2,1)S(1)}, u32[]{:S(2)}) copy-start(bf16[1024,768]{1,0:T(8,128)(2,1)S(1)} %get-tuple-element.80.refs_6_.refs_3_) | copy-start | bytes 4718596
  20.1 3.6 %collective-permute-start = (bf16[1024,768]{1,0:T(8,128)(2,1)S(1)}, bf16[1024,768]{1,0:T(8,128)(2,1)S(1)}, u32[]{:S(2)}, u32[]{:S(2)}) collective-permute-start(bf16[1024,768]{1,0:T(8,128)(2,1)S(1)} %get-tuple-element.80.refs_6_.refs_3_), channel_id=1, source_target_pairs={{0,1},{1,0},{2,3},{3,2},{4,5},{5,4},{6,7},{7,6},{8,9},{9,8},{10,11... | collective-permute-start | bytes 4718600 | tf_op jit(solution)/shard_map/ppermute | solution.py:696
  23.7 17.9 %copy-start.11 = (bf16[1024,768]{1,0:T(8,128)(2,1)}, bf16[1024,768]{1,0:T(8,128)(2,1)S(1)}, u32[]{:S(2)}) copy-start(bf16[1024,768]{1,0:T(8,128)(2,1)S(1)} %collective-permute-done.refs_7_.refs_4_) | copy-start | bytes 4718596
  41.6 8.8 %collective-permute-start.2 = (bf16[1024,768]{1,0:T(8,128)(2,1)S(1)}, bf16[1024,768]{1,0:T(8,128)(2,1)S(1)}, u32[]{:S(2)}, u32[]{:S(2)}) collective-permute-start(bf16[1024,768]{1,0:T(8,128)(2,1)S(1)} %get-tuple-element.85.refs_3_), channel_id=1, source_target_pairs={{0,1},{1,0},{2,3},{3,2},{4,5},{5,4},{6,7},{7,6},{8,9},{9,8},{10,11... | collective-permute-start | bytes 4718600 | tf_op jit(solution)/shard_map/ppermute | solution.py:696
  42.0 26.7 %collective-permute-start.1 = (bf16[384,1536]{1,0:T(8,128)(2,1)S(1)}, bf16[384,1536]{1,0:T(8,128)(2,1)S(1)}, u32[]{:S(2)}, u32[]{:S(2)}) collective-permute-start(bf16[384,1536]{1,0:T(8,128)(2,1)S(1)} %get-tuple-element.84), channel_id=1, source_target_pairs={{0,2},{1,5},{2,0},{3,7},{4,6},{5,1},{6,4},{7,3},{8,10},{9,13},{10,... | collective-permute-start | bytes 3538952 | tf_op jit(solution)/shard_map/ppermute | solution.py:709
  48.7 8.1 %copy-start.3 = (f32[8,1536]{1,0:T(8,128)}, f32[8,1536]{1,0:T(8,128)S(1)}, u32[]{:S(2)}) copy-start(f32[8,1536]{1,0:T(8,128)S(1)} %get-tuple-element.92.refs_10_.refs_7_) | copy-start | bytes 147460
  48.7 31.3 %collective-permute-start.5 = (bf16[384,1536]{1,0:T(8,128)(2,1)S(1)}, bf16[384,1536]{1,0:T(8,128)(2,1)S(1)}, u32[]{:S(2)}, u32[]{:S(2)}) collective-permute-start(bf16[384,1536]{1,0:T(8,128)(2,1)S(1)} %get-tuple-element.108), channel_id=1, source_target_pairs={{0,8},{1,9},{2,10},{3,11},{4,12},{5,13},{6,14},{7,15},{8,0},{9,1},... | collective-permute-start | bytes 3538952 | tf_op jit(solution)/shard_map/ppermute | solution.py:709
  50.4 7.1 %copy-start.21 = (bf16[1024,768]{1,0:T(8,128)(2,1)S(1)}, bf16[1024,768]{1,0:T(8,128)(2,1)}, u32[]{:S(2)}) copy-start(bf16[1024,768]{1,0:T(8,128)(2,1)} %get-tuple-element.100.refs_7_) | copy-start | bytes 4718596
  50.4 7.1 %copy-start.23 = (bf16[1024,384]{1,0:T(8,128)(2,1)S(1)}, bf16[1024,384]{1,0:T(8,128)(2,1)}, u32[]{:S(2)}) copy-start(bf16[1024,384]{1,0:T(8,128)(2,1)} %get-tuple-element.96.refs_2_) | copy-start | bytes 2359300
  50.4 7.1 %copy-start.24 = (bf16[1024,384]{1,0:T(8,128)(2,1)S(1)}, bf16[1024,384]{1,0:T(8,128)(2,1)}, u32[]{:S(2)}) copy-start(bf16[1024,384]{1,0:T(8,128)(2,1)} %get-tuple-element.95.refs_1_) | copy-start | bytes 2359300
  50.4 7.0 %copy-start.25 = (bf16[1024,384]{1,0:T(8,128)(2,1)S(1)}, bf16[1024,384]{1,0:T(8,128)(2,1)}, u32[]{:S(2)}) copy-start(bf16[1024,384]{1,0:T(8,128)(2,1)} %get-tuple-element.97.refs_3_) | copy-start | bytes 2359300
  56.8 10.3 %copy-start.5 = (f32[8,768]{1,0:T(8,128)}, f32[8,768]{1,0:T(8,128)S(1)}, u32[]{:S(2)}) copy-start(f32[8,768]{1,0:T(8,128)S(1)} %get-tuple-element.101.refs_8_.refs_5_) | copy-start | bytes 73732
  56.9 11.9 %collective-permute-start.3 = (bf16[384,384]{1,0:T(8,128)(2,1)S(1)}, bf16[384,384]{1,0:T(8,128)(2,1)S(1)}, u32[]{:S(2)}, u32[]{:S(2)}) collective-permute-start(bf16[384,384]{1,0:T(8,128)(2,1)S(1)} %get-tuple-element.94), channel_id=1, source_target_pairs={{0,2},{1,5},{2,0},{3,7},{4,6},{5,1},{6,4},{7,3},{8,10},{9,13},{10,... | collective-permute-start | bytes 884744 | tf_op jit(solution)/shard_map/ppermute | solution.py:709
  67.2 12.9 %collective-permute-start.6 = (bf16[384,384]{1,0:T(8,128)(2,1)S(1)}, bf16[384,384]{1,0:T(8,128)(2,1)S(1)}, u32[]{:S(2)}, u32[]{:S(2)}) collective-permute-start(bf16[384,384]{1,0:T(8,128)(2,1)S(1)} %get-tuple-element.110), channel_id=1, source_target_pairs={{0,2},{1,5},{2,0},{3,7},{4,6},{5,1},{6,4},{7,3},{8,10},{9,13},{10,... | collective-permute-start | bytes 884744 | tf_op jit(solution)/shard_map/ppermute | solution.py:709
  69.1 10.9 %collective-permute-start.4 = (bf16[192,1536]{1,0:T(8,128)(2,1)S(1)}, bf16[192,1536]{1,0:T(8,128)(2,1)S(1)}, u32[]{:S(2)}, u32[]{:S(2)}) collective-permute-start(bf16[192,1536]{1,0:T(8,128)(2,1)S(1)} %get-tuple-element.106), channel_id=1, source_target_pairs={{0,4},{1,3},{2,6},{3,1},{4,0},{5,7},{6,2},{7,5},{8,12},{9,11},{10,... | collective-permute-start | bytes 1769480 | tf_op jit(solution)/shard_map/ppermute | solution.py:709
  79.5 12.7 %collective-permute-start.9 = (bf16[384,384]{1,0:T(8,128)(2,1)S(1)}, bf16[384,384]{1,0:T(8,128)(2,1)S(1)}, u32[]{:S(2)}, u32[]{:S(2)}) collective-permute-start(bf16[384,384]{1,0:T(8,128)(2,1)S(1)} %get-tuple-element.120), channel_id=1, source_target_pairs={{0,2},{1,5},{2,0},{3,7},{4,6},{5,1},{6,4},{7,3},{8,10},{9,13},{10,... | collective-permute-start | bytes 884744 | tf_op jit(solution)/shard_map/ppermute | solution.py:709
  80.5 12.1 %collective-permute-start.8 = (bf16[192,1536]{1,0:T(8,128)(2,1)S(1)}, bf16[192,1536]{1,0:T(8,128)(2,1)S(1)}, u32[]{:S(2)}, u32[]{:S(2)}) collective-permute-start(bf16[192,1536]{1,0:T(8,128)(2,1)S(1)} %get-tuple-element.118), channel_id=1, source_target_pairs={{0,2},{1,5},{2,0},{3,7},{4,6},{5,1},{6,4},{7,3},{8,10},{9,13},{10,... | collective-permute-start | bytes 1769480 | tf_op jit(solution)/shard_map/ppermute | solution.py:709
  82.1 10.1 %collective-permute-start.7 = (bf16[96,1536]{1,0:T(8,128)(2,1)S(1)}, bf16[96,1536]{1,0:T(8,128)(2,1)S(1)}, u32[]{:S(2)}, u32[]{:S(2)}) collective-permute-start(bf16[96,1536]{1,0:T(8,128)(2,1)S(1)} %get-tuple-element.116), channel_id=1, source_target_pairs={{0,8},{1,9},{2,10},{3,11},{4,12},{5,13},{6,14},{7,15},{8,0},{9,1},... | collective-permute-start | bytes 884744 | tf_op jit(solution)/shard_map/ppermute | solution.py:709
  91.6 7.5 %collective-permute-start.10 = (bf16[384,384]{1,0:T(8,128)(2,1)S(1)}, bf16[384,384]{1,0:T(8,128)(2,1)S(1)}, u32[]{:S(2)}, u32[]{:S(2)}) collective-permute-start(bf16[384,384]{1,0:T(8,128)(2,1)S(1)} %get-tuple-element.125), channel_id=1, source_target_pairs={{0,2},{1,5},{2,0},{3,7},{4,6},{5,1},{6,4},{7,3},{8,10},{9,13},{10,... | collective-permute-start | bytes 884744 | tf_op jit(solution)/shard_map/ppermute | solution.py:709
  93.4 17.3 %collective-permute-start.14 = (bf16[48,1536]{1,0:T(8,128)(2,1)S(1)}, bf16[48,1536]{1,0:T(8,128)(2,1)S(1)}, u32[]{:S(2)}, u32[]{:S(2)}) collective-permute-start(bf16[48,1536]{1,0:T(8,128)(2,1)S(1)} %get-tuple-element.129.refs_4_), channel_id=1, source_target_pairs={{0,16},{1,17},{2,18},{3,19},{4,20},{5,21},{6,22},{7,23},{8,24},{9,... | collective-permute-start | bytes 442376 | tf_op jit(solution)/shard_map/ppermute | solution.py:709
  99.0 6.4 %collective-permute-start.15 = (bf16[1024,768]{1,0:T(8,128)(2,1)S(1)}, bf16[1024,768]{1,0:T(8,128)(2,1)S(1)}, u32[]{:S(2)}, u32[]{:S(2)}) collective-permute-start(bf16[1024,768]{1,0:T(8,128)(2,1)S(1)} %first.1.refs_8_.refs_2_), channel_id=1, source_target_pairs={{0,1},{1,0},{2,3},{3,2},{4,5},{5,4},{6,7},{7,6},{8,9},{9,8},{10,11... | collective-permute-start | bytes 4718600 | tf_op jit(solution)/shard_map/ppermute | solution.py:696
  99.3 13.2 %collective-permute-start.12 = (bf16[192,1536]{1,0:T(8,128)(2,1)S(1)}, bf16[192,1536]{1,0:T(8,128)(2,1)S(1)}, u32[]{:S(2)}, u32[]{:S(2)}) collective-permute-start(bf16[192,1536]{1,0:T(8,128)(2,1)S(1)} %get-tuple-element.130.refs_2_), channel_id=1, source_target_pairs={{0,4},{1,3},{2,6},{3,1},{4,0},{5,7},{6,2},{7,5},{8,12},{9,11},{10,... | collective-permute-start | bytes 1769480 | tf_op jit(solution)/shard_map/ppermute | solution.py:709
  100.3 12.2 %collective-permute-start.13 = (bf16[96,1536]{1,0:T(8,128)(2,1)S(1)}, bf16[96,1536]{1,0:T(8,128)(2,1)S(1)}, u32[]{:S(2)}, u32[]{:S(2)}) collective-permute-start(bf16[96,1536]{1,0:T(8,128)(2,1)S(1)} %get-tuple-element.133), channel_id=1, source_target_pairs={{0,4},{1,3},{2,6},{3,1},{4,0},{5,7},{6,2},{7,5},{8,12},{9,11},{10,... | collective-permute-start | bytes 884744 | tf_op jit(solution)/shard_map/ppermute | solution.py:709
  104.8 12.8 %collective-permute-start.11 = (bf16[1024,768]{1,0:T(8,128)(2,1)S(1)}, bf16[1024,768]{1,0:T(8,128)(2,1)S(1)}, u32[]{:S(2)}, u32[]{:S(2)}) collective-permute-start(bf16[1024,768]{1,0:T(8,128)(2,1)S(1)} %down.1.refs_11_.refs_5_), channel_id=1, source_target_pairs={{0,1},{1,0},{2,3},{3,2},{4,5},{5,4},{6,7},{7,6},{8,9},{9,8},{10,11... | collective-permute-start | bytes 4718600 | tf_op jit(solution)/shard_map/ppermute | solution.py:696
  109.6 11.9 %collective-permute-start.16 = (f32[16,768]{1,0:T(8,128)S(1)}, f32[16,768]{1,0:T(8,128)S(1)}, u32[]{:S(2)}, u32[]{:S(2)}) collective-permute-start(f32[16,768]{1,0:T(8,128)S(1)} %get-tuple-element.136.refs_2_.refs_0_), channel_id=1, source_target_pairs={{0,2},{2,0},{4,6},{6,4},{8,10},{10,8},{12,14},{14,12},{16,18},{18,... | collective-permute-start | bytes 147464 | tf_op jit(solution)/shard_map/ppermute | solution.py:696
  114.2 11.9 %collective-permute-start.18 = (bf16[96,1536]{1,0:T(8,128)(2,1)S(1)}, bf16[96,1536]{1,0:T(8,128)(2,1)S(1)}, u32[]{:S(2)}, u32[]{:S(2)}) collective-permute-start(bf16[96,1536]{1,0:T(8,128)(2,1)S(1)} %get-tuple-element.140), channel_id=1, source_target_pairs={{0,8},{1,9},{2,10},{3,11},{4,12},{5,13},{6,14},{7,15},{8,0},{9,1},... | collective-permute-start | bytes 884744 | tf_op jit(solution)/shard_map/ppermute | solution.py:709
  115.9 14.0 %collective-permute-start.20 = (bf16[48,1536]{1,0:T(8,128)(2,1)S(1)}, bf16[48,1536]{1,0:T(8,128)(2,1)S(1)}, u32[]{:S(2)}, u32[]{:S(2)}) collective-permute-start(bf16[48,1536]{1,0:T(8,128)(2,1)S(1)} %get-tuple-element.137.refs_7_), channel_id=1, source_target_pairs={{0,16},{1,17},{2,18},{3,19},{4,20},{5,21},{6,22},{7,23},{8,24},{9,... | collective-permute-start | bytes 442376 | tf_op jit(solution)/shard_map/ppermute | solution.py:709
  122.9 4.4 %collective-permute-start.17 = (f32[16,768]{1,0:T(8,128)S(1)}, f32[16,768]{1,0:T(8,128)S(1)}, u32[]{:S(2)}, u32[]{:S(2)}) collective-permute-start(f32[16,768]{1,0:T(8,128)S(1)} %add.71.refs_2_.refs_0_), channel_id=1, source_target_pairs={{0,4},{2,6},{4,0},{6,2},{8,12},{10,14},{12,8},{14,10},{16,20},{18,... | collective-permute-start | bytes 147464 | tf_op jit(solution)/shard_map/ppermute | solution.py:696
  126.9 8.9 %collective-permute-start.22 = (bf16[48,1536]{1,0:T(8,128)(2,1)S(1)}, bf16[48,1536]{1,0:T(8,128)(2,1)S(1)}, u32[]{:S(2)}, u32[]{:S(2)}) collective-permute-start(bf16[48,1536]{1,0:T(8,128)(2,1)S(1)} %get-tuple-element.141.refs_2_), channel_id=1, source_target_pairs={{0,16},{1,17},{2,18},{3,19},{4,20},{5,21},{6,22},{7,23},{8,24},{9,... | collective-permute-start | bytes 442376 | tf_op jit(solution)/shard_map/ppermute | solution.py:709
  127.3 4.6 %collective-permute-start.19 = (f32[16,768]{1,0:T(8,128)S(1)}, f32[16,768]{1,0:T(8,128)S(1)}, u32[]{:S(2)}, u32[]{:S(2)}) collective-permute-start(f32[16,768]{1,0:T(8,128)S(1)} %add.72.refs_2_.refs_0_), channel_id=1, source_target_pairs={{0,8},{2,10},{4,12},{6,14},{8,0},{10,2},{12,4},{14,6},{16,24},{18,... | collective-permute-start | bytes 147464 | tf_op jit(solution)/shard_map/ppermute | solution.py:696
  132.9 5.0 %collective-permute-start.21 = (f32[16,768]{1,0:T(8,128)S(1)}, f32[16,768]{1,0:T(8,128)S(1)}, u32[]{:S(2)}, u32[]{:S(2)}) collective-permute-start(f32[16,768]{1,0:T(8,128)S(1)} %add.73.refs_2_.refs_0_), channel_id=1, source_target_pairs={{0,16},{2,18},{4,20},{6,22},{8,24},{10,26},{12,28},{14,30},{16,0},... | collective-permute-start | bytes 147464 | tf_op jit(solution)/shard_map/ppermute | solution.py:696
  (21 other events, 68.7 us)
where the time goes:
time: 141 us
  Pallas kernels  95.9 us (68%)
  starting transfers between devices  28.1 us (20%)
  local copies, waits for them, and re-layouts  8.23 us (6%)
  waiting for transfers between devices  7.32 us (5%)
    pallas_call x24, Pallas kernels, call(): pl.pallas_call(body, name=name, out_shape=tuple((pins[m.kind](m.shape, m....  95.9 us
    ppermute x15, starting transfers between devices, exchange(): self.came = lax.ppermute(self.send, ('dp', 'mp'), pairs)  19.7 us
    ppermute x8, starting transfers between devices, swap(): return lax.ppermute(values, axis, [(i, i ^ 1 << bit) for i in range(size)])  8.32 us
    unnamed x60, local copies, waits for them, and re-layouts  6.38 us
    ppermute x8, waiting for transfers between devices, swap(): return lax.ppermute(values, axis, [(i, i ^ 1 << bit) for i in range(size)])  3.77 us
    ppermute x15, waiting for transfers between devices, exchange(): self.came = lax.ppermute(self.send, ('dp', 'mp'), pairs)  3.55 us
  transfers between devices with their start and end apart: 23, of which 6 were waited for; matrix products, arithmetic and copies ran while one was open for 0% of the time, Pallas kernels for 43%

commit v1 on v0

--- a/solution.py
+++ b/solution.py
@@ -11,7 +11,7 @@
 EPSILON = 1e-06
 MASKED = 1e30
 LANES = 128
-TOTALS_AT = 32
+TOTALS_AT = (32, 48, 64)
 bf16 = jnp.bfloat16
 f32 = jnp.float32
 
@@ -97,7 +97,7 @@
         pass
 
 
-pins = {"v": pltpu.VMEM, "h": pltpu.HBM, "c": pltpu.HBM, "p": pltpu.VMEM, "q": pltpu.HBM}
+pins = {"v": pltpu.VMEM, "h": pltpu.HBM, "c": pltpu.HBM, "p": pltpu.VMEM, "q": pltpu.HBM, "x": pltpu.HBM}
 
 
 def pinned(given):
@@ -112,7 +112,7 @@
 
 def call(chain, kernel, name, outs, args, scratch=(), limit=9, covers=True):
     if chain.last is not None and all(g.array is not chain.last for g in args):
-        args = [*args, Given(chain.last, "w")]
+        args = [*args, Given(chain.last, chain.kind)]
     ahead = [m for m in outs if m.kind == "p"]
     kernel_args = len(args)
     args = [*args, *(Given(m.source, "q") for m in ahead)]
@@ -145,7 +145,7 @@
         for g, ref in zip(args, ins):
             if g.kind == "h":
                 given.append(Arriving(arrivals.pop(0), ref, ready.pop(0), g.pieces, g.columns))
-            elif g.kind not in "wq":
+            elif g.kind not in "wxq":
                 given.append(ref if g.kind == "s" else Arriving(ref))
         waiting = [one for one in given if isinstance(one, Arriving) and one.pending]
         small = [one for one in waiting if len(one.ref.shape) == 1]
@@ -178,7 +178,7 @@
         for copy in fetches:
             copy.wait()
 
-    spaces = {"s": pltpu.SMEM, "v": pltpu.VMEM, "h": pltpu.HBM, "c": pltpu.HBM, "w": pl.ANY, "p": pltpu.VMEM, "q": pltpu.HBM}
+    spaces = {"s": pltpu.SMEM, "v": pltpu.VMEM, "h": pltpu.HBM, "c": pltpu.HBM, "w": pl.ANY, "p": pltpu.VMEM, "q": pltpu.HBM, "x": pltpu.HBM}
     results = pl.pallas_call(
         body,
         name=name,
@@ -189,7 +189,9 @@
         compiler_params=pltpu.CompilerParams(vmem_limit_bytes=limit << 20),
         cost_estimate=pl.CostEstimate(flops=2 * 10**10 * covers, bytes_accessed=1, transcendentals=0),
     )(*(pinned(g) for g in args))
-    chain.last = min(results, key=lambda result: result.size * result.dtype.itemsize)
+    size = lambda pair: pair[0].size * pair[0].dtype.itemsize
+    chain.last, kind = min(((result, m.kind) for m, result in zip(outs, results)), key=size)
+    chain.kind = "x" if kind in "hc" else "w"
     return results
 
 
@@ -244,14 +246,18 @@
     return ref[...][None, :]
 
 
-def log_total_lanes(feature, head, log_total):
-    lane = lane_of(feature.shape)
-    rest = -log_total
-    for piece in range(3):
-        part_of = rest.astype(bf16).astype(f32)
-        rest = rest - part_of
-        feature = jnp.where(lane == TOTALS_AT + 3 * head + piece, part_of, feature)
-    return feature
+def is_total(lane, head):
+    found = lane == TOTALS_AT[0] + head
+    for start in TOTALS_AT[1:]:
+        found = found | (lane == start + head)
+    return found
+
+
+def in_pieces(values, lane):
+    first = values.astype(bf16).astype(f32)
+    second = (values - first).astype(bf16).astype(f32)
+    third = values - first - second
+    return jnp.where(lane < TOTALS_AT[1], first, jnp.where(lane < TOTALS_AT[2], second, third))
 
 
 def attend(queries, keys, values, id_k, mixed, features, block):
@@ -261,7 +267,7 @@
     def _(index):
         span = row_span(index, block)
         ids = features[span, :]
-        feature = ids.astype(f32)
+        feature = jnp.zeros((block, LANES), f32)
         for pair in range(queries.shape[1] // LANES):
             cols = slice(pair * LANES, (pair + 1) * LANES)
             wide_keys = jnp.concatenate([keys[:, cols], id_k[...]], axis=1)
@@ -275,18 +281,18 @@
                 term = dot(exponent.astype(bf16), head_half(value, half))
                 total = term if total is None else total + term
                 inverses.append(1.0 / totals)
-                feature = log_total_lanes(feature, 2 * pair + half, jnp.log(totals))
+                feature = jnp.where(is_total(lane, 2 * pair + half), -jnp.log(totals), feature)
             mixed[span, cols] = (
                 total * jnp.where(lane < HEAD_DIM, inverses[0], inverses[1])
             ).astype(bf16)
-        features[span, :] = feature.astype(bf16)
+        features[span, :] = ids + in_pieces(feature, lane).astype(bf16)
 
 
 def attend_shifted(queries, keys, values, id_k, mixed, features, block):
     @pl.loop(0, queries.shape[0] // block)
     def _(index):
         span = row_span(index, block)
-        ids = jnp.where(lane_of((block, LANES)) < TOTALS_AT, features[span, :], jnp.zeros((), bf16))
+        ids = features[span, :]
 
         @pl.loop(0, queries.shape[1] // LANES)
         def _(pair):
@@ -300,9 +306,9 @@
                 totals = jnp.sum(exponent, axis=1, keepdims=True)
                 term = dot(exponent.astype(bf16), head_half(values[:, cols], half)) / totals
                 total = term if total is None else total + term
-                features[span, :] = log_total_lanes(
-                    features[span, :].astype(f32), 2 * pair + half, largest + jnp.log(totals)
-                ).astype(bf16)
+                lane = lane_of((block, LANES))
+                feature = jnp.where(is_total(lane, 2 * pair + half), -(largest + jnp.log(totals)), 0.0)
+                features[span, :] += in_pieces(feature, lane).astype(bf16)
             mixed[span, cols] = total.astype(bf16)
 
 
@@ -334,9 +340,8 @@
     block = rows // tokens.pieces
     gain, bias = gain(), bias()
 
-    @pl.loop(0, tokens.pieces)
-    def _(index):
-        span = row_span(index, block)
+    def norm(index):
+        span = row_span(index, block) if not isinstance(index, int) else pl.ds(index * block, block)
         row = index * block + lax.broadcasted_iota(jnp.int32, (block, LANES), 0)
         same = (row >= starts) & (row < ends)
         features.ref[span, :] = same.astype(f32).astype(bf16)
@@ -346,11 +351,8 @@
         hidden.send(index)
         id_k.send(index)
 
-    weight, qv_bias = weight(), qv_bias()
-
-    @pl.loop(0, tokens.pieces)
-    def _(index):
-        span = row_span(index, block)
+    def project(index):
+        span = row_span(index, block) if not isinstance(index, int) else pl.ds(index * block, block)
         low = hidden.ref[span, :]
         raised = (dot(low, weight[0]) + qv_bias[0:1, :]).astype(bf16)
         queries.ref[span, :] = (raised.astype(f32) * scale).astype(bf16)
@@ -359,12 +361,22 @@
         for one in (queries, keys, values):
             one.send(index)
 
+    norm(0)
+    weight, qv_bias = weight(), qv_bias()
+
+    @pl.loop(0, tokens.pieces - 1)
+    def _(index):
+        project(index)
+        norm(index + 1)
+
+    project(tokens.pieces - 1)
+
     bounded = largest_norms(queries.ref) * largest_norms(keys.ref) <= 4000.0
     operands = [one.ref for one in (queries, keys, values, id_k, mixed, features)]
 
     @pl.when(bounded)
     def _():
-        attend(*operands, rows // 2)
+        attend(*operands, rows // 4)
 
     @pl.when(jnp.logical_not(bounded))
     def _():
@@ -546,9 +558,8 @@
     key = keys[:, cols]
     turned[...] = key.T
     for half in range(2):
-        at = TOTALS_AT + 3 * (2 * pair + half)
         wide_keys[half, :, :LANES] = key
-        wide_keys[half, :, LANES:] = id_k[...] + ((lane >= at) & (lane < at + 3)).astype(f32).astype(bf16)
+        wide_keys[half, :, LANES:] = id_k[...] + is_total(lane, 2 * pair + half).astype(f32).astype(bf16)
     block = rows // 2
     key_total[...] = jnp.zeros_like(key_total)
     value_total[...] = jnp.zeros_like(value_total)
@@ -653,6 +664,19 @@
 
 def add_kernel(given, made):
     made[0].ref[...] = given[0]()[...] + given[1]()[...]
+
+
+def spread_kernel(given, made):
+    total = given[0]()[...] + given[1]()[...]
+    *singles, qv, ups = made
+    width = total.shape[1]
+    for row, one in zip((0, 1, 3, 4, 5, 6), singles):
+        one.ref[...] = total[row]
+    local = qv.ref.shape[1]
+    for row in range(2):
+        qv.ref[row : row + 1] = total[2:3, row * local : (row + 1) * local]
+    for row in range(ups.ref.shape[0] // width):
+        ups.ref[pl.ds(row * width, width)] = total[7 + row]
 
 
 def output_kernel(given, made):
@@ -1012,23 +1036,30 @@
     qkv_total, out_total = finish(
         chain, [flow_qkv], final_qkv_kernel, [(3, mine, local), (mine, local)]
     )
-    all_sum_step(bits[-1])
-    ups = units // width
+    *singles, qv_sum, up_sum = call(
+        chain,
+        spread_kernel,
+        "spread",
+        [*[Made((width,), f32, "h")] * 6, Made((2, local), f32, "h"), Made((units,), f32, "h")],
+        [near(vectors), near(swap(vectors, "dp", bits[-1], n_dp))],
+        limit=4,
+    )
+    gain_one, bias_one, gain_two, bias_two, out_bias_sum, down_bias_sum = singles
     return (
         output,
         tokens_grad,
-        vectors[0],
-        vectors[1],
+        gain_one,
+        bias_one,
         jnp.transpose(qkv_total, (1, 0, 2)),
-        vectors[2].reshape(2, local),
+        qv_sum,
         out_total.T,
-        vectors[5],
-        vectors[3],
-        vectors[4],
+        out_bias_sum,
+        gain_two,
+        bias_two,
         up_total,
-        vectors[7 : 7 + ups].reshape(-1),
+        up_sum,
         down_total.T,
-        vectors[6],
+        down_bias_sum,
     )
 
 

time: 141 us -> 136 us (0.965)
  local copies, waits for them, and re-layouts: 8.23 us -> 1.06 us
  waiting for transfers between devices: 7.32 us -> 9.68 us
    unnamed x60 -> x50, local copies, waits for them, and re-layouts: 6.38 us -> 1.06 us
    ppermute x15, waiting for transfers between devices: 3.55 us -> 6.29 us  [exchange(): self.came = lax.ppermute(self.send, ('dp', 'mp'), pairs)]
  transfers between devices with their start and end apart: 23 -> 23, of which waited for: 6 -> 5; matrix products, arithmetic and copies ran while one was open for 0% -> 0% of each run, Pallas kernels for 43% -> 44%
where the time goes in v1:
time: 136 us
  Pallas kernels  95.7 us (70%)
  starting transfers between devices  28.2 us (21%)
  waiting for transfers between devices  9.68 us (7%)
    pallas_call x24, Pallas kernels, call(): pl.pallas_call(body, name=name, out_shape=tuple((pins[m.kind](m.shape, m....  95.7 us
    ppermute x15, starting transfers between devices, exchange(): self.came = lax.ppermute(self.send, ('dp', 'mp'), pairs)  19.7 us
    ppermute x8, starting transfers between devices, swap(): return lax.ppermute(values, axis, [(i, i ^ 1 << bit) for i in range(size)])  8.45 us
    ppermute x15, waiting for transfers between devices, exchange(): self.came = lax.ppermute(self.send, ('dp', 'mp'), pairs)  6.29 us
    ppermute x8, waiting for transfers between devices, swap(): return lax.ppermute(values, axis, [(i, i ^ 1 << bit) for i in range(size)])  3.38 us
  transfers between devices with their start and end apart: 23, of which 5 were waited for; matrix products, arithmetic and copies ran while one was open for 0% of the time, Pallas kernels for 44%

profile of v1, /device:TPU:0, one launch (start us, length us, event | category | flops | bytes accessed | tf_op | source)
XLA Modules:
  0.0 135.9 jit_solution(9709337311678780817)
XLA Ops:
  1.3 17.8 %qkv_attention.1 = (bf16[1024,768]{1,0:T(8,128)(2,1)}, bf16[1024,384]{1,0:T(8,128)(2,1)}, bf16[1024,384]{1,0:T(8,128)(2,1)}, bf16[1024,384]{1,0:T(8,128)(2,1)}, ...) custom-call(s32[1,16]{1,0:T(1,128)S(1)} %copy-done.12, ...), custom_call_target="tpu_custom_call" | custom-call | flops 20000000000 | bytes 1 | tf_op jit(solution)/shard_map/qkv_attention/pallas_call | solution.py:182
  19.6 3.0 %collective-permute-done.refs_7_.refs_4_ = bf16[1024,768]{1,0:T(8,128)(2,1)S(1)} collective-permute-done((bf16[1024,768]{1,0:T(8,128)(2,1)S(1)}, bf16[1024,768]{1,0:T(8,128)(2,1)S(1)}, u32[]{:S(2)}, u32[]{:S(2)}) %collective-permute-start) | collective-permute-done | bytes 1572896 | tf_op jit(solution)/shard_map/ppermute | solution.py:720
  22.7 16.8 %mlp.1 = (bf16[1024,768]{1,0:T(8,128)(2,1)S(1)}, bf16[1024,768]{1,0:T(8,128)(2,1)}, f32[1024,128]{1,0:T(8,128)}, bf16[1024,1536]{1,0:T(8,128)(2,1)}, bf16[1024,1...) custom-call(s32[1,16]{1,0:T(1,128)S(1)} %copy-done.13, ...), custom_call_target="tpu_custom_call" | custom-call | flops 20000000000 | bytes 1 | tf_op jit(solution)/shard_map/mlp/pallas_call | solution.py:182
  39.9 2.6 %collective-permute-start.1 = (bf16[384,1536]{1,0:T(8,128)(2,1)S(1)}, bf16[384,1536]{1,0:T(8,128)(2,1)S(1)}, u32[]{:S(2)}, u32[]{:S(2)}) collective-permute-start(bf16[384,1536]{1,0:T(8,128)(2,1)S(1)} %get-tuple-element.92), channel_id=1, source_target_pairs={{0,2},{1,5},{2,0},{3,7},{4,6},{5,1},{6,4},{7,3},{8,10},{9,13},{10,... | collective-permute-start | bytes 3538952 | tf_op jit(solution)/shard_map/ppermute | solution.py:733
  42.5 4.0 %up_grad.1 = (bf16[384,1536]{1,0:T(8,128)(2,1)S(1)}, bf16[384,1536]{1,0:T(8,128)(2,1)S(1)}, f32[8,1536]{1,0:T(8,128)S(1)}) custom-call(s32[16]{0:T(128)S(1)} %get-tuple-element.162.refs_0_, bf16[1024,768]{1,0:T(8,128)(2,1)S(1)} %get-tuple-element.97.refs_1_, bf16[1024,1536]{1,0:T(8,128)(2,1)S(1)} %get-tuple-element.98.refs_2_, ...), custom_call_target="tpu_custom_call" | custom-call | flops 20000000000 | bytes 1 | tf_op jit(solution)/shard_map/up_grad/pallas_call | solution.py:182
  46.6 1.6 %collective-permute-start.5 = (bf16[384,1536]{1,0:T(8,128)(2,1)S(1)}, bf16[384,1536]{1,0:T(8,128)(2,1)S(1)}, u32[]{:S(2)}, u32[]{:S(2)}) collective-permute-start(bf16[384,1536]{1,0:T(8,128)(2,1)S(1)} %get-tuple-element.116), channel_id=1, source_target_pairs={{0,8},{1,9},{2,10},{3,11},{4,12},{5,13},{6,14},{7,15},{8,0},{9,1},... | collective-permute-start | bytes 3538952 | tf_op jit(solution)/shard_map/ppermute | solution.py:733
  48.4 6.4 %middle.1 = (f32[1024,768]{1,0:T(8,128)}, bf16[1024,384]{1,0:T(8,128)(2,1)S(1)}, f32[8,768]{1,0:T(8,128)S(1)}, bf16[384,384]{1,0:T(8,128)(2,1)S(1)}, bf16[384,384]{1,0:T(8,128)(2,1)S(1)}) custom-call(s32[1,16]{1,0:T(1,128)S(1)} %copy-done.13, s32[16]{0:T(128)S(1)} %get-tuple-element.163.refs_1_.refs_0_, f32[768]{0:T(1024)} %refs_2_.6, ...), custom_call_target="tpu_custom_call" | custom-call | flops 20000000000 | bytes 1 | tf_op jit(solution)/shard_map/middle/pallas_call | solution.py:182
  55.4 9.7 %attention_back0.1 = (bf16[1024,384]{1,0:T(8,128)(2,1)S(1)}, f32[8,384]{1,0:T(8,128)S(1)}, bf16[384,384]{1,0:T(8,128)(2,1)S(1)}, bf16[384,384]{1,0:T(8,128)(2,1)S(1)}, bf16[784,1024]{1,0:T(8,128)(2,1)}) custom-call(s32[16]{0:T(128)S(1)} %get-tuple-element.163.refs_1_.refs_0_, bf16[1024,384]{1,0:T(8,128)(2,1)S(1)} %copy-done.20, ...), custom_call_target="tpu_custom_call" | custom-call | flops 20000000000 | bytes 1 | tf_op jit(solution)/shard_map/attention_back0/pallas_call | solution.py:182
  65.1 1.6 %collective-permute-start.6 = (bf16[384,384]{1,0:T(8,128)(2,1)S(1)}, bf16[384,384]{1,0:T(8,128)(2,1)S(1)}, u32[]{:S(2)}, u32[]{:S(2)}) collective-permute-start(bf16[384,384]{1,0:T(8,128)(2,1)S(1)} %get-tuple-element.118), channel_id=1, source_target_pairs={{0,2},{1,5},{2,0},{3,7},{4,6},{5,1},{6,4},{7,3},{8,10},{9,13},{10,... | collective-permute-start | bytes 884744 | tf_op jit(solution)/shard_map/ppermute | solution.py:733
  67.1 1.6 %collective-permute-start.4 = (bf16[192,1536]{1,0:T(8,128)(2,1)S(1)}, bf16[192,1536]{1,0:T(8,128)(2,1)S(1)}, u32[]{:S(2)}, u32[]{:S(2)}) collective-permute-start(bf16[192,1536]{1,0:T(8,128)(2,1)S(1)} %get-tuple-element.114), channel_id=1, source_target_pairs={{0,4},{1,3},{2,6},{3,1},{4,0},{5,7},{6,2},{7,5},{8,12},{9,11},{10,... | collective-permute-start | bytes 1769480 | tf_op jit(solution)/shard_map/ppermute | solution.py:733
  68.7 8.7 %attention_back1.1 = (bf16[1024,384]{1,0:T(8,128)(2,1)S(1)}, f32[8,384]{1,0:T(8,128)S(1)}, bf16[384,384]{1,0:T(8,128)(2,1)S(1)}, bf16[384,384]{1,0:T(8,128)(2,1)S(1)}) custom-call(s32[16]{0:T(128)S(1)} %get-tuple-element.163.refs_1_.refs_0_, bf16[1024,384]{1,0:T(8,128)(2,1)S(1)} %copy-done.20, bf16[1024,384]{1,0:T(8,128)(2,1)S(1)} %copy-done.19, ...), custom_call_target="tpu_custom_call" | custom-call | flops 20000000000 | bytes 1 | tf_op jit(solution)/shard_map/attention_back1/pallas_call | solution.py:182
  78.4 1.6 %collective-permute-start.8 = (bf16[192,1536]{1,0:T(8,128)(2,1)S(1)}, bf16[192,1536]{1,0:T(8,128)(2,1)S(1)}, u32[]{:S(2)}, u32[]{:S(2)}) collective-permute-start(bf16[192,1536]{1,0:T(8,128)(2,1)S(1)} %get-tuple-element.126), channel_id=1, source_target_pairs={{0,2},{1,5},{2,0},{3,7},{4,6},{5,1},{6,4},{7,3},{8,10},{9,13},{10,... | collective-permute-start | bytes 1769480 | tf_op jit(solution)/shard_map/ppermute | solution.py:733
  80.4 9.0 %attention_back2.1 = (bf16[1024,384]{1,0:T(8,128)(2,1)S(1)}, f32[8,384]{1,0:T(8,128)S(1)}, bf16[384,384]{1,0:T(8,128)(2,1)S(1)}, bf16[384,384]{1,0:T(8,128)(2,1)S(1)}) custom-call(s32[16]{0:T(128)S(1)} %get-tuple-element.163.refs_1_.refs_0_, bf16[1024,384]{1,0:T(8,128)(2,1)S(1)} %copy-done.20, bf16[1024,384]{1,0:T(8,128)(2,1)S(1)} %copy-done.19, ...), custom_call_target="tpu_custom_call" | custom-call | flops 20000000000 | bytes 1 | tf_op jit(solution)/shard_map/attention_back2/pallas_call | solution.py:182
  90.5 0.8 fold.8
  91.3 2.6 %collective-permute-start.14 = (bf16[48,1536]{1,0:T(8,128)(2,1)S(1)}, bf16[48,1536]{1,0:T(8,128)(2,1)S(1)}, u32[]{:S(2)}, u32[]{:S(2)}) collective-permute-start(bf16[48,1536]{1,0:T(8,128)(2,1)S(1)} %get-tuple-element.137.refs_4_), channel_id=1, source_target_pairs={{0,16},{1,17},{2,18},{3,19},{4,20},{5,21},{6,22},{7,23},{8,24},{9,... | collective-permute-start | bytes 442376 | tf_op jit(solution)/shard_map/ppermute | solution.py:733
  94.0 2.9 %first.1.refs_8_.refs_2_ = bf16[1024,768]{1,0:T(8,128)(2,1)S(1)} custom-call(bf16[1024,384]{1,0:T(8,128)(2,1)S(1)} %get-tuple-element.134.refs_0_, bf16[1024,384]{1,0:T(8,128)(2,1)S(1)} %get-tuple-element.135.refs_1_, bf16[1024,384]{1,0:T(8,128)(2,1)S(1)} %get-tuple-element.136.refs_2_, bf16[3,768,384]{2,1,0:T(8,128)(2,1)S(1)} %bitcast.5, ...), custom_call_target="tpu_custom_call" | custom-call | flops 20000000000 | bytes 1 | tf_op jit(solution)/shard_map/first/pallas_call | solution.py:182
  97.2 1.0 collective-permute-start.12
  98.2 1.1 collective-permute-start.13
  99.6 3.1 %down.1.refs_11_.refs_5_ = bf16[1024,768]{1,0:T(8,128)(2,1)S(1)} custom-call(bf16[1536,768]{1,0:T(8,128)(2,1)S(1)} %copy-done.6, bf16[1024,1536]{1,0:T(8,128)(2,1)S(1)} %copy-done.14, bf16[192,1536]{1,0:T(8,128)(2,1)S(1)} %get-tuple-element.138.refs_2_), custom_call_target="tpu_custom_call" | custom-call | flops 20000000000 | bytes 1 | tf_op jit(solution)/shard_map/down/pallas_call | solution.py:182
  103.3 4.2 %last.1 = (f32[1024,768]{1,0:T(8,128)}, f32[16,768]{1,0:T(8,128)S(1)}) custom-call(f32[768]{0:T(1024)} %refs_0_.10, bf16[1024,768]{1,0:T(8,128)(2,1)S(1)} %copy-done.1, bf16[1024,768]{1,0:T(8,128)(2,1)S(1)} %first.1.refs_8_.refs_2_, bf16[1024,768]{1,0:T(8,128)(2,1)S(1)} %collective-permute-done.15.refs_3_, f32[1024,768]{1,0:T(8,128)S(1)} %copy-done, ...), custom_call_target="tpu_custom_call" | custom-call | bytes 1 | tf_op jit(solution)/shard_map/last/pallas_call | solution.py:182
  107.5 1.2 collective-permute-start.16
  108.7 1.7 %final.3.refs_4_ = f32[48,1536]{1,0:T(8,128)} custom-call(f32[48,1536]{1,0:T(8,128)} %get-tuple-element.142.refs_0_, bf16[48,1536]{1,0:T(8,128)(2,1)S(1)} %collective-permute-done.14.refs_1_, f32[16,768]{1,0:T(8,128)S(1)} %get-tuple-element.144.refs_2_.refs_0_), custom_call_target="tpu_custom_call" | custom-call | bytes 1 | tf_op jit(solution)/shard_map/final/pallas_call | solution.py:182
  111.2 1.6 %collective-permute-start.18 = (bf16[96,1536]{1,0:T(8,128)(2,1)S(1)}, bf16[96,1536]{1,0:T(8,128)(2,1)S(1)}, u32[]{:S(2)}, u32[]{:S(2)}) collective-permute-start(bf16[96,1536]{1,0:T(8,128)(2,1)S(1)} %get-tuple-element.148), channel_id=1, source_target_pairs={{0,8},{1,9},{2,10},{3,11},{4,12},{5,13},{6,14},{7,15},{8,0},{9,1},... | collective-permute-start | bytes 884744 | tf_op jit(solution)/shard_map/ppermute | solution.py:733
  112.8 1.7 %collective-permute-start.20 = (bf16[48,1536]{1,0:T(8,128)(2,1)S(1)}, bf16[48,1536]{1,0:T(8,128)(2,1)S(1)}, u32[]{:S(2)}, u32[]{:S(2)}) collective-permute-start(bf16[48,1536]{1,0:T(8,128)(2,1)S(1)} %get-tuple-element.145.refs_7_), channel_id=1, source_target_pairs={{0,16},{1,17},{2,18},{3,19},{4,20},{5,21},{6,22},{7,23},{8,24},{9,... | collective-permute-start | bytes 442376 | tf_op jit(solution)/shard_map/ppermute | solution.py:733
  114.5 3.9 %output.1.refs_2_ = bf16[1024,768]{1,0:T(8,128)(2,1)} custom-call(f32[768]{0:T(1024)} %refs_0_.11, f32[768]{0:T(1024)} %refs_1_.5, bf16[1024,768]{1,0:T(8,128)(2,1)} %refs_2_.7, bf16[1024,768]{1,0:T(8,128)(2,1)} %copy-done.9, bf16[1024,768]{1,0:T(8,128)(2,1)} %copy-done.10, bf16[1024,768]{1,0:T(8,128)(2,1)S(1)} %down.1.refs_11_.refs_5_, ...), custom_call_target="tpu_custom_call" | custom-call | flops 20000000000 | bytes 1 | tf_op jit(solution)/shard_map/output/pallas_call | solution.py:182
  118.4 1.0 collective-permute-start.17
  119.5 3.6 %collective-permute-done.18.refs_1_ = bf16[96,1536]{1,0:T(8,128)(2,1)S(1)} collective-permute-done((bf16[96,1536]{1,0:T(8,128)(2,1)S(1)}, bf16[96,1536]{1,0:T(8,128)(2,1)S(1)}, u32[]{:S(2)}, u32[]{:S(2)}) %collective-permute-start.18) | collective-permute-done | bytes 294944 | tf_op jit(solution)/shard_map/ppermute | solution.py:733
  124.3 2.5 %collective-permute-start.19 = (f32[16,768]{1,0:T(8,128)S(1)}, f32[16,768]{1,0:T(8,128)S(1)}, u32[]{:S(2)}, u32[]{:S(2)}) collective-permute-start(f32[16,768]{1,0:T(8,128)S(1)} %add.64.refs_2_.refs_0_), channel_id=1, source_target_pairs={{0,8},{2,10},{4,12},{6,14},{8,0},{10,2},{12,4},{14,6},{16,24},{18,... | collective-permute-start | bytes 147464 | tf_op jit(solution)/shard_map/ppermute | solution.py:720
  126.8 1.7 %final.4.refs_2_ = f32[48,1536]{1,0:T(8,128)} custom-call(f32[48,1536]{1,0:T(8,128)} %get-tuple-element.150.refs_0_, bf16[48,1536]{1,0:T(8,128)(2,1)S(1)} %collective-permute-done.20.refs_1_, f32[16,768]{1,0:T(8,128)S(1)} %add.64.refs_2_.refs_0_), custom_call_target="tpu_custom_call" | custom-call | flops 20000000000 | bytes 1 | tf_op jit(solution)/shard_map/final/pallas_call | solution.py:182
  128.9 2.1 %collective-permute-start.21 = (f32[16,768]{1,0:T(8,128)S(1)}, f32[16,768]{1,0:T(8,128)S(1)}, u32[]{:S(2)}, u32[]{:S(2)}) collective-permute-start(f32[16,768]{1,0:T(8,128)S(1)} %add.65.refs_2_.refs_0_), channel_id=1, source_target_pairs={{0,16},{2,18},{4,20},{6,22},{8,24},{10,26},{12,28},{14,30},{16,0},... | collective-permute-start | bytes 147464 | tf_op jit(solution)/shard_map/ppermute | solution.py:720
  131.1 2.2 %collective-permute-done.22.refs_1_ = bf16[48,1536]{1,0:T(8,128)(2,1)S(1)} collective-permute-done((bf16[48,1536]{1,0:T(8,128)(2,1)S(1)}, bf16[48,1536]{1,0:T(8,128)(2,1)S(1)}, u32[]{:S(2)}, u32[]{:S(2)}) %collective-permute-start.22) | collective-permute-done | bytes 147488 | tf_op jit(solution)/shard_map/ppermute | solution.py:733
  133.3 1.7 %final.5 = (f32[3,48,384]{2,1,0:T(8,128)}, f32[48,384]{1,0:T(8,128)}) custom-call(f32[48,1536]{1,0:T(8,128)} %get-tuple-element.151.refs_0_, bf16[48,1536]{1,0:T(8,128)(2,1)S(1)} %collective-permute-done.22.refs_1_, f32[16,768]{1,0:T(8,128)S(1)} %add.65.refs_2_.refs_0_), custom_call_target="tpu_custom_call" | custom-call | flops 20000000000 | bytes 1 | tf_op jit(solution)/shard_map/final/pallas_call | solution.py:182
  (89 shorter events, 9.3 us)
Async XLA Ops:
  1.3 21.4 %copy-start.13 = (s32[1,16]{1,0:T(1,128)S(1)}, s32[1,16]{1,0:T(1,128)}, u32[]{:S(2)}) copy-start(s32[1,16]{1,0:T(1,128)} %refs_0_.8) | copy-start | bytes 196
  19.1 20.4 %copy-start.9 = (bf16[1024,768]{1,0:T(8,128)(2,1)}, bf16[1024,768]{1,0:T(8,128)(2,1)S(1)}, u32[]{:S(2)}) copy-start(bf16[1024,768]{1,0:T(8,128)(2,1)S(1)} %get-tuple-element.88.refs_6_.refs_3_) | copy-start | bytes 4718596
  19.1 3.6 %collective-permute-start = (bf16[1024,768]{1,0:T(8,128)(2,1)S(1)}, bf16[1024,768]{1,0:T(8,128)(2,1)S(1)}, u32[]{:S(2)}, u32[]{:S(2)}) collective-permute-start(bf16[1024,768]{1,0:T(8,128)(2,1)S(1)} %get-tuple-element.88.refs_6_.refs_3_), channel_id=1, source_target_pairs={{0,1},{1,0},{2,3},{3,2},{4,5},{5,4},{6,7},{7,6},{8,9},{9,8},{10,11... | collective-permute-start | bytes 4718600 | tf_op jit(solution)/shard_map/ppermute | solution.py:720
  22.7 16.8 %copy-start.10 = (bf16[1024,768]{1,0:T(8,128)(2,1)}, bf16[1024,768]{1,0:T(8,128)(2,1)S(1)}, u32[]{:S(2)}) copy-start(bf16[1024,768]{1,0:T(8,128)(2,1)S(1)} %collective-permute-done.refs_7_.refs_4_) | copy-start | bytes 4718596
  39.5 8.8 %collective-permute-start.2 = (bf16[1024,768]{1,0:T(8,128)(2,1)S(1)}, bf16[1024,768]{1,0:T(8,128)(2,1)S(1)}, u32[]{:S(2)}, u32[]{:S(2)}) collective-permute-start(bf16[1024,768]{1,0:T(8,128)(2,1)S(1)} %get-tuple-element.93.refs_3_), channel_id=1, source_target_pairs={{0,1},{1,0},{2,3},{3,2},{4,5},{5,4},{6,7},{7,6},{8,9},{9,8},{10,11... | collective-permute-start | bytes 4718600 | tf_op jit(solution)/shard_map/ppermute | solution.py:720
  39.9 26.8 %collective-permute-start.1 = (bf16[384,1536]{1,0:T(8,128)(2,1)S(1)}, bf16[384,1536]{1,0:T(8,128)(2,1)S(1)}, u32[]{:S(2)}, u32[]{:S(2)}) collective-permute-start(bf16[384,1536]{1,0:T(8,128)(2,1)S(1)} %get-tuple-element.92), channel_id=1, source_target_pairs={{0,2},{1,5},{2,0},{3,7},{4,6},{5,1},{6,4},{7,3},{8,10},{9,13},{10,... | collective-permute-start | bytes 3538952 | tf_op jit(solution)/shard_map/ppermute | solution.py:733
  46.6 8.1 %copy-start.2 = (f32[8,1536]{1,0:T(8,128)}, f32[8,1536]{1,0:T(8,128)S(1)}, u32[]{:S(2)}) copy-start(f32[8,1536]{1,0:T(8,128)S(1)} %get-tuple-element.100.refs_10_.refs_7_) | copy-start | bytes 147460
  46.6 31.4 %collective-permute-start.5 = (bf16[384,1536]{1,0:T(8,128)(2,1)S(1)}, bf16[384,1536]{1,0:T(8,128)(2,1)S(1)}, u32[]{:S(2)}, u32[]{:S(2)}) collective-permute-start(bf16[384,1536]{1,0:T(8,128)(2,1)S(1)} %get-tuple-element.116), channel_id=1, source_target_pairs={{0,8},{1,9},{2,10},{3,11},{4,12},{5,13},{6,14},{7,15},{8,0},{9,1},... | collective-permute-start | bytes 3538952 | tf_op jit(solution)/shard_map/ppermute | solution.py:733
  48.3 7.1 %copy-start.17 = (bf16[1024,768]{1,0:T(8,128)(2,1)S(1)}, bf16[1024,768]{1,0:T(8,128)(2,1)}, u32[]{:S(2)}) copy-start(bf16[1024,768]{1,0:T(8,128)(2,1)} %get-tuple-element.108.refs_7_) | copy-start | bytes 4718596
  48.3 7.1 %copy-start.19 = (bf16[1024,384]{1,0:T(8,128)(2,1)S(1)}, bf16[1024,384]{1,0:T(8,128)(2,1)}, u32[]{:S(2)}) copy-start(bf16[1024,384]{1,0:T(8,128)(2,1)} %get-tuple-element.104.refs_2_) | copy-start | bytes 2359300
  48.3 7.1 %copy-start.20 = (bf16[1024,384]{1,0:T(8,128)(2,1)S(1)}, bf16[1024,384]{1,0:T(8,128)(2,1)}, u32[]{:S(2)}) copy-start(bf16[1024,384]{1,0:T(8,128)(2,1)} %get-tuple-element.103.refs_1_) | copy-start | bytes 2359300
  48.3 7.0 %copy-start.21 = (bf16[1024,384]{1,0:T(8,128)(2,1)S(1)}, bf16[1024,384]{1,0:T(8,128)(2,1)}, u32[]{:S(2)}) copy-start(bf16[1024,384]{1,0:T(8,128)(2,1)} %get-tuple-element.105.refs_3_) | copy-start | bytes 2359300
  54.8 10.4 %copy-start.4 = (f32[8,768]{1,0:T(8,128)}, f32[8,768]{1,0:T(8,128)S(1)}, u32[]{:S(2)}) copy-start(f32[8,768]{1,0:T(8,128)S(1)} %get-tuple-element.109.refs_8_.refs_5_) | copy-start | bytes 73732
  54.8 11.9 %collective-permute-start.3 = (bf16[384,384]{1,0:T(8,128)(2,1)S(1)}, bf16[384,384]{1,0:T(8,128)(2,1)S(1)}, u32[]{:S(2)}, u32[]{:S(2)}) collective-permute-start(bf16[384,384]{1,0:T(8,128)(2,1)S(1)} %get-tuple-element.102), channel_id=1, source_target_pairs={{0,2},{1,5},{2,0},{3,7},{4,6},{5,1},{6,4},{7,3},{8,10},{9,13},{10,... | collective-permute-start | bytes 884744 | tf_op jit(solution)/shard_map/ppermute | solution.py:733
  65.1 12.9 %collective-permute-start.6 = (bf16[384,384]{1,0:T(8,128)(2,1)S(1)}, bf16[384,384]{1,0:T(8,128)(2,1)S(1)}, u32[]{:S(2)}, u32[]{:S(2)}) collective-permute-start(bf16[384,384]{1,0:T(8,128)(2,1)S(1)} %get-tuple-element.118), channel_id=1, source_target_pairs={{0,2},{1,5},{2,0},{3,7},{4,6},{5,1},{6,4},{7,3},{8,10},{9,13},{10,... | collective-permute-start | bytes 884744 | tf_op jit(solution)/shard_map/ppermute | solution.py:733
  67.1 10.9 %collective-permute-start.4 = (bf16[192,1536]{1,0:T(8,128)(2,1)S(1)}, bf16[192,1536]{1,0:T(8,128)(2,1)S(1)}, u32[]{:S(2)}, u32[]{:S(2)}) collective-permute-start(bf16[192,1536]{1,0:T(8,128)(2,1)S(1)} %get-tuple-element.114), channel_id=1, source_target_pairs={{0,4},{1,3},{2,6},{3,1},{4,0},{5,7},{6,2},{7,5},{8,12},{9,11},{10,... | collective-permute-start | bytes 1769480 | tf_op jit(solution)/shard_map/ppermute | solution.py:733
  77.4 12.7 %collective-permute-start.9 = (bf16[384,384]{1,0:T(8,128)(2,1)S(1)}, bf16[384,384]{1,0:T(8,128)(2,1)S(1)}, u32[]{:S(2)}, u32[]{:S(2)}) collective-permute-start(bf16[384,384]{1,0:T(8,128)(2,1)S(1)} %get-tuple-element.128), channel_id=1, source_target_pairs={{0,2},{1,5},{2,0},{3,7},{4,6},{5,1},{6,4},{7,3},{8,10},{9,13},{10,... | collective-permute-start | bytes 884744 | tf_op jit(solution)/shard_map/ppermute | solution.py:733
  78.4 12.1 %collective-permute-start.8 = (bf16[192,1536]{1,0:T(8,128)(2,1)S(1)}, bf16[192,1536]{1,0:T(8,128)(2,1)S(1)}, u32[]{:S(2)}, u32[]{:S(2)}) collective-permute-start(bf16[192,1536]{1,0:T(8,128)(2,1)S(1)} %get-tuple-element.126), channel_id=1, source_target_pairs={{0,2},{1,5},{2,0},{3,7},{4,6},{5,1},{6,4},{7,3},{8,10},{9,13},{10,... | collective-permute-start | bytes 1769480 | tf_op jit(solution)/shard_map/ppermute | solution.py:733
  80.0 10.1 %collective-permute-start.7 = (bf16[96,1536]{1,0:T(8,128)(2,1)S(1)}, bf16[96,1536]{1,0:T(8,128)(2,1)S(1)}, u32[]{:S(2)}, u32[]{:S(2)}) collective-permute-start(bf16[96,1536]{1,0:T(8,128)(2,1)S(1)} %get-tuple-element.124), channel_id=1, source_target_pairs={{0,8},{1,9},{2,10},{3,11},{4,12},{5,13},{6,14},{7,15},{8,0},{9,1},... | collective-permute-start | bytes 884744 | tf_op jit(solution)/shard_map/ppermute | solution.py:733
  89.5 7.5 %collective-permute-start.10 = (bf16[384,384]{1,0:T(8,128)(2,1)S(1)}, bf16[384,384]{1,0:T(8,128)(2,1)S(1)}, u32[]{:S(2)}, u32[]{:S(2)}) collective-permute-start(bf16[384,384]{1,0:T(8,128)(2,1)S(1)} %get-tuple-element.133), channel_id=1, source_target_pairs={{0,2},{1,5},{2,0},{3,7},{4,6},{5,1},{6,4},{7,3},{8,10},{9,13},{10,... | collective-permute-start | bytes 884744 | tf_op jit(solution)/shard_map/ppermute | solution.py:733
  91.3 17.3 %collective-permute-start.14 = (bf16[48,1536]{1,0:T(8,128)(2,1)S(1)}, bf16[48,1536]{1,0:T(8,128)(2,1)S(1)}, u32[]{:S(2)}, u32[]{:S(2)}) collective-permute-start(bf16[48,1536]{1,0:T(8,128)(2,1)S(1)} %get-tuple-element.137.refs_4_), channel_id=1, source_target_pairs={{0,16},{1,17},{2,18},{3,19},{4,20},{5,21},{6,22},{7,23},{8,24},{9,... | collective-permute-start | bytes 442376 | tf_op jit(solution)/shard_map/ppermute | solution.py:733
  96.9 6.4 %collective-permute-start.15 = (bf16[1024,768]{1,0:T(8,128)(2,1)S(1)}, bf16[1024,768]{1,0:T(8,128)(2,1)S(1)}, u32[]{:S(2)}, u32[]{:S(2)}) collective-permute-start(bf16[1024,768]{1,0:T(8,128)(2,1)S(1)} %first.1.refs_8_.refs_2_), channel_id=1, source_target_pairs={{0,1},{1,0},{2,3},{3,2},{4,5},{5,4},{6,7},{7,6},{8,9},{9,8},{10,11... | collective-permute-start | bytes 4718600 | tf_op jit(solution)/shard_map/ppermute | solution.py:720
  97.2 13.2 %collective-permute-start.12 = (bf16[192,1536]{1,0:T(8,128)(2,1)S(1)}, bf16[192,1536]{1,0:T(8,128)(2,1)S(1)}, u32[]{:S(2)}, u32[]{:S(2)}) collective-permute-start(bf16[192,1536]{1,0:T(8,128)(2,1)S(1)} %get-tuple-element.138.refs_2_), channel_id=1, source_target_pairs={{0,4},{1,3},{2,6},{3,1},{4,0},{5,7},{6,2},{7,5},{8,12},{9,11},{10,... | collective-permute-start | bytes 1769480 | tf_op jit(solution)/shard_map/ppermute | solution.py:733
  98.2 12.2 %collective-permute-start.13 = (bf16[96,1536]{1,0:T(8,128)(2,1)S(1)}, bf16[96,1536]{1,0:T(8,128)(2,1)S(1)}, u32[]{:S(2)}, u32[]{:S(2)}) collective-permute-start(bf16[96,1536]{1,0:T(8,128)(2,1)S(1)} %get-tuple-element.141), channel_id=1, source_target_pairs={{0,4},{1,3},{2,6},{3,1},{4,0},{5,7},{6,2},{7,5},{8,12},{9,11},{10,... | collective-permute-start | bytes 884744 | tf_op jit(solution)/shard_map/ppermute | solution.py:733
  102.7 11.8 %collective-permute-start.11 = (bf16[1024,768]{1,0:T(8,128)(2,1)S(1)}, bf16[1024,768]{1,0:T(8,128)(2,1)S(1)}, u32[]{:S(2)}, u32[]{:S(2)}) collective-permute-start(bf16[1024,768]{1,0:T(8,128)(2,1)S(1)} %down.1.refs_11_.refs_5_), channel_id=1, source_target_pairs={{0,1},{1,0},{2,3},{3,2},{4,5},{5,4},{6,7},{7,6},{8,9},{9,8},{10,11... | collective-permute-start | bytes 4718600 | tf_op jit(solution)/shard_map/ppermute | solution.py:720
  107.5 10.9 %collective-permute-start.16 = (f32[16,768]{1,0:T(8,128)S(1)}, f32[16,768]{1,0:T(8,128)S(1)}, u32[]{:S(2)}, u32[]{:S(2)}) collective-permute-start(f32[16,768]{1,0:T(8,128)S(1)} %get-tuple-element.144.refs_2_.refs_0_), channel_id=1, source_target_pairs={{0,2},{2,0},{4,6},{6,4},{8,10},{10,8},{12,14},{14,12},{16,18},{18,... | collective-permute-start | bytes 147464 | tf_op jit(solution)/shard_map/ppermute | solution.py:720
  111.2 11.9 %collective-permute-start.18 = (bf16[96,1536]{1,0:T(8,128)(2,1)S(1)}, bf16[96,1536]{1,0:T(8,128)(2,1)S(1)}, u32[]{:S(2)}, u32[]{:S(2)}) collective-permute-start(bf16[96,1536]{1,0:T(8,128)(2,1)S(1)} %get-tuple-element.148), channel_id=1, source_target_pairs={{0,8},{1,9},{2,10},{3,11},{4,12},{5,13},{6,14},{7,15},{8,0},{9,1},... | collective-permute-start | bytes 884744 | tf_op jit(solution)/shard_map/ppermute | solution.py:733
  112.8 14.0 %collective-permute-start.20 = (bf16[48,1536]{1,0:T(8,128)(2,1)S(1)}, bf16[48,1536]{1,0:T(8,128)(2,1)S(1)}, u32[]{:S(2)}, u32[]{:S(2)}) collective-permute-start(bf16[48,1536]{1,0:T(8,128)(2,1)S(1)} %get-tuple-element.145.refs_7_), channel_id=1, source_target_pairs={{0,16},{1,17},{2,18},{3,19},{4,20},{5,21},{6,22},{7,23},{8,24},{9,... | collective-permute-start | bytes 442376 | tf_op jit(solution)/shard_map/ppermute | solution.py:733
  118.4 5.8 %collective-permute-start.17 = (f32[16,768]{1,0:T(8,128)S(1)}, f32[16,768]{1,0:T(8,128)S(1)}, u32[]{:S(2)}, u32[]{:S(2)}) collective-permute-start(f32[16,768]{1,0:T(8,128)S(1)} %add.63.refs_2_.refs_0_), channel_id=1, source_target_pairs={{0,4},{2,6},{4,0},{6,2},{8,12},{10,14},{12,8},{14,10},{16,20},{18,... | collective-permute-start | bytes 147464 | tf_op jit(solution)/shard_map/ppermute | solution.py:720
  123.8 9.5 %collective-permute-start.22 = (bf16[48,1536]{1,0:T(8,128)(2,1)S(1)}, bf16[48,1536]{1,0:T(8,128)(2,1)S(1)}, u32[]{:S(2)}, u32[]{:S(2)}) collective-permute-start(bf16[48,1536]{1,0:T(8,128)(2,1)S(1)} %get-tuple-element.149.refs_2_), channel_id=1, source_target_pairs={{0,16},{1,17},{2,18},{3,19},{4,20},{5,21},{6,22},{7,23},{8,24},{9,... | collective-permute-start | bytes 442376 | tf_op jit(solution)/shard_map/ppermute | solution.py:733
  124.3 4.6 %collective-permute-start.19 = (f32[16,768]{1,0:T(8,128)S(1)}, f32[16,768]{1,0:T(8,128)S(1)}, u32[]{:S(2)}, u32[]{:S(2)}) collective-permute-start(f32[16,768]{1,0:T(8,128)S(1)} %add.64.refs_2_.refs_0_), channel_id=1, source_target_pairs={{0,8},{2,10},{4,12},{6,14},{8,0},{10,2},{12,4},{14,6},{16,24},{18,... | collective-permute-start | bytes 147464 | tf_op jit(solution)/shard_map/ppermute | solution.py:720
  128.9 6.1 %collective-permute-start.21 = (f32[16,768]{1,0:T(8,128)S(1)}, f32[16,768]{1,0:T(8,128)S(1)}, u32[]{:S(2)}, u32[]{:S(2)}) collective-permute-start(f32[16,768]{1,0:T(8,128)S(1)} %add.65.refs_2_.refs_0_), channel_id=1, source_target_pairs={{0,16},{2,18},{4,20},{6,22},{8,24},{10,26},{12,28},{14,30},{16,0},... | collective-permute-start | bytes 147464 | tf_op jit(solution)/shard_map/ppermute | solution.py:720
  (16 other events, 68.5 us)

commit v2 on v1

--- a/solution.py
+++ b/solution.py
@@ -260,7 +260,7 @@
     return jnp.where(lane < TOTALS_AT[1], first, jnp.where(lane < TOTALS_AT[2], second, third))
 
 
-def attend(queries, keys, values, id_k, mixed, features, block):
+def attend(queries, keys, values, id_k, mixed, wide, features, block):
     lane = lane_of((block, LANES))
 
     @pl.loop(0, queries.shape[0] // block)
@@ -282,13 +282,13 @@
                 total = term if total is None else total + term
                 inverses.append(1.0 / totals)
                 feature = jnp.where(is_total(lane, 2 * pair + half), -jnp.log(totals), feature)
-            mixed[span, cols] = (
-                total * jnp.where(lane < HEAD_DIM, inverses[0], inverses[1])
-            ).astype(bf16)
+            total = total * jnp.where(lane < HEAD_DIM, inverses[0], inverses[1])
+            wide[span, cols] = total
+            mixed[span, cols] = total.astype(bf16)
         features[span, :] = ids + in_pieces(feature, lane).astype(bf16)
 
 
-def attend_shifted(queries, keys, values, id_k, mixed, features, block):
+def attend_shifted(queries, keys, values, id_k, mixed, wide, features, block):
     @pl.loop(0, queries.shape[0] // block)
     def _(index):
         span = row_span(index, block)
@@ -309,6 +309,7 @@
                 lane = lane_of((block, LANES))
                 feature = jnp.where(is_total(lane, 2 * pair + half), -(largest + jnp.log(totals)), 0.0)
                 features[span, :] += in_pieces(feature, lane).astype(bf16)
+            wide[span, cols] = total
             mixed[span, cols] = total.astype(bf16)
 
 
@@ -325,7 +326,7 @@
 
 def qkv_kernel(given, made):
     lengths, gain, bias, tokens, weight, qv_bias, out_weight = given
-    hidden, queries, keys, values, id_k, mixed, features, part = made[:8]
+    hidden, queries, keys, values, id_k, mixed, wide, features, part = made
     rows = tokens.ref.shape[0]
     slots = lengths.shape[1]
     lane = lane_of((1, LANES))
@@ -372,7 +373,7 @@
     project(tokens.pieces - 1)
 
     bounded = largest_norms(queries.ref) * largest_norms(keys.ref) <= 4000.0
-    operands = [one.ref for one in (queries, keys, values, id_k, mixed, features)]
+    operands = [one.ref for one in (queries, keys, values, id_k, mixed, wide, features)]
 
     @pl.when(bounded)
     def _():
@@ -382,8 +383,8 @@
     def _():
         attend_shifted(*operands, LANES)
 
-    mixed.send()
-    features.send()
+    for one in (mixed, wide, features):
+        one.send()
     out_weight = out_weight()
 
     @pl.loop(0, 4)
@@ -508,9 +509,9 @@
 
 
 def middle_kernel(blocks, given, made, normed_back, ordered):
-    lengths, place, gain, norm_mine, norm_other, normed_two, inverse_two, cotangent, weight, mixed = given
+    lengths, place, gain, norm_mine, norm_other, normed_two, inverse_two, cotangent, weight, mixed, wide = given
     used = rows_used(lengths)
-    resid, grad_mixed, sums, keep, send = made
+    resid, grad_mixed, grad_features, sums, keep, send = made
     rows = norm_mine.ref.shape[0]
     block = 256
     sums.ref[...] = jnp.zeros_like(sums.ref)
@@ -538,18 +539,33 @@
         sums.ref[2:3, :] += column_sum(low.astype(f32))
 
     grad_mixed.ref[...] = dot_t(normed_back[...], weight()[...]).astype(bf16)
+    wide = wide()
+
+    @pl.loop(0, rows // block)
+    def _(index):
+        span = row_span(index, block)
+        lane = lane_of((block, LANES))
+        centres = jnp.zeros((block, LANES), f32)
+        for pair in range(wide.shape[1] // LANES):
+            cols = slice(pair * LANES, (pair + 1) * LANES)
+            product = grad_mixed.ref[span, cols].astype(f32) * wide[span, cols]
+            for half in range(2):
+                centre = jnp.sum(head_half(product, half), axis=1, keepdims=True)
+                centres = jnp.where(is_total(lane, 2 * pair + half), -centre, centres)
+        grad_features.ref[span, :] = in_pieces(centres, lane).astype(bf16)
+
     order_columns(normed_back[...], place, ordered, blocks)
     weight_grad(ordered, mixed(), keep, send)
 
 
-def attention_back_kernel(pair, blocks, given, made, wide_keys, turned, key_total, value_total):
-    given, before = given[:8], given[8:]
-    place, keys, queries, values, id_k, features, grad_mixed, hidden = given
+def attention_back_kernel(pair, blocks, given, made, wide_keys, wide_values, turned, key_total, value_total):
+    given, before = given[:9], given[9:]
+    place, keys, queries, values, id_k, features, grad_mixed, grad_features, hidden = given
     if pair == 0:
         *made, ordered = made
         ordered = ordered.ref
-    queries, keys, values, id_k, features, grad_mixed = (
-        one() for one in (queries, keys, values, id_k, features, grad_mixed)
+    queries, keys, values, id_k, features, grad_mixed, grad_features = (
+        one() for one in (queries, keys, values, id_k, features, grad_mixed, grad_features)
     )
     grads, sums, keep, send = made
     rows = queries.shape[0]
@@ -559,7 +575,10 @@
     turned[...] = key.T
     for half in range(2):
         wide_keys[half, :, :LANES] = key
-        wide_keys[half, :, LANES:] = id_k[...] + is_total(lane, 2 * pair + half).astype(f32).astype(bf16)
+        ones = is_total(lane, 2 * pair + half).astype(f32).astype(bf16)
+        wide_keys[half, :, LANES:] = id_k[...] + ones
+        wide_values[half, :, :LANES] = values[:, cols]
+        wide_values[half, :, LANES:] = jnp.broadcast_to(ones, (rows, LANES))
     block = rows // 2
     key_total[...] = jnp.zeros_like(key_total)
     value_total[...] = jnp.zeros_like(value_total)
@@ -568,15 +587,14 @@
     def _(index):
         span = row_span(index, block)
         query, grad, feature = queries[span, cols], grad_mixed[span, cols], features[span, :]
-        value = values[:, cols]
+        grad_feature = grad_features[span, :]
         key_term = value_term = None
         turned_grads = []
         for half in range(2):
             one_query, one_grad = head_half(query, half), head_half(grad, half)
             probs = jnp.exp(dot_t(wide_keys[half], jnp.concatenate([one_query, feature], axis=1)))
-            grad_probs = dot_t(value, one_grad)
-            centre = jnp.sum(probs * grad_probs, axis=0, keepdims=True)
-            grad_scores = (probs * (grad_probs - centre)).astype(bf16)
+            centred = dot_t(wide_values[half], jnp.concatenate([one_grad, grad_feature], axis=1))
+            grad_scores = (probs * centred).astype(bf16)
             value_one = dot(probs.astype(bf16), one_grad)
             key_one = dot(grad_scores, one_query)
             value_term = value_one if half == 0 else value_term + value_one
@@ -734,7 +752,7 @@
         self.step += 1
 
 
-def fold(chain, flows, ready=()):
+def fold(chain, flows, ready=(), covers=True):
     halved = [(flow.keep.shape[0] // 2, flow.keep.shape[1]) for flow in flows]
     if ready:
         columns = sum(flow.keep.shape[1] for flow in (*ready, *flows))
@@ -750,6 +768,7 @@
         outs,
         [Given(array, "v") for pair in pairs for array in pair],
         limit=8,
+        covers=covers,
     )
     for index in range(len(halved)):
         flows[index].keep, flows[index].send = results[2 * index : 2 * index + 2]
@@ -812,7 +831,7 @@
     halves = lambda columns: [Made((width // 2, columns), bf16, "v")] * 2
     turned = pltpu.VMEM((width + 16, rows), bf16)
 
-    hidden_one, queries, keys, values, id_k, mixed, features, part = call(
+    hidden_one, queries, keys, values, id_k, mixed, mixed_wide, features, part = call(
         chain,
         qkv_kernel,
         "qkv_attention",
@@ -821,6 +840,7 @@
             *[Made((rows, local), bf16, "h", 4)] * 3,
             Made((rows, LANES), bf16, "h", 4),
             Made((rows, local), bf16, "h"),
+            Made((rows, local), f32, "h"),
             Made((rows, LANES), bf16, "h"),
             Made((rows, width), bf16, "v", 4),
         ],
@@ -878,13 +898,14 @@
     up_keep, up_send, up_sums = weights("up_grad", hidden_two, grad_pre, long_place, True)
     flow_up = Flow(long_orders, n_dp, *arranged((up_keep, up_send), long_place, n_dp))
     flow_up.exchange()
-    resid, grad_mixed, middle_sums, out_keep, out_send = call(
+    resid, grad_mixed, grad_features, middle_sums, out_keep, out_send = call(
         chain,
         functools.partial(middle_kernel, n_dp),
         "middle",
         [
             Made((rows, width), f32, "h", 4),
             Made((rows, local), bf16, "v"),
+            Made((rows, LANES), bf16, "v"),
             Made((8, width), f32, "v"),
             *halves(local),
         ],
@@ -897,6 +918,7 @@
             *map(near, (normed_two, inverse_two, cotangent)),
             near(out_weight),
             near(mixed),
+            near(mixed_wide),
         ],
         scratch=[pltpu.VMEM((rows, width), bf16), turned],
         limit=16,
@@ -918,11 +940,12 @@
             ],
             [
                 Given(near_place, "s"),
-                *map(near, (keys, queries, values, id_k, features, grad_mixed)),
+                *map(near, (keys, queries, values, id_k, features, grad_mixed, grad_features)),
                 near(hiddens[-1]),
                 *(near(array) for pieces in before for array in pieces),
             ],
             scratch=[
+                pltpu.VMEM((2, rows, 2 * LANES), bf16),
                 pltpu.VMEM((2, rows, 2 * LANES), bf16),
                 pltpu.VMEM((LANES, rows), bf16),
                 pltpu.VMEM((rows, LANES), f32),
@@ -957,6 +980,7 @@
     flow_qkv = flow_of(halves_qkv[-1])
     exchange(flow_qkv)
     fold(chain, [flow_down, flow_up, *flows_next])
+    exchange(flow_up)
     (first_part,) = call(
         chain,
         first_kernel,
@@ -967,19 +991,11 @@
     )
     first_other = swap(first_part, "mp", 0, 2)
     fold(chain, [flow_qkv], [flow_out, flow_first, *flows_next])
-    exchange(flow_qkv, flow_up)
+    exchange(flow_qkv)
+    fold(chain, [flow_up])
     last_step = len(rest) == 1
     if last_step:
-        exchange(flow_down)
-    (down_part,) = call(
-        chain,
-        down_kernel,
-        "down",
-        [Made((rows, width), bf16, "v", 4)],
-        [near(down_weight), near(activated)],
-        limit=10,
-    )
-    down_other = swap(down_part, "mp", 0, 2)
+        exchange(flow_down, flow_up)
     tokens_grad, vectors = call(
         chain,
         last_kernel,
@@ -990,23 +1006,41 @@
             *map(near, (tokens, first_part, first_other, resid, middle_sums, down_sums, up_sums, *sums)),
         ],
         limit=14,
-        covers=False,
     )
     shape = (width // n_dp, units)
+    fold(chain, [flow_qkv], covers=False)
+    exchange(flow_qkv)
     if last_step:
-        (down_total,) = finish(chain, [flow_down], final_kernel, [shape], False)
-    fold(chain, [flow_qkv, flow_up])
-    exchange(flow_qkv, flow_up)
+        down_total, up_total = finish(chain, [flow_down, flow_up], final_kernel, [shape] * 2, False)
     if not last_step:
-        exchange(flow_down)
-
-    def all_sum_step(bit):
+        exchange(flow_down, flow_up)
+
+    def all_sum_step(bit, covers=True):
         nonlocal vectors
         other = swap(vectors, "dp", bit, n_dp)
         (vectors,) = call(
-            chain, add_kernel, "add", [Made((16, width), f32, "v")], [near(vectors), near(other)], limit=4
+            chain,
+            add_kernel,
+            "add",
+            [Made((16, width), f32, "v")],
+            [near(vectors), near(other)],
+            limit=4,
+            covers=covers,
         )
 
+    all_sum_step(bits[0], False)
+    (down_part,) = call(
+        chain,
+        down_kernel,
+        "down",
+        [Made((rows, width), bf16, "v", 4)],
+        [near(down_weight), near(activated)],
+        limit=10,
+    )
+    down_other = swap(down_part, "mp", 0, 2)
+    fold(chain, [flow_qkv])
+    exchange(flow_qkv)
+    all_sum_step(bits[1], False)
     (output,) = call(
         chain,
         output_kernel,
@@ -1018,14 +1052,8 @@
         ],
         limit=16,
     )
-    all_sum_step(bits[0])
-    fold(chain, [flow_qkv])
-    exchange(flow_qkv)
-    all_sum_step(bits[1])
-    if last_step:
-        (up_total,) = finish(chain, [flow_up], final_kernel, [shape])
     for bit in bits[2:-1]:
-        all_sum_step(bit)
+        all_sum_step(bit, False)
     flows = [flow_qkv, flow_up, flow_down]
     for step in range(1, len(rest)):
         fold(chain, flows)

time: 136 us -> 131 us (0.963)
  Pallas kernels: 95.7 us -> 92.9 us
  waiting for transfers between devices: 9.68 us -> 7.96 us
  starting transfers between devices: 28.2 us -> 26.6 us
    pallas_call x24, Pallas kernels: 95.7 us -> 92.9 us  [call(): pl.pallas_call(body, name=name, out_shape=tuple((pins[m.kind](m.shape, m....]
    ppermute x15, waiting for transfers between devices: 6.29 us -> 4.31 us  [exchange(): self.came = lax.ppermute(self.send, ('dp', 'mp'), pairs)]
    ppermute x8, starting transfers between devices: 8.45 us -> 6.67 us  [swap(): return lax.ppermute(values, axis, [(i, i ^ 1 << bit) for i in range(size)])]
  transfers between devices with their start and end apart: 23 -> 23, of which waited for: 5 -> 7; matrix products, arithmetic and copies ran while one was open for 0% -> 0% of each run, Pallas kernels for 44% -> 44%
where the time goes in v2:
time: 131 us
  Pallas kernels  92.9 us (71%)
  starting transfers between devices  26.6 us (20%)
  waiting for transfers between devices  7.96 us (6%)
  local copies, waits for them, and re-layouts  2 us (2%)
  between operations  1.32 us (1%)
    pallas_call x24, Pallas kernels, call(): pl.pallas_call(body, name=name, out_shape=tuple((pins[m.kind](m.shape, m....  92.9 us
    ppermute x15, starting transfers between devices, exchange(): self.came = lax.ppermute(self.send, ('dp', 'mp'), pairs)  19.9 us
    ppermute x8, starting transfers between devices, swap(): return lax.ppermute(values, axis, [(i, i ^ 1 << bit) for i in range(size)])  6.67 us
    ppermute x15, waiting for transfers between devices, exchange(): self.came = lax.ppermute(self.send, ('dp', 'mp'), pairs)  4.31 us
    ppermute x8, waiting for transfers between devices, swap(): return lax.ppermute(values, axis, [(i, i ^ 1 << bit) for i in range(size)])  3.66 us
  transfers between devices with their start and end apart: 23, of which 7 were waited for; matrix products, arithmetic and copies ran while one was open for 0% of the time, Pallas kernels for 44%

profile of v2, /device:TPU:0, one launch (start us, length us, event | category | flops | bytes accessed | tf_op | source)
XLA Modules:
  0.0 130.8 jit_solution(15377520673644076145)
XLA Ops:
  1.3 17.8 %qkv_attention.1 = (bf16[1024,768]{1,0:T(8,128)(2,1)}, bf16[1024,384]{1,0:T(8,128)(2,1)}, bf16[1024,384]{1,0:T(8,128)(2,1)}, bf16[1024,384]{1,0:T(8,128)(2,1)}, ...) custom-call(s32[1,16]{1,0:T(1,128)S(1)} %copy-done.7, ...), custom_call_target="tpu_custom_call" | custom-call | flops 20000000000 | bytes 1 | tf_op jit(solution)/shard_map/qkv_attention/pallas_call | solution.py:182
  19.7 3.0 %collective-permute-done.refs_7_.refs_4_ = bf16[1024,768]{1,0:T(8,128)(2,1)S(1)} collective-permute-done((bf16[1024,768]{1,0:T(8,128)(2,1)S(1)}, bf16[1024,768]{1,0:T(8,128)(2,1)S(1)}, u32[]{:S(2)}, u32[]{:S(2)}) %collective-permute-start) | collective-permute-done | bytes 1572896 | tf_op jit(solution)/shard_map/ppermute | solution.py:738
  22.7 16.7 %mlp.1 = (bf16[1024,768]{1,0:T(8,128)(2,1)S(1)}, bf16[1024,768]{1,0:T(8,128)(2,1)}, f32[1024,128]{1,0:T(8,128)}, bf16[1024,1536]{1,0:T(8,128)(2,1)}, bf16[1024,1...) custom-call(s32[1,16]{1,0:T(1,128)S(1)} %copy-done.8, ...), custom_call_target="tpu_custom_call" | custom-call | flops 20000000000 | bytes 1 | tf_op jit(solution)/shard_map/mlp/pallas_call | solution.py:182
  39.4 2.9 %collective-permute-start.2 = (bf16[384,1536]{1,0:T(8,128)(2,1)S(1)}, bf16[384,1536]{1,0:T(8,128)(2,1)S(1)}, u32[]{:S(2)}, u32[]{:S(2)}) collective-permute-start(bf16[384,1536]{1,0:T(8,128)(2,1)S(1)} %get-tuple-element.115), channel_id=1, source_target_pairs={{0,2},{1,5},{2,0},{3,7},{4,6},{5,1},{6,4},{7,3},{8,10},{9,13},{10,... | collective-permute-start | bytes 3538952 | tf_op jit(solution)/shard_map/ppermute | solution.py:751
  42.4 4.0 %up_grad.1 = (bf16[384,1536]{1,0:T(8,128)(2,1)S(1)}, bf16[384,1536]{1,0:T(8,128)(2,1)S(1)}, f32[8,1536]{1,0:T(8,128)S(1)}) custom-call(s32[16]{0:T(128)S(1)} %get-tuple-element.170.refs_0_, bf16[1024,768]{1,0:T(8,128)(2,1)S(1)} %get-tuple-element.104.refs_1_, bf16[1024,1536]{1,0:T(8,128)(2,1)S(1)} %get-tuple-element.105.refs_2_, ...), custom_call_target="tpu_custom_call" | custom-call | flops 20000000000 | bytes 1 | tf_op jit(solution)/shard_map/up_grad/pallas_call | solution.py:182
  46.5 1.6 %collective-permute-start.5 = (bf16[384,1536]{1,0:T(8,128)(2,1)S(1)}, bf16[384,1536]{1,0:T(8,128)(2,1)S(1)}, u32[]{:S(2)}, u32[]{:S(2)}) collective-permute-start(bf16[384,1536]{1,0:T(8,128)(2,1)S(1)} %get-tuple-element.124), channel_id=1, source_target_pairs={{0,8},{1,9},{2,10},{3,11},{4,12},{5,13},{6,14},{7,15},{8,0},{9,1},... | collective-permute-start | bytes 3538952 | tf_op jit(solution)/shard_map/ppermute | solution.py:751
  48.2 8.1 %middle.1 = (f32[1024,768]{1,0:T(8,128)}, bf16[1024,384]{1,0:T(8,128)(2,1)S(1)}, bf16[1024,128]{1,0:T(8,128)(2,1)S(1)}, f32[8,768]{1,0:T(8,128)S(1)}, bf16[384,3...) custom-call(s32[1,16]{1,0:T(1,128)S(1)} %copy-done.8, s32[16]{0:T(128)S(1)} %get-tuple-element.171.refs_1_.refs_0_, ...), custom_call_target="tpu_custom_call" | custom-call | flops 20000000000 | bytes 1 | tf_op jit(solution)/shard_map/middle/pallas_call | solution.py:182
  56.3 1.4 %collective-permute-start.3 = (bf16[384,384]{1,0:T(8,128)(2,1)S(1)}, bf16[384,384]{1,0:T(8,128)(2,1)S(1)}, u32[]{:S(2)}, u32[]{:S(2)}) collective-permute-start(bf16[384,384]{1,0:T(8,128)(2,1)S(1)} %get-tuple-element.117), channel_id=1, source_target_pairs={{0,2},{1,5},{2,0},{3,7},{4,6},{5,1},{6,4},{7,3},{8,10},{9,13},{10,... | collective-permute-start | bytes 884744 | tf_op jit(solution)/shard_map/ppermute | solution.py:751
  57.8 8.8 %attention_back0.1 = (bf16[1024,384]{1,0:T(8,128)(2,1)S(1)}, f32[8,384]{1,0:T(8,128)S(1)}, bf16[384,384]{1,0:T(8,128)(2,1)S(1)}, bf16[384,384]{1,0:T(8,128)(2,1)S(1)}, bf16[784,1024]{1,0:T(8,128)(2,1)}) custom-call(s32[16]{0:T(128)S(1)} %get-tuple-element.171.refs_1_.refs_0_, bf16[1024,384]{1,0:T(8,128)(2,1)S(1)} %copy-done.17, ...), custom_call_target="tpu_custom_call" | custom-call | flops 20000000000 | bytes 1 | tf_op jit(solution)/shard_map/attention_back0/pallas_call | solution.py:182
  67.6 1.6 %collective-permute-start.4 = (bf16[192,1536]{1,0:T(8,128)(2,1)S(1)}, bf16[192,1536]{1,0:T(8,128)(2,1)S(1)}, u32[]{:S(2)}, u32[]{:S(2)}) collective-permute-start(bf16[192,1536]{1,0:T(8,128)(2,1)S(1)} %get-tuple-element.122), channel_id=1, source_target_pairs={{0,4},{1,3},{2,6},{3,1},{4,0},{5,7},{6,2},{7,5},{8,12},{9,11},{10,... | collective-permute-start | bytes 1769480 | tf_op jit(solution)/shard_map/ppermute | solution.py:751
  69.2 7.7 %attention_back1.1 = (bf16[1024,384]{1,0:T(8,128)(2,1)S(1)}, f32[8,384]{1,0:T(8,128)S(1)}, bf16[384,384]{1,0:T(8,128)(2,1)S(1)}, bf16[384,384]{1,0:T(8,128)(2,1)S(1)}) custom-call(s32[16]{0:T(128)S(1)} %get-tuple-element.171.refs_1_.refs_0_, bf16[1024,384]{1,0:T(8,128)(2,1)S(1)} %copy-done.17, bf16[1024,384]{1,0:T(8,128)(2,1)S(1)} %copy-done.16, ...), custom_call_target="tpu_custom_call" | custom-call | flops 20000000000 | bytes 1 | tf_op jit(solution)/shard_map/attention_back1/pallas_call | solution.py:182
  77.0 0.9 collective-permute-start.9
  80.3 8.0 %attention_back2.1 = (bf16[1024,384]{1,0:T(8,128)(2,1)S(1)}, f32[8,384]{1,0:T(8,128)S(1)}, bf16[384,384]{1,0:T(8,128)(2,1)S(1)}, bf16[384,384]{1,0:T(8,128)(2,1)S(1)}) custom-call(s32[16]{0:T(128)S(1)} %get-tuple-element.171.refs_1_.refs_0_, bf16[1024,384]{1,0:T(8,128)(2,1)S(1)} %copy-done.17, bf16[1024,384]{1,0:T(8,128)(2,1)S(1)} %copy-done.16, ...), custom_call_target="tpu_custom_call" | custom-call | flops 20000000000 | bytes 1 | tf_op jit(solution)/shard_map/attention_back2/pallas_call | solution.py:182
  88.3 1.6 %collective-permute-start.12 = (bf16[384,384]{1,0:T(8,128)(2,1)S(1)}, bf16[384,384]{1,0:T(8,128)(2,1)S(1)}, u32[]{:S(2)}, u32[]{:S(2)}) collective-permute-start(bf16[384,384]{1,0:T(8,128)(2,1)S(1)} %get-tuple-element.146), channel_id=1, source_target_pairs={{0,2},{1,5},{2,0},{3,7},{4,6},{5,1},{6,4},{7,3},{8,10},{9,13},{10,... | collective-permute-start | bytes 884744 | tf_op jit(solution)/shard_map/ppermute | solution.py:751
  91.0 2.7 %collective-permute-start.14 = (bf16[48,1536]{1,0:T(8,128)(2,1)S(1)}, bf16[48,1536]{1,0:T(8,128)(2,1)S(1)}, u32[]{:S(2)}, u32[]{:S(2)}) collective-permute-start(bf16[48,1536]{1,0:T(8,128)(2,1)S(1)} %get-tuple-element.137.refs_4_), channel_id=1, source_target_pairs={{0,16},{1,17},{2,18},{3,19},{4,20},{5,21},{6,22},{7,23},{8,24},{9,... | collective-permute-start | bytes 442376 | tf_op jit(solution)/shard_map/ppermute | solution.py:751
  93.6 1.0 collective-permute-start.11
  94.6 2.8 %first.1.refs_8_.refs_2_ = bf16[1024,768]{1,0:T(8,128)(2,1)S(1)} custom-call(bf16[1024,384]{1,0:T(8,128)(2,1)S(1)} %get-tuple-element.112.refs_0_, bf16[1024,384]{1,0:T(8,128)(2,1)S(1)} %get-tuple-element.120.refs_1_, bf16[1024,384]{1,0:T(8,128)(2,1)S(1)} %get-tuple-element.129.refs_2_, bf16[3,768,384]{2,1,0:T(8,128)(2,1)S(1)} %bitcast.5, ...), custom_call_target="tpu_custom_call" | custom-call | flops 20000000000 | bytes 1 | tf_op jit(solution)/shard_map/first/pallas_call | solution.py:182
  97.7 1.1 collective-permute-start.16
  98.8 1.5 %collective-permute-done.11.refs_1_ = bf16[96,1536]{1,0:T(8,128)(2,1)S(1)} collective-permute-done((bf16[96,1536]{1,0:T(8,128)(2,1)S(1)}, bf16[96,1536]{1,0:T(8,128)(2,1)S(1)}, u32[]{:S(2)}, u32[]{:S(2)}) %collective-permute-start.11) | collective-permute-done | bytes 294944 | tf_op jit(solution)/shard_map/ppermute | solution.py:751
  101.8 1.0 copy-done.10
  102.8 4.4 %last.1 = (f32[1024,768]{1,0:T(8,128)}, f32[16,768]{1,0:T(8,128)S(1)}) custom-call(f32[768]{0:T(1024)} %refs_0_.9, bf16[1024,768]{1,0:T(8,128)(2,1)S(1)} %copy-done.3, bf16[1024,768]{1,0:T(8,128)(2,1)S(1)} %first.1.refs_8_.refs_2_, bf16[1024,768]{1,0:T(8,128)(2,1)S(1)} %collective-permute-done.10.refs_3_, f32[1024,768]{1,0:T(8,128)S(1)} %copy-done.10, ...), custom_call_target="tpu_custom_call" | custom-call | flops 20000000000 | bytes 1 | tf_op jit(solution)/shard_map/last/pallas_call | solution.py:182
  107.2 0.9 collective-permute-start.13
  108.2 1.1 collective-permute-start.19
  109.5 1.8 %final.2 = (f32[48,1536]{1,0:T(8,128)}, f32[48,1536]{1,0:T(8,128)}) custom-call(f32[48,1536]{1,0:T(8,128)} %get-tuple-element.150.refs_0_, bf16[48,1536]{1,0:T(8,128)(2,1)S(1)} %collective-permute-done.14.refs_1_, f32[48,1536]{1,0:T(8,128)} %get-tuple-element.151.refs_2_, bf16[48,1536]{1,0:T(8,128)(2,1)S(1)} %collective-permute-done.15.refs_3_, ...), custom_call_target="tpu_custom_call" | custom-call | bytes 1 | tf_op jit(solution)/shard_map/final/pallas_call | solution.py:182
  111.4 1.8 %collective-permute-start.18 = (f32[16,768]{1,0:T(8,128)S(1)}, f32[16,768]{1,0:T(8,128)S(1)}, u32[]{:S(2)}, u32[]{:S(2)}) collective-permute-start(f32[16,768]{1,0:T(8,128)S(1)} %add.63.refs_2_.refs_0_), channel_id=1, source_target_pairs={{0,4},{2,6},{4,0},{6,2},{8,12},{10,14},{12,8},{14,10},{16,20},{18,... | collective-permute-start | bytes 147464 | tf_op jit(solution)/shard_map/ppermute | solution.py:738
  113.2 3.1 %down.1.refs_2_.refs_5_ = bf16[1024,768]{1,0:T(8,128)(2,1)S(1)} custom-call(bf16[1536,768]{1,0:T(8,128)(2,1)S(1)} %copy-done, bf16[1024,1536]{1,0:T(8,128)(2,1)S(1)} %copy-done.9, f32[16,768]{1,0:T(8,128)S(1)} %add.63.refs_2_.refs_0_), custom_call_target="tpu_custom_call" | custom-call | flops 20000000000 | bytes 1 | tf_op jit(solution)/shard_map/down/pallas_call | solution.py:182
  117.2 1.7 %collective-permute-start.22 = (bf16[48,1536]{1,0:T(8,128)(2,1)S(1)}, bf16[48,1536]{1,0:T(8,128)(2,1)S(1)}, u32[]{:S(2)}, u32[]{:S(2)}) collective-permute-start(bf16[48,1536]{1,0:T(8,128)(2,1)S(1)} %get-tuple-element.156.refs_2_), channel_id=1, source_target_pairs={{0,16},{1,17},{2,18},{3,19},{4,20},{5,21},{6,22},{7,23},{8,24},{9,... | collective-permute-start | bytes 442376 | tf_op jit(solution)/shard_map/ppermute | solution.py:751
  118.9 1.8 %collective-permute-start.20 = (f32[16,768]{1,0:T(8,128)S(1)}, f32[16,768]{1,0:T(8,128)S(1)}, u32[]{:S(2)}, u32[]{:S(2)}) collective-permute-start(f32[16,768]{1,0:T(8,128)S(1)} %add.64.refs_7_.refs_0_), channel_id=1, source_target_pairs={{0,8},{2,10},{4,12},{6,14},{8,0},{10,2},{12,4},{14,6},{16,24},{18,... | collective-permute-start | bytes 147464 | tf_op jit(solution)/shard_map/ppermute | solution.py:738
  120.7 3.9 %output.1.refs_2_ = bf16[1024,768]{1,0:T(8,128)(2,1)} custom-call(f32[768]{0:T(1024)} %refs_0_.11, f32[768]{0:T(1024)} %refs_1_.5, bf16[1024,768]{1,0:T(8,128)(2,1)} %refs_2_.7, bf16[1024,768]{1,0:T(8,128)(2,1)} %copy-done.4, bf16[1024,768]{1,0:T(8,128)(2,1)} %copy-done.5, bf16[1024,768]{1,0:T(8,128)(2,1)S(1)} %down.1.refs_2_.refs_5_, ...), custom_call_target="tpu_custom_call" | custom-call | flops 20000000000 | bytes 1 | tf_op jit(solution)/shard_map/output/pallas_call | solution.py:182
  124.6 1.5 %collective-permute-start.21 = (f32[16,768]{1,0:T(8,128)S(1)}, f32[16,768]{1,0:T(8,128)S(1)}, u32[]{:S(2)}, u32[]{:S(2)}) collective-permute-start(f32[16,768]{1,0:T(8,128)S(1)} %add.65.refs_2_.refs_0_), channel_id=1, source_target_pairs={{0,16},{2,18},{4,20},{6,22},{8,24},{10,26},{12,28},{14,30},{16,0},... | collective-permute-start | bytes 147464 | tf_op jit(solution)/shard_map/ppermute | solution.py:738
  126.0 1.5 %collective-permute-done.22.refs_1_ = bf16[48,1536]{1,0:T(8,128)(2,1)S(1)} collective-permute-done((bf16[48,1536]{1,0:T(8,128)(2,1)S(1)}, bf16[48,1536]{1,0:T(8,128)(2,1)S(1)}, u32[]{:S(2)}, u32[]{:S(2)}) %collective-permute-start.22) | collective-permute-done | bytes 147488 | tf_op jit(solution)/shard_map/ppermute | solution.py:751
  127.5 1.7 %final.3 = (f32[3,48,384]{2,1,0:T(8,128)}, f32[48,384]{1,0:T(8,128)}) custom-call(f32[48,1536]{1,0:T(8,128)} %get-tuple-element.158.refs_0_, bf16[48,1536]{1,0:T(8,128)(2,1)S(1)} %collective-permute-done.22.refs_1_, f32[16,768]{1,0:T(8,128)S(1)} %add.65.refs_2_.refs_0_), custom_call_target="tpu_custom_call" | custom-call | flops 20000000000 | bytes 1 | tf_op jit(solution)/shard_map/final/pallas_call | solution.py:182
  (95 shorter events, 9.9 us)
Async XLA Ops:
  1.3 21.4 %copy-start.8 = (s32[1,16]{1,0:T(1,128)S(1)}, s32[1,16]{1,0:T(1,128)}, u32[]{:S(2)}) copy-start(s32[1,16]{1,0:T(1,128)} %refs_0_.8) | copy-start | bytes 196
  19.1 20.3 %copy-start.4 = (bf16[1024,768]{1,0:T(8,128)(2,1)}, bf16[1024,768]{1,0:T(8,128)(2,1)S(1)}, u32[]{:S(2)}) copy-start(bf16[1024,768]{1,0:T(8,128)(2,1)S(1)} %get-tuple-element.92.refs_6_.refs_3_) | copy-start | bytes 4718596
  19.1 3.6 %collective-permute-start = (bf16[1024,768]{1,0:T(8,128)(2,1)S(1)}, bf16[1024,768]{1,0:T(8,128)(2,1)S(1)}, u32[]{:S(2)}, u32[]{:S(2)}) collective-permute-start(bf16[1024,768]{1,0:T(8,128)(2,1)S(1)} %get-tuple-element.92.refs_6_.refs_3_), channel_id=1, source_target_pairs={{0,1},{1,0},{2,3},{3,2},{4,5},{5,4},{6,7},{7,6},{8,9},{9,8},{10,11... | collective-permute-start | bytes 4718600 | tf_op jit(solution)/shard_map/ppermute | solution.py:738
  22.7 16.7 %copy-start.5 = (bf16[1024,768]{1,0:T(8,128)(2,1)}, bf16[1024,768]{1,0:T(8,128)(2,1)S(1)}, u32[]{:S(2)}) copy-start(bf16[1024,768]{1,0:T(8,128)(2,1)S(1)} %collective-permute-done.refs_7_.refs_4_) | copy-start | bytes 4718596
  39.4 27.9 %collective-permute-start.2 = (bf16[384,1536]{1,0:T(8,128)(2,1)S(1)}, bf16[384,1536]{1,0:T(8,128)(2,1)S(1)}, u32[]{:S(2)}, u32[]{:S(2)}) collective-permute-start(bf16[384,1536]{1,0:T(8,128)(2,1)S(1)} %get-tuple-element.115), channel_id=1, source_target_pairs={{0,2},{1,5},{2,0},{3,7},{4,6},{5,1},{6,4},{7,3},{8,10},{9,13},{10,... | collective-permute-start | bytes 3538952 | tf_op jit(solution)/shard_map/ppermute | solution.py:751
  42.4 5.8 %collective-permute-start.1 = (bf16[1024,768]{1,0:T(8,128)(2,1)S(1)}, bf16[1024,768]{1,0:T(8,128)(2,1)S(1)}, u32[]{:S(2)}, u32[]{:S(2)}) collective-permute-start(bf16[1024,768]{1,0:T(8,128)(2,1)S(1)} %get-tuple-element.99.refs_3_), channel_id=1, source_target_pairs={{0,1},{1,0},{2,3},{3,2},{4,5},{5,4},{6,7},{7,6},{8,9},{9,8},{10,11... | collective-permute-start | bytes 4718600 | tf_op jit(solution)/shard_map/ppermute | solution.py:738
  46.5 9.8 %copy-start.22 = (f32[8,1536]{1,0:T(8,128)}, f32[8,1536]{1,0:T(8,128)S(1)}, u32[]{:S(2)}) copy-start(f32[8,1536]{1,0:T(8,128)S(1)} %get-tuple-element.107.refs_11_.refs_7_) | copy-start | bytes 147460
  46.5 31.4 %collective-permute-start.5 = (bf16[384,1536]{1,0:T(8,128)(2,1)S(1)}, bf16[384,1536]{1,0:T(8,128)(2,1)S(1)}, u32[]{:S(2)}, u32[]{:S(2)}) collective-permute-start(bf16[384,1536]{1,0:T(8,128)(2,1)S(1)} %get-tuple-element.124), channel_id=1, source_target_pairs={{0,8},{1,9},{2,10},{3,11},{4,12},{5,13},{6,14},{7,15},{8,0},{9,1},... | collective-permute-start | bytes 3538952 | tf_op jit(solution)/shard_map/ppermute | solution.py:751
  48.2 9.6 %copy-start.14 = (bf16[1024,768]{1,0:T(8,128)(2,1)S(1)}, bf16[1024,768]{1,0:T(8,128)(2,1)}, u32[]{:S(2)}) copy-start(bf16[1024,768]{1,0:T(8,128)(2,1)} %get-tuple-element.110.refs_8_) | copy-start | bytes 4718596
  48.2 9.6 %copy-start.16 = (bf16[1024,384]{1,0:T(8,128)(2,1)S(1)}, bf16[1024,384]{1,0:T(8,128)(2,1)}, u32[]{:S(2)}) copy-start(bf16[1024,384]{1,0:T(8,128)(2,1)} %get-tuple-element.96.refs_2_) | copy-start | bytes 2359300
  48.2 9.6 %copy-start.17 = (bf16[1024,384]{1,0:T(8,128)(2,1)S(1)}, bf16[1024,384]{1,0:T(8,128)(2,1)}, u32[]{:S(2)}) copy-start(bf16[1024,384]{1,0:T(8,128)(2,1)} %get-tuple-element.95.refs_1_) | copy-start | bytes 2359300
  56.3 10.3 %copy-start.24 = (f32[8,768]{1,0:T(8,128)}, f32[8,768]{1,0:T(8,128)S(1)}, u32[]{:S(2)}) copy-start(f32[8,768]{1,0:T(8,128)S(1)} %get-tuple-element.111.refs_9_.refs_5_) | copy-start | bytes 73732
  56.3 11.0 %collective-permute-start.3 = (bf16[384,384]{1,0:T(8,128)(2,1)S(1)}, bf16[384,384]{1,0:T(8,128)(2,1)S(1)}, u32[]{:S(2)}, u32[]{:S(2)}) collective-permute-start(bf16[384,384]{1,0:T(8,128)(2,1)S(1)} %get-tuple-element.117), channel_id=1, source_target_pairs={{0,2},{1,5},{2,0},{3,7},{4,6},{5,1},{6,4},{7,3},{8,10},{9,13},{10,... | collective-permute-start | bytes 884744 | tf_op jit(solution)/shard_map/ppermute | solution.py:751
  66.6 11.3 %collective-permute-start.6 = (bf16[384,384]{1,0:T(8,128)(2,1)S(1)}, bf16[384,384]{1,0:T(8,128)(2,1)S(1)}, u32[]{:S(2)}, u32[]{:S(2)}) collective-permute-start(bf16[384,384]{1,0:T(8,128)(2,1)S(1)} %get-tuple-element.126), channel_id=1, source_target_pairs={{0,2},{1,5},{2,0},{3,7},{4,6},{5,1},{6,4},{7,3},{8,10},{9,13},{10,... | collective-permute-start | bytes 884744 | tf_op jit(solution)/shard_map/ppermute | solution.py:751
  67.6 11.2 %collective-permute-start.4 = (bf16[192,1536]{1,0:T(8,128)(2,1)S(1)}, bf16[192,1536]{1,0:T(8,128)(2,1)S(1)}, u32[]{:S(2)}, u32[]{:S(2)}) collective-permute-start(bf16[192,1536]{1,0:T(8,128)(2,1)S(1)} %get-tuple-element.122), channel_id=1, source_target_pairs={{0,4},{1,3},{2,6},{3,1},{4,0},{5,7},{6,2},{7,5},{8,12},{9,11},{10,... | collective-permute-start | bytes 1769480 | tf_op jit(solution)/shard_map/ppermute | solution.py:751
  77.0 12.9 %collective-permute-start.9 = (bf16[384,384]{1,0:T(8,128)(2,1)S(1)}, bf16[384,384]{1,0:T(8,128)(2,1)S(1)}, u32[]{:S(2)}, u32[]{:S(2)}) collective-permute-start(bf16[384,384]{1,0:T(8,128)(2,1)S(1)} %get-tuple-element.135), channel_id=1, source_target_pairs={{0,2},{1,5},{2,0},{3,7},{4,6},{5,1},{6,4},{7,3},{8,10},{9,13},{10,... | collective-permute-start | bytes 884744 | tf_op jit(solution)/shard_map/ppermute | solution.py:751
  79.3 10.6 %collective-permute-start.7 = (bf16[96,1536]{1,0:T(8,128)(2,1)S(1)}, bf16[96,1536]{1,0:T(8,128)(2,1)S(1)}, u32[]{:S(2)}, u32[]{:S(2)}) collective-permute-start(bf16[96,1536]{1,0:T(8,128)(2,1)S(1)} %get-tuple-element.131), channel_id=1, source_target_pairs={{0,8},{1,9},{2,10},{3,11},{4,12},{5,13},{6,14},{7,15},{8,0},{9,1},... | collective-permute-start | bytes 884744 | tf_op jit(solution)/shard_map/ppermute | solution.py:751
  79.8 10.3 %collective-permute-start.8 = (bf16[192,1536]{1,0:T(8,128)(2,1)S(1)}, bf16[192,1536]{1,0:T(8,128)(2,1)S(1)}, u32[]{:S(2)}, u32[]{:S(2)}) collective-permute-start(bf16[192,1536]{1,0:T(8,128)(2,1)S(1)} %get-tuple-element.133), channel_id=1, source_target_pairs={{0,2},{1,5},{2,0},{3,7},{4,6},{5,1},{6,4},{7,3},{8,10},{9,13},{10,... | collective-permute-start | bytes 1769480 | tf_op jit(solution)/shard_map/ppermute | solution.py:751
  88.3 9.2 %collective-permute-start.12 = (bf16[384,384]{1,0:T(8,128)(2,1)S(1)}, bf16[384,384]{1,0:T(8,128)(2,1)S(1)}, u32[]{:S(2)}, u32[]{:S(2)}) collective-permute-start(bf16[384,384]{1,0:T(8,128)(2,1)S(1)} %get-tuple-element.146), channel_id=1, source_target_pairs={{0,2},{1,5},{2,0},{3,7},{4,6},{5,1},{6,4},{7,3},{8,10},{9,13},{10,... | collective-permute-start | bytes 884744 | tf_op jit(solution)/shard_map/ppermute | solution.py:751
  91.0 18.4 %collective-permute-start.14 = (bf16[48,1536]{1,0:T(8,128)(2,1)S(1)}, bf16[48,1536]{1,0:T(8,128)(2,1)S(1)}, u32[]{:S(2)}, u32[]{:S(2)}) collective-permute-start(bf16[48,1536]{1,0:T(8,128)(2,1)S(1)} %get-tuple-element.137.refs_4_), channel_id=1, source_target_pairs={{0,16},{1,17},{2,18},{3,19},{4,20},{5,21},{6,22},{7,23},{8,24},{9,... | collective-permute-start | bytes 442376 | tf_op jit(solution)/shard_map/ppermute | solution.py:751
  93.6 6.7 %collective-permute-start.11 = (bf16[96,1536]{1,0:T(8,128)(2,1)S(1)}, bf16[96,1536]{1,0:T(8,128)(2,1)S(1)}, u32[]{:S(2)}, u32[]{:S(2)}) collective-permute-start(bf16[96,1536]{1,0:T(8,128)(2,1)S(1)} %get-tuple-element.140), channel_id=1, source_target_pairs={{0,4},{1,3},{2,6},{3,1},{4,0},{5,7},{6,2},{7,5},{8,12},{9,11},{10,... | collective-permute-start | bytes 884744 | tf_op jit(solution)/shard_map/ppermute | solution.py:751
  97.5 4.1 %collective-permute-start.10 = (bf16[1024,768]{1,0:T(8,128)(2,1)S(1)}, bf16[1024,768]{1,0:T(8,128)(2,1)S(1)}, u32[]{:S(2)}, u32[]{:S(2)}) collective-permute-start(bf16[1024,768]{1,0:T(8,128)(2,1)S(1)} %first.1.refs_8_.refs_2_), channel_id=1, source_target_pairs={{0,1},{1,0},{2,3},{3,2},{4,5},{5,4},{6,7},{7,6},{8,9},{9,8},{10,11... | collective-permute-start | bytes 4718600 | tf_op jit(solution)/shard_map/ppermute | solution.py:738
  97.7 10.4 %collective-permute-start.16 = (bf16[192,1536]{1,0:T(8,128)(2,1)S(1)}, bf16[192,1536]{1,0:T(8,128)(2,1)S(1)}, u32[]{:S(2)}, u32[]{:S(2)}) collective-permute-start(bf16[192,1536]{1,0:T(8,128)(2,1)S(1)} %get-tuple-element.147.refs_2_), channel_id=1, source_target_pairs={{0,4},{1,3},{2,6},{3,1},{4,0},{5,7},{6,2},{7,5},{8,12},{9,11},{10,... | collective-permute-start | bytes 1769480 | tf_op jit(solution)/shard_map/ppermute | solution.py:751
  101.1 8.4 %collective-permute-start.15 = (bf16[48,1536]{1,0:T(8,128)(2,1)S(1)}, bf16[48,1536]{1,0:T(8,128)(2,1)S(1)}, u32[]{:S(2)}, u32[]{:S(2)}) collective-permute-start(bf16[48,1536]{1,0:T(8,128)(2,1)S(1)} %get-tuple-element.148.refs_11_), channel_id=1, source_target_pairs={{0,16},{1,17},{2,18},{3,19},{4,20},{5,21},{6,22},{7,23},{8,24},{9,... | collective-permute-start | bytes 442376 | tf_op jit(solution)/shard_map/ppermute | solution.py:751
  102.8 10.4 %copy-start.9 = (bf16[1024,1536]{1,0:T(8,128)(2,1)S(1)}, bf16[1024,1536]{1,0:T(8,128)(2,1)}, u32[]{:S(2)}) copy-start(bf16[1024,1536]{1,0:T(8,128)(2,1)} %get-tuple-element.94.refs_1_) | copy-start | bytes 9437188
  107.2 4.2 %collective-permute-start.13 = (f32[16,768]{1,0:T(8,128)S(1)}, f32[16,768]{1,0:T(8,128)S(1)}, u32[]{:S(2)}, u32[]{:S(2)}) collective-permute-start(f32[16,768]{1,0:T(8,128)S(1)} %get-tuple-element.149.refs_2_.refs_0_), channel_id=1, source_target_pairs={{0,2},{2,0},{4,6},{6,4},{8,10},{10,8},{12,14},{14,12},{16,18},{18,... | collective-permute-start | bytes 147464 | tf_op jit(solution)/shard_map/ppermute | solution.py:738
  108.2 8.2 %collective-permute-start.19 = (bf16[96,1536]{1,0:T(8,128)(2,1)S(1)}, bf16[96,1536]{1,0:T(8,128)(2,1)S(1)}, u32[]{:S(2)}, u32[]{:S(2)}) collective-permute-start(bf16[96,1536]{1,0:T(8,128)(2,1)S(1)} %get-tuple-element.153.refs_4_), channel_id=1, source_target_pairs={{0,8},{1,9},{2,10},{3,11},{4,12},{5,13},{6,14},{7,15},{8,0},{9,1},... | collective-permute-start | bytes 884744 | tf_op jit(solution)/shard_map/ppermute | solution.py:751
  111.4 7.5 %collective-permute-start.18 = (f32[16,768]{1,0:T(8,128)S(1)}, f32[16,768]{1,0:T(8,128)S(1)}, u32[]{:S(2)}, u32[]{:S(2)}) collective-permute-start(f32[16,768]{1,0:T(8,128)S(1)} %add.63.refs_2_.refs_0_), channel_id=1, source_target_pairs={{0,4},{2,6},{4,0},{6,2},{8,12},{10,14},{12,8},{14,10},{16,20},{18,... | collective-permute-start | bytes 147464 | tf_op jit(solution)/shard_map/ppermute | solution.py:738
  116.3 4.4 %collective-permute-start.17 = (bf16[1024,768]{1,0:T(8,128)(2,1)S(1)}, bf16[1024,768]{1,0:T(8,128)(2,1)S(1)}, u32[]{:S(2)}, u32[]{:S(2)}) collective-permute-start(bf16[1024,768]{1,0:T(8,128)(2,1)S(1)} %down.1.refs_2_.refs_5_), channel_id=1, source_target_pairs={{0,1},{1,0},{2,3},{3,2},{4,5},{5,4},{6,7},{7,6},{8,9},{9,8},{10,11... | collective-permute-start | bytes 4718600 | tf_op jit(solution)/shard_map/ppermute | solution.py:738
  117.2 10.4 %collective-permute-start.22 = (bf16[48,1536]{1,0:T(8,128)(2,1)S(1)}, bf16[48,1536]{1,0:T(8,128)(2,1)S(1)}, u32[]{:S(2)}, u32[]{:S(2)}) collective-permute-start(bf16[48,1536]{1,0:T(8,128)(2,1)S(1)} %get-tuple-element.156.refs_2_), channel_id=1, source_target_pairs={{0,16},{1,17},{2,18},{3,19},{4,20},{5,21},{6,22},{7,23},{8,24},{9,... | collective-permute-start | bytes 442376 | tf_op jit(solution)/shard_map/ppermute | solution.py:751
  118.9 5.7 %collective-permute-start.20 = (f32[16,768]{1,0:T(8,128)S(1)}, f32[16,768]{1,0:T(8,128)S(1)}, u32[]{:S(2)}, u32[]{:S(2)}) collective-permute-start(f32[16,768]{1,0:T(8,128)S(1)} %add.64.refs_7_.refs_0_), channel_id=1, source_target_pairs={{0,8},{2,10},{4,12},{6,14},{8,0},{10,2},{12,4},{14,6},{16,24},{18,... | collective-permute-start | bytes 147464 | tf_op jit(solution)/shard_map/ppermute | solution.py:738
  124.6 5.3 %collective-permute-start.21 = (f32[16,768]{1,0:T(8,128)S(1)}, f32[16,768]{1,0:T(8,128)S(1)}, u32[]{:S(2)}, u32[]{:S(2)}) collective-permute-start(f32[16,768]{1,0:T(8,128)S(1)} %add.65.refs_2_.refs_0_), channel_id=1, source_target_pairs={{0,16},{2,18},{4,20},{6,22},{8,24},{10,26},{12,28},{14,30},{16,0},... | collective-permute-start | bytes 147464 | tf_op jit(solution)/shard_map/ppermute | solution.py:738
  (19 other events, 93.9 us)

commit v3 on v2

--- a/solution.py
+++ b/solution.py
@@ -239,6 +239,8 @@
 
 
 def row_span(index, size):
+    if isinstance(index, int):
+        return pl.ds(index * size, size)
     return pl.ds(pl.multiple_of(index * size, size), size)
 
 
@@ -394,13 +396,36 @@
         part.send(index)
 
 
-def mlp_kernel(blocks, given, made, ordered, grad_mlp):
-    lengths, place, out_bias, gain, bias, tokens, mine, other, up_bias, up, down, cotangent = given
-    hidden, normed_two, inverse_two, active_out, grad_pre, part, down_bias_grad, keep, send = made
+def grad_active_kernel(blocks, given, made, grad_mlp):
+    lengths, place, cotangent, down = given
+    ordered, grad_active, down_bias_grad = made[:3]
+    used = rows_used(lengths)
+    rows = grad_mlp.shape[0]
+    block = rows // cotangent.pieces
+    down_bias_grad.ref[...] = jnp.zeros_like(down_bias_grad.ref)
+
+    @pl.loop(0, cotangent.pieces)
+    def _(index):
+        span = row_span(index, block)
+        row = index * block + lax.broadcasted_iota(jnp.int32, (block, 1), 0)
+        grad = jnp.where(row < used, cotangent.ready(index)[span, :].astype(f32), 0.0)
+        down_bias_grad.ref[...] += column_sum(grad)
+        grad_mlp[span, :] = grad.astype(bf16)
+
+    order_columns(grad_mlp[...], place, ordered.ref, blocks)
+    down = down()
+
+    @pl.loop(0, cotangent.pieces)
+    def _(index):
+        span = row_span(index, block)
+        grad_active.ref[span, :] = dot_t(grad_mlp[span, :], down[...])
+
+
+def mlp_kernel(given, made):
+    out_bias, gain, bias, tokens, mine, other, up_bias, up, ordered, grad_active = given
+    hidden, normed_two, inverse_two, active_out, grad_pre, part, keep, send = made
     rows = hidden.ref.shape[0]
-    used = rows_used(lengths)
     block, tile = rows // 4, 512
-    down_bias_grad.ref[...] = jnp.zeros_like(down_bias_grad.ref)
     out_bias, gain, bias = out_bias(), gain(), bias()
 
     @pl.loop(0, rows // block)
@@ -415,21 +440,17 @@
         normed_two.ref[span, :] = normed.astype(bf16)
         inverse_two.ref[span, :] = jnp.broadcast_to(inverse, (block, LANES))
         hidden.ref[span, :] = (normed * vector(gain) + vector(bias)).astype(bf16)
-        row = index * block + lax.broadcasted_iota(jnp.int32, (block, 1), 0)
-        grad = jnp.where(row < used, cotangent.ready(index)[span, :].astype(f32), 0.0)
-        down_bias_grad.ref[...] += column_sum(grad)
-        grad_mlp[span, :] = grad.astype(bf16)
         for one in (normed_two, inverse_two):
             one.send(index)
 
-    up_bias, up, down = up_bias(), up(), down()
+    up_bias, up, grad_active = up_bias(), up(), grad_active()
 
     block = rows // 2
 
     @pl.loop(0, rows // block)
     def _(index):
         span = row_span(index, block)
-        low, grad = hidden.ref[span, :], grad_mlp[span, :]
+        low = hidden.ref[span, :]
         total = None
         for start in range(0, up.shape[1], tile):
             cols = slice(start, start + tile)
@@ -442,15 +463,14 @@
             slope = share + (active * (1.0 - share)) * (
                 (2 * 0.7978845608028654) + (6 * 0.7978845608028654 * 0.044715) * square
             )
-            grad_low = (dot_t(grad, down[cols, :]) * slope).astype(bf16)
+            grad_low = (grad_active[span, cols] * slope).astype(bf16)
             grad_pre.ref[span, cols] = grad_low
             term = dot_t(grad_low, up[:, cols])
             total = term if total is None else total + term
         active_out.send(index)
         part.ref[span, :] = total.astype(bf16)
 
-    order_columns(grad_mlp[...], place, ordered, blocks)
-    weight_grad(ordered, active_out.ref, keep, send)
+    weight_grad(ordered(), active_out.ref, keep, send)
 
 
 def down_kernel(given, made):
@@ -583,8 +603,7 @@
     key_total[...] = jnp.zeros_like(key_total)
     value_total[...] = jnp.zeros_like(value_total)
 
-    @pl.loop(0, 2)
-    def _(index):
+    def half_of_queries(index):
         span = row_span(index, block)
         query, grad, feature = queries[span, cols], grad_mixed[span, cols], features[span, :]
         grad_feature = grad_features[span, :]
@@ -603,6 +622,12 @@
         key_total[...] += key_term
         value_total[...] += value_term
         grads.ref[span, :LANES] = (jnp.concatenate(turned_grads, axis=0).T * HEAD_DIM**-0.5).astype(bf16)
+
+    if pair == 0:
+        half_of_queries(0)
+        half_of_queries(1)
+    else:
+        pl.loop(0, 2)(half_of_queries)
 
     grads.ref[:, LANES : 2 * LANES] = key_total[...].astype(bf16)
     grads.ref[:, 2 * LANES :] = value_total[...].astype(bf16)
@@ -850,12 +875,24 @@
         limit=28,
     )
     other = swap(part, "mp", 0, 2)
-    (
-        hidden_two, normed_two, inverse_two, activated, grad_pre, norm_part, down_sums,
-        down_keep, down_send,
-    ) = call(
+    turned_grad, grad_active, down_sums, near_tokens, near_up = call(
         chain,
-        functools.partial(mlp_kernel, n_dp),
+        functools.partial(grad_active_kernel, n_dp),
+        "grad_active",
+        [
+            Made((width + 16, rows), bf16, "v"),
+            Made((rows, units), f32, "v"),
+            Made((1, width), f32, "v"),
+            fetch(tokens),
+            fetch(up_weight),
+        ],
+        [scalars, Given(near_place, "s"), far(cotangent, 4), far(down_weight)],
+        scratch=[pltpu.VMEM((rows, width), bf16)],
+        limit=16,
+    )
+    hidden_two, normed_two, inverse_two, activated, grad_pre, norm_part, down_keep, down_send = call(
+        chain,
+        mlp_kernel,
         "mlp",
         [
             Made((rows, width), bf16, "v"),
@@ -864,21 +901,17 @@
             Made((rows, units), bf16, "h", 2),
             Made((rows, units), bf16, "v"),
             Made((rows, width), bf16, "v"),
-            Made((1, width), f32, "v"),
             *halves(units),
         ],
         [
-            scalars,
-            Given(near_place, "s"),
             *map(far, (out_bias, ln2_gain, ln2_bias)),
-            far(tokens, 4),
-            near(part),
-            near(other),
-            *map(far, (up_bias, up_weight, down_weight)),
-            far(cotangent, 4),
+            *map(near, (near_tokens, part, other)),
+            far(up_bias),
+            near(near_up),
+            near(turned_grad),
+            near(grad_active),
         ],
-        scratch=[turned, pltpu.VMEM((rows, width), bf16)],
-        limit=30,
+        limit=22,
     )
     norm_other = swap(norm_part, "mp", 0, 2)
 

time: 131 us -> 129 us (0.985)
  waiting for transfers between devices: 7.96 us -> 5.48 us
  Pallas kernels: 92.9 us -> 94.3 us
    ppermute x8, waiting for transfers between devices: 3.66 us -> 1.02 us  [swap(): return lax.ppermute(values, axis, [(i, i ^ 1 << bit) for i in range(size)])]
    pallas_call x24 -> x25, Pallas kernels: 92.9 us -> 94.3 us  [call(): pl.pallas_call(body, name=name, out_shape=tuple((pins[m.kind](m.shape, m....]
  transfers between devices with their start and end apart: 23 -> 23, of which waited for: 7 -> 7; matrix products, arithmetic and copies ran while one was open for 0% -> 0% of each run, Pallas kernels for 44% -> 49%
where the time goes in v3:
time: 129 us
  Pallas kernels  94.3 us (73%)
  starting transfers between devices  26.2 us (20%)
  waiting for transfers between devices  5.48 us (4%)
  local copies, waits for them, and re-layouts  1.49 us (1%)
  between operations  1.34 us (1%)
    pallas_call x25, Pallas kernels, call(): pl.pallas_call(body, name=name, out_shape=tuple((pins[m.kind](m.shape, m....  94.3 us
    ppermute x15, starting transfers between devices, exchange(): self.came = lax.ppermute(self.send, ('dp', 'mp'), pairs)  19.8 us
    ppermute x8, starting transfers between devices, swap(): return lax.ppermute(values, axis, [(i, i ^ 1 << bit) for i in range(size)])  6.5 us
    ppermute x15, waiting for transfers between devices, exchange(): self.came = lax.ppermute(self.send, ('dp', 'mp'), pairs)  4.46 us
  transfers between devices with their start and end apart: 23, of which 7 were waited for; matrix products, arithmetic and copies ran while one was open for 0% of the time, Pallas kernels for 49%

profile of v3, /device:TPU:0, one launch (start us, length us, event | category | flops | bytes accessed | tf_op | source)
XLA Modules:
  0.0 128.9 jit_solution(9539351962004678683)
XLA Ops:
  1.3 17.8 %qkv_attention.1 = (bf16[1024,768]{1,0:T(8,128)(2,1)}, bf16[1024,384]{1,0:T(8,128)(2,1)}, bf16[1024,384]{1,0:T(8,128)(2,1)}, bf16[1024,384]{1,0:T(8,128)(2,1)}, ...) custom-call(s32[1,16]{1,0:T(1,128)S(1)} %copy-done.7, ...), custom_call_target="tpu_custom_call" | custom-call | flops 20000000000 | bytes 1 | tf_op jit(solution)/shard_map/qkv_attention/pallas_call | solution.py:182
  19.7 6.0 %grad_active.1 = (bf16[784,1024]{1,0:T(8,128)(2,1)S(1)}, f32[1024,1536]{1,0:T(8,128)S(1)}, f32[1,768]{1,0:T(1,128)S(1)}, bf16[1024,768]{1,0:T(8,128)(2,1)S(1)}, bf16[768,1536]{1,0:T(8,128)(2,1)S(1)}) custom-call(s32[1,16]{1,0:T(1,128)S(1)} %copy-done.8, s32[16]{0:T(128)S(1)} %get-tuple-element.179.refs_1_.refs_0_, bf16[1024,768]{1,0:T(8,128)(2,1)} %refs_7_.1, ...), custom_call_target="tpu_custom_call" | custom-call | flops 20000000000 | bytes 1 | tf_op jit(solution)/shard_map/grad_active/pallas_call | solution.py:182
  25.7 13.2 %mlp.1 = (bf16[1024,768]{1,0:T(8,128)(2,1)S(1)}, bf16[1024,768]{1,0:T(8,128)(2,1)}, f32[1024,128]{1,0:T(8,128)}, bf16[1024,1536]{1,0:T(8,128)(2,1)}, bf16[1024,1...) custom-call(f32[768]{0:T(1024)} %refs_0_.13, ...), custom_call_target="tpu_custom_call" | custom-call | flops 20000000000 | bytes 1 | tf_op jit(solution)/shard_map/mlp/pallas_call | solution.py:182
  38.9 2.6 %collective-permute-start.2 = (bf16[384,1536]{1,0:T(8,128)(2,1)S(1)}, bf16[384,1536]{1,0:T(8,128)(2,1)S(1)}, u32[]{:S(2)}, u32[]{:S(2)}) collective-permute-start(bf16[384,1536]{1,0:T(8,128)(2,1)S(1)} %get-tuple-element.123), channel_id=1, source_target_pairs={{0,2},{1,5},{2,0},{3,7},{4,6},{5,1},{6,4},{7,3},{8,10},{9,13},{10,... | collective-permute-start | bytes 3538952 | tf_op jit(solution)/shard_map/ppermute | solution.py:776
  41.8 4.0 %up_grad.1 = (bf16[384,1536]{1,0:T(8,128)(2,1)S(1)}, bf16[384,1536]{1,0:T(8,128)(2,1)S(1)}, f32[8,1536]{1,0:T(8,128)S(1)}) custom-call(s32[16]{0:T(128)S(1)} %get-tuple-element.178.refs_0_, bf16[1024,768]{1,0:T(8,128)(2,1)S(1)} %get-tuple-element.113.refs_1_, bf16[1024,1536]{1,0:T(8,128)(2,1)S(1)} %get-tuple-element.114.refs_2_, ...), custom_call_target="tpu_custom_call" | custom-call | flops 20000000000 | bytes 1 | tf_op jit(solution)/shard_map/up_grad/pallas_call | solution.py:182
  45.8 1.6 %collective-permute-start.5 = (bf16[384,1536]{1,0:T(8,128)(2,1)S(1)}, bf16[384,1536]{1,0:T(8,128)(2,1)S(1)}, u32[]{:S(2)}, u32[]{:S(2)}) collective-permute-start(bf16[384,1536]{1,0:T(8,128)(2,1)S(1)} %get-tuple-element.132), channel_id=1, source_target_pairs={{0,8},{1,9},{2,10},{3,11},{4,12},{5,13},{6,14},{7,15},{8,0},{9,1},... | collective-permute-start | bytes 3538952 | tf_op jit(solution)/shard_map/ppermute | solution.py:776
  47.6 8.3 %middle.1 = (f32[1024,768]{1,0:T(8,128)}, bf16[1024,384]{1,0:T(8,128)(2,1)S(1)}, bf16[1024,128]{1,0:T(8,128)(2,1)S(1)}, f32[8,768]{1,0:T(8,128)S(1)}, bf16[384,3...) custom-call(s32[1,16]{1,0:T(1,128)S(1)} %copy-done.8, s32[16]{0:T(128)S(1)} %get-tuple-element.179.refs_1_.refs_0_, ...), custom_call_target="tpu_custom_call" | custom-call | flops 20000000000 | bytes 1 | tf_op jit(solution)/shard_map/middle/pallas_call | solution.py:182
  55.9 1.6 %collective-permute-start.3 = (bf16[384,384]{1,0:T(8,128)(2,1)S(1)}, bf16[384,384]{1,0:T(8,128)(2,1)S(1)}, u32[]{:S(2)}, u32[]{:S(2)}) collective-permute-start(bf16[384,384]{1,0:T(8,128)(2,1)S(1)} %get-tuple-element.125), channel_id=1, source_target_pairs={{0,2},{1,5},{2,0},{3,7},{4,6},{5,1},{6,4},{7,3},{8,10},{9,13},{10,... | collective-permute-start | bytes 884744 | tf_op jit(solution)/shard_map/ppermute | solution.py:776
  57.5 7.6 %attention_back0.1 = (bf16[1024,384]{1,0:T(8,128)(2,1)S(1)}, f32[8,384]{1,0:T(8,128)S(1)}, bf16[384,384]{1,0:T(8,128)(2,1)S(1)}, bf16[384,384]{1,0:T(8,128)(2,1)S(1)}, bf16[784,1024]{1,0:T(8,128)(2,1)}) custom-call(s32[16]{0:T(128)S(1)} %get-tuple-element.179.refs_1_.refs_0_, bf16[1024,384]{1,0:T(8,128)(2,1)S(1)} %copy-done.17, ...), custom_call_target="tpu_custom_call" | custom-call | flops 20000000000 | bytes 1 | tf_op jit(solution)/shard_map/attention_back0/pallas_call | solution.py:182
  66.0 1.4 %collective-permute-start.4 = (bf16[192,1536]{1,0:T(8,128)(2,1)S(1)}, bf16[192,1536]{1,0:T(8,128)(2,1)S(1)}, u32[]{:S(2)}, u32[]{:S(2)}) collective-permute-start(bf16[192,1536]{1,0:T(8,128)(2,1)S(1)} %get-tuple-element.130), channel_id=1, source_target_pairs={{0,4},{1,3},{2,6},{3,1},{4,0},{5,7},{6,2},{7,5},{8,12},{9,11},{10,... | collective-permute-start | bytes 1769480 | tf_op jit(solution)/shard_map/ppermute | solution.py:776
  67.4 7.7 %attention_back1.1 = (bf16[1024,384]{1,0:T(8,128)(2,1)S(1)}, f32[8,384]{1,0:T(8,128)S(1)}, bf16[384,384]{1,0:T(8,128)(2,1)S(1)}, bf16[384,384]{1,0:T(8,128)(2,1)S(1)}) custom-call(s32[16]{0:T(128)S(1)} %get-tuple-element.179.refs_1_.refs_0_, bf16[1024,384]{1,0:T(8,128)(2,1)S(1)} %copy-done.17, bf16[1024,384]{1,0:T(8,128)(2,1)S(1)} %copy-done.16, ...), custom_call_target="tpu_custom_call" | custom-call | flops 20000000000 | bytes 1 | tf_op jit(solution)/shard_map/attention_back1/pallas_call | solution.py:182
  75.1 1.3 %collective-permute-start.9 = (bf16[384,384]{1,0:T(8,128)(2,1)S(1)}, bf16[384,384]{1,0:T(8,128)(2,1)S(1)}, u32[]{:S(2)}, u32[]{:S(2)}) collective-permute-start(bf16[384,384]{1,0:T(8,128)(2,1)S(1)} %get-tuple-element.143), channel_id=1, source_target_pairs={{0,2},{1,5},{2,0},{3,7},{4,6},{5,1},{6,4},{7,3},{8,10},{9,13},{10,... | collective-permute-start | bytes 884744 | tf_op jit(solution)/shard_map/ppermute | solution.py:776
  78.4 8.0 %attention_back2.1 = (bf16[1024,384]{1,0:T(8,128)(2,1)S(1)}, f32[8,384]{1,0:T(8,128)S(1)}, bf16[384,384]{1,0:T(8,128)(2,1)S(1)}, bf16[384,384]{1,0:T(8,128)(2,1)S(1)}) custom-call(s32[16]{0:T(128)S(1)} %get-tuple-element.179.refs_1_.refs_0_, bf16[1024,384]{1,0:T(8,128)(2,1)S(1)} %copy-done.17, bf16[1024,384]{1,0:T(8,128)(2,1)S(1)} %copy-done.16, ...), custom_call_target="tpu_custom_call" | custom-call | flops 20000000000 | bytes 1 | tf_op jit(solution)/shard_map/attention_back2/pallas_call | solution.py:182
  86.4 1.6 %collective-permute-start.12 = (bf16[384,384]{1,0:T(8,128)(2,1)S(1)}, bf16[384,384]{1,0:T(8,128)(2,1)S(1)}, u32[]{:S(2)}, u32[]{:S(2)}) collective-permute-start(bf16[384,384]{1,0:T(8,128)(2,1)S(1)} %get-tuple-element.154), channel_id=1, source_target_pairs={{0,2},{1,5},{2,0},{3,7},{4,6},{5,1},{6,4},{7,3},{8,10},{9,13},{10,... | collective-permute-start | bytes 884744 | tf_op jit(solution)/shard_map/ppermute | solution.py:776
  89.1 2.7 %collective-permute-start.14 = (bf16[48,1536]{1,0:T(8,128)(2,1)S(1)}, bf16[48,1536]{1,0:T(8,128)(2,1)S(1)}, u32[]{:S(2)}, u32[]{:S(2)}) collective-permute-start(bf16[48,1536]{1,0:T(8,128)(2,1)S(1)} %get-tuple-element.145.refs_4_), channel_id=1, source_target_pairs={{0,16},{1,17},{2,18},{3,19},{4,20},{5,21},{6,22},{7,23},{8,24},{9,... | collective-permute-start | bytes 442376 | tf_op jit(solution)/shard_map/ppermute | solution.py:776
  91.7 1.0 collective-permute-start.11
  92.8 2.8 %first.1.refs_8_.refs_2_ = bf16[1024,768]{1,0:T(8,128)(2,1)S(1)} custom-call(bf16[1024,384]{1,0:T(8,128)(2,1)S(1)} %get-tuple-element.120.refs_0_, bf16[1024,384]{1,0:T(8,128)(2,1)S(1)} %get-tuple-element.128.refs_1_, bf16[1024,384]{1,0:T(8,128)(2,1)S(1)} %get-tuple-element.137.refs_2_, bf16[3,768,384]{2,1,0:T(8,128)(2,1)S(1)} %bitcast.5, ...), custom_call_target="tpu_custom_call" | custom-call | flops 20000000000 | bytes 1 | tf_op jit(solution)/shard_map/first/pallas_call | solution.py:182
  95.9 1.1 collective-permute-start.16
  96.9 1.5 %collective-permute-done.11.refs_1_ = bf16[96,1536]{1,0:T(8,128)(2,1)S(1)} collective-permute-done((bf16[96,1536]{1,0:T(8,128)(2,1)S(1)}, bf16[96,1536]{1,0:T(8,128)(2,1)S(1)}, u32[]{:S(2)}, u32[]{:S(2)}) %collective-permute-start.11) | collective-permute-done | bytes 294944 | tf_op jit(solution)/shard_map/ppermute | solution.py:776
  99.2 1.0 collective-permute-start.15
  100.9 4.4 %last.1 = (f32[1024,768]{1,0:T(8,128)}, f32[16,768]{1,0:T(8,128)S(1)}) custom-call(f32[768]{0:T(1024)} %refs_0_.11, bf16[1024,768]{1,0:T(8,128)(2,1)S(1)} %copy-done.3, bf16[1024,768]{1,0:T(8,128)(2,1)S(1)} %first.1.refs_8_.refs_2_, bf16[1024,768]{1,0:T(8,128)(2,1)S(1)} %collective-permute-done.10.refs_3_, f32[1024,768]{1,0:T(8,128)S(1)} %copy-done.10, ...), custom_call_target="tpu_custom_call" | custom-call | flops 20000000000 | bytes 1 | tf_op jit(solution)/shard_map/last/pallas_call | solution.py:182
  105.3 1.3 %collective-permute-start.13 = (f32[16,768]{1,0:T(8,128)S(1)}, f32[16,768]{1,0:T(8,128)S(1)}, u32[]{:S(2)}, u32[]{:S(2)}) collective-permute-start(f32[16,768]{1,0:T(8,128)S(1)} %get-tuple-element.157.refs_2_.refs_0_), channel_id=1, source_target_pairs={{0,2},{2,0},{4,6},{6,4},{8,10},{10,8},{12,14},{14,12},{16,18},{18,... | collective-permute-start | bytes 147464 | tf_op jit(solution)/shard_map/ppermute | solution.py:763
  108.0 1.8 %final.2 = (f32[48,1536]{1,0:T(8,128)}, f32[48,1536]{1,0:T(8,128)}) custom-call(f32[48,1536]{1,0:T(8,128)} %get-tuple-element.158.refs_0_, bf16[48,1536]{1,0:T(8,128)(2,1)S(1)} %collective-permute-done.14.refs_1_, f32[48,1536]{1,0:T(8,128)} %get-tuple-element.159.refs_2_, bf16[48,1536]{1,0:T(8,128)(2,1)S(1)} %collective-permute-done.15.refs_3_, ...), custom_call_target="tpu_custom_call" | custom-call | bytes 1 | tf_op jit(solution)/shard_map/final/pallas_call | solution.py:182
  109.9 1.1 collective-permute-start.18
  111.0 3.1 %down.1.refs_2_.refs_5_ = bf16[1024,768]{1,0:T(8,128)(2,1)S(1)} custom-call(bf16[1536,768]{1,0:T(8,128)(2,1)S(1)} %copy-done, bf16[1024,1536]{1,0:T(8,128)(2,1)S(1)} %copy-done.9, f32[16,768]{1,0:T(8,128)S(1)} %add.63.refs_2_.refs_0_), custom_call_target="tpu_custom_call" | custom-call | flops 20000000000 | bytes 1 | tf_op jit(solution)/shard_map/down/pallas_call | solution.py:182
  115.3 1.7 %collective-permute-start.22 = (bf16[48,1536]{1,0:T(8,128)(2,1)S(1)}, bf16[48,1536]{1,0:T(8,128)(2,1)S(1)}, u32[]{:S(2)}, u32[]{:S(2)}) collective-permute-start(bf16[48,1536]{1,0:T(8,128)(2,1)S(1)} %get-tuple-element.164.refs_2_), channel_id=1, source_target_pairs={{0,16},{1,17},{2,18},{3,19},{4,20},{5,21},{6,22},{7,23},{8,24},{9,... | collective-permute-start | bytes 442376 | tf_op jit(solution)/shard_map/ppermute | solution.py:776
  117.0 1.8 %collective-permute-start.20 = (f32[16,768]{1,0:T(8,128)S(1)}, f32[16,768]{1,0:T(8,128)S(1)}, u32[]{:S(2)}, u32[]{:S(2)}) collective-permute-start(f32[16,768]{1,0:T(8,128)S(1)} %add.64.refs_7_.refs_0_), channel_id=1, source_target_pairs={{0,8},{2,10},{4,12},{6,14},{8,0},{10,2},{12,4},{14,6},{16,24},{18,... | collective-permute-start | bytes 147464 | tf_op jit(solution)/shard_map/ppermute | solution.py:763
  118.8 3.9 %output.1.refs_2_ = bf16[1024,768]{1,0:T(8,128)(2,1)} custom-call(f32[768]{0:T(1024)} %refs_0_.13, f32[768]{0:T(1024)} %refs_1_.7, bf16[1024,768]{1,0:T(8,128)(2,1)} %refs_2_.9, bf16[1024,768]{1,0:T(8,128)(2,1)} %copy-done.4, bf16[1024,768]{1,0:T(8,128)(2,1)} %copy-done.5, bf16[1024,768]{1,0:T(8,128)(2,1)S(1)} %down.1.refs_2_.refs_5_, ...), custom_call_target="tpu_custom_call" | custom-call | flops 20000000000 | bytes 1 | tf_op jit(solution)/shard_map/output/pallas_call | solution.py:182
  122.7 1.4 %collective-permute-start.21 = (f32[16,768]{1,0:T(8,128)S(1)}, f32[16,768]{1,0:T(8,128)S(1)}, u32[]{:S(2)}, u32[]{:S(2)}) collective-permute-start(f32[16,768]{1,0:T(8,128)S(1)} %add.65.refs_2_.refs_0_), channel_id=1, source_target_pairs={{0,16},{2,18},{4,20},{6,22},{8,24},{10,26},{12,28},{14,30},{16,0},... | collective-permute-start | bytes 147464 | tf_op jit(solution)/shard_map/ppermute | solution.py:763
  124.1 1.2 collective-permute-done.22.refs_1_
  125.3 1.7 %final.3 = (f32[3,48,384]{2,1,0:T(8,128)}, f32[48,384]{1,0:T(8,128)}) custom-call(f32[48,1536]{1,0:T(8,128)} %get-tuple-element.166.refs_0_, bf16[48,1536]{1,0:T(8,128)(2,1)S(1)} %collective-permute-done.22.refs_1_, f32[16,768]{1,0:T(8,128)S(1)} %add.65.refs_2_.refs_0_), custom_call_target="tpu_custom_call" | custom-call | flops 20000000000 | bytes 1 | tf_op jit(solution)/shard_map/final/pallas_call | solution.py:182
  127.0 1.0 collective-permute-done.21.refs_1_
  (96 shorter events, 10.5 us)
Async XLA Ops:
  1.3 18.4 %copy-start.8 = (s32[1,16]{1,0:T(1,128)S(1)}, s32[1,16]{1,0:T(1,128)}, u32[]{:S(2)}) copy-start(s32[1,16]{1,0:T(1,128)} %refs_0_.10) | copy-start | bytes 196
  19.1 6.6 %collective-permute-start = (bf16[1024,768]{1,0:T(8,128)(2,1)S(1)}, bf16[1024,768]{1,0:T(8,128)(2,1)S(1)}, u32[]{:S(2)}, u32[]{:S(2)}) collective-permute-start(bf16[1024,768]{1,0:T(8,128)(2,1)S(1)} %get-tuple-element.96.refs_4_.refs_3_), channel_id=1, source_target_pairs={{0,1},{1,0},{2,3},{3,2},{4,5},{5,4},{6,7},{7,6},{8,9},{9,8},{10,11... | collective-permute-start | bytes 4718600 | tf_op jit(solution)/shard_map/ppermute | solution.py:763
  25.7 13.2 %copy-start.26 = (f32[1,768]{1,0:T(1,128)}, f32[1,768]{1,0:T(1,128)S(1)}, u32[]{:S(2)}) copy-start(f32[1,768]{1,0:T(1,128)S(1)} %get-tuple-element.102.refs_10_.refs_6_) | copy-start | bytes 9220
  25.7 13.2 %copy-start.5 = (bf16[1024,768]{1,0:T(8,128)(2,1)}, bf16[1024,768]{1,0:T(8,128)(2,1)S(1)}, u32[]{:S(2)}) copy-start(bf16[1024,768]{1,0:T(8,128)(2,1)S(1)} %collective-permute-done.refs_5_.refs_4_) | copy-start | bytes 4718596
  38.9 26.8 %collective-permute-start.2 = (bf16[384,1536]{1,0:T(8,128)(2,1)S(1)}, bf16[384,1536]{1,0:T(8,128)(2,1)S(1)}, u32[]{:S(2)}, u32[]{:S(2)}) collective-permute-start(bf16[384,1536]{1,0:T(8,128)(2,1)S(1)} %get-tuple-element.123), channel_id=1, source_target_pairs={{0,2},{1,5},{2,0},{3,7},{4,6},{5,1},{6,4},{7,3},{8,10},{9,13},{10,... | collective-permute-start | bytes 3538952 | tf_op jit(solution)/shard_map/ppermute | solution.py:776
  41.5 6.0 %collective-permute-start.1 = (bf16[1024,768]{1,0:T(8,128)(2,1)S(1)}, bf16[1024,768]{1,0:T(8,128)(2,1)S(1)}, u32[]{:S(2)}, u32[]{:S(2)}) collective-permute-start(bf16[1024,768]{1,0:T(8,128)(2,1)S(1)} %get-tuple-element.108.refs_3_), channel_id=1, source_target_pairs={{0,1},{1,0},{2,3},{3,2},{4,5},{5,4},{6,7},{7,6},{8,9},{9,8},{10,11... | collective-permute-start | bytes 4718600 | tf_op jit(solution)/shard_map/ppermute | solution.py:763
  45.8 10.1 %copy-start.22 = (f32[8,1536]{1,0:T(8,128)}, f32[8,1536]{1,0:T(8,128)S(1)}, u32[]{:S(2)}) copy-start(f32[8,1536]{1,0:T(8,128)S(1)} %get-tuple-element.115.refs_11_.refs_7_) | copy-start | bytes 147460
  45.8 30.6 %collective-permute-start.5 = (bf16[384,1536]{1,0:T(8,128)(2,1)S(1)}, bf16[384,1536]{1,0:T(8,128)(2,1)S(1)}, u32[]{:S(2)}, u32[]{:S(2)}) collective-permute-start(bf16[384,1536]{1,0:T(8,128)(2,1)S(1)} %get-tuple-element.132), channel_id=1, source_target_pairs={{0,8},{1,9},{2,10},{3,11},{4,12},{5,13},{6,14},{7,15},{8,0},{9,1},... | collective-permute-start | bytes 3538952 | tf_op jit(solution)/shard_map/ppermute | solution.py:776
  47.5 9.9 %copy-start.14 = (bf16[1024,768]{1,0:T(8,128)(2,1)S(1)}, bf16[1024,768]{1,0:T(8,128)(2,1)}, u32[]{:S(2)}) copy-start(bf16[1024,768]{1,0:T(8,128)(2,1)} %get-tuple-element.118.refs_8_) | copy-start | bytes 4718596
  47.6 9.9 %copy-start.16 = (bf16[1024,384]{1,0:T(8,128)(2,1)S(1)}, bf16[1024,384]{1,0:T(8,128)(2,1)}, u32[]{:S(2)}) copy-start(bf16[1024,384]{1,0:T(8,128)(2,1)} %get-tuple-element.105.refs_2_) | copy-start | bytes 2359300
  47.6 9.9 %copy-start.17 = (bf16[1024,384]{1,0:T(8,128)(2,1)S(1)}, bf16[1024,384]{1,0:T(8,128)(2,1)}, u32[]{:S(2)}) copy-start(bf16[1024,384]{1,0:T(8,128)(2,1)} %get-tuple-element.104.refs_1_) | copy-start | bytes 2359300
  47.6 9.9 %copy-start.18 = (bf16[1024,384]{1,0:T(8,128)(2,1)S(1)}, bf16[1024,384]{1,0:T(8,128)(2,1)}, u32[]{:S(2)}) copy-start(bf16[1024,384]{1,0:T(8,128)(2,1)} %get-tuple-element.106.refs_3_) | copy-start | bytes 2359300
  55.9 9.8 %collective-permute-start.3 = (bf16[384,384]{1,0:T(8,128)(2,1)S(1)}, bf16[384,384]{1,0:T(8,128)(2,1)S(1)}, u32[]{:S(2)}, u32[]{:S(2)}) collective-permute-start(bf16[384,384]{1,0:T(8,128)(2,1)S(1)} %get-tuple-element.125), channel_id=1, source_target_pairs={{0,2},{1,5},{2,0},{3,7},{4,6},{5,1},{6,4},{7,3},{8,10},{9,13},{10,... | collective-permute-start | bytes 884744 | tf_op jit(solution)/shard_map/ppermute | solution.py:776
  65.1 11.4 %collective-permute-start.6 = (bf16[384,384]{1,0:T(8,128)(2,1)S(1)}, bf16[384,384]{1,0:T(8,128)(2,1)S(1)}, u32[]{:S(2)}, u32[]{:S(2)}) collective-permute-start(bf16[384,384]{1,0:T(8,128)(2,1)S(1)} %get-tuple-element.134), channel_id=1, source_target_pairs={{0,2},{1,5},{2,0},{3,7},{4,6},{5,1},{6,4},{7,3},{8,10},{9,13},{10,... | collective-permute-start | bytes 884744 | tf_op jit(solution)/shard_map/ppermute | solution.py:776
  66.0 10.9 %collective-permute-start.4 = (bf16[192,1536]{1,0:T(8,128)(2,1)S(1)}, bf16[192,1536]{1,0:T(8,128)(2,1)S(1)}, u32[]{:S(2)}, u32[]{:S(2)}) collective-permute-start(bf16[192,1536]{1,0:T(8,128)(2,1)S(1)} %get-tuple-element.130), channel_id=1, source_target_pairs={{0,4},{1,3},{2,6},{3,1},{4,0},{5,7},{6,2},{7,5},{8,12},{9,11},{10,... | collective-permute-start | bytes 1769480 | tf_op jit(solution)/shard_map/ppermute | solution.py:776
  75.1 12.9 %collective-permute-start.9 = (bf16[384,384]{1,0:T(8,128)(2,1)S(1)}, bf16[384,384]{1,0:T(8,128)(2,1)S(1)}, u32[]{:S(2)}, u32[]{:S(2)}) collective-permute-start(bf16[384,384]{1,0:T(8,128)(2,1)S(1)} %get-tuple-element.143), channel_id=1, source_target_pairs={{0,2},{1,5},{2,0},{3,7},{4,6},{5,1},{6,4},{7,3},{8,10},{9,13},{10,... | collective-permute-start | bytes 884744 | tf_op jit(solution)/shard_map/ppermute | solution.py:776
  77.4 10.6 %collective-permute-start.7 = (bf16[96,1536]{1,0:T(8,128)(2,1)S(1)}, bf16[96,1536]{1,0:T(8,128)(2,1)S(1)}, u32[]{:S(2)}, u32[]{:S(2)}) collective-permute-start(bf16[96,1536]{1,0:T(8,128)(2,1)S(1)} %get-tuple-element.139), channel_id=1, source_target_pairs={{0,8},{1,9},{2,10},{3,11},{4,12},{5,13},{6,14},{7,15},{8,0},{9,1},... | collective-permute-start | bytes 884744 | tf_op jit(solution)/shard_map/ppermute | solution.py:776
  77.9 10.3 %collective-permute-start.8 = (bf16[192,1536]{1,0:T(8,128)(2,1)S(1)}, bf16[192,1536]{1,0:T(8,128)(2,1)S(1)}, u32[]{:S(2)}, u32[]{:S(2)}) collective-permute-start(bf16[192,1536]{1,0:T(8,128)(2,1)S(1)} %get-tuple-element.141), channel_id=1, source_target_pairs={{0,2},{1,5},{2,0},{3,7},{4,6},{5,1},{6,4},{7,3},{8,10},{9,13},{10,... | collective-permute-start | bytes 1769480 | tf_op jit(solution)/shard_map/ppermute | solution.py:776
  86.4 9.3 %collective-permute-start.12 = (bf16[384,384]{1,0:T(8,128)(2,1)S(1)}, bf16[384,384]{1,0:T(8,128)(2,1)S(1)}, u32[]{:S(2)}, u32[]{:S(2)}) collective-permute-start(bf16[384,384]{1,0:T(8,128)(2,1)S(1)} %get-tuple-element.154), channel_id=1, source_target_pairs={{0,2},{1,5},{2,0},{3,7},{4,6},{5,1},{6,4},{7,3},{8,10},{9,13},{10,... | collective-permute-start | bytes 884744 | tf_op jit(solution)/shard_map/ppermute | solution.py:776
  89.1 18.4 %collective-permute-start.14 = (bf16[48,1536]{1,0:T(8,128)(2,1)S(1)}, bf16[48,1536]{1,0:T(8,128)(2,1)S(1)}, u32[]{:S(2)}, u32[]{:S(2)}) collective-permute-start(bf16[48,1536]{1,0:T(8,128)(2,1)S(1)} %get-tuple-element.145.refs_4_), channel_id=1, source_target_pairs={{0,16},{1,17},{2,18},{3,19},{4,20},{5,21},{6,22},{7,23},{8,24},{9,... | collective-permute-start | bytes 442376 | tf_op jit(solution)/shard_map/ppermute | solution.py:776
  91.7 6.7 %collective-permute-start.11 = (bf16[96,1536]{1,0:T(8,128)(2,1)S(1)}, bf16[96,1536]{1,0:T(8,128)(2,1)S(1)}, u32[]{:S(2)}, u32[]{:S(2)}) collective-permute-start(bf16[96,1536]{1,0:T(8,128)(2,1)S(1)} %get-tuple-element.148), channel_id=1, source_target_pairs={{0,4},{1,3},{2,6},{3,1},{4,0},{5,7},{6,2},{7,5},{8,12},{9,11},{10,... | collective-permute-start | bytes 884744 | tf_op jit(solution)/shard_map/ppermute | solution.py:776
  95.6 4.6 %collective-permute-start.10 = (bf16[1024,768]{1,0:T(8,128)(2,1)S(1)}, bf16[1024,768]{1,0:T(8,128)(2,1)S(1)}, u32[]{:S(2)}, u32[]{:S(2)}) collective-permute-start(bf16[1024,768]{1,0:T(8,128)(2,1)S(1)} %first.1.refs_8_.refs_2_), channel_id=1, source_target_pairs={{0,1},{1,0},{2,3},{3,2},{4,5},{5,4},{6,7},{7,6},{8,9},{9,8},{10,11... | collective-permute-start | bytes 4718600 | tf_op jit(solution)/shard_map/ppermute | solution.py:763
  95.9 10.7 %collective-permute-start.16 = (bf16[192,1536]{1,0:T(8,128)(2,1)S(1)}, bf16[192,1536]{1,0:T(8,128)(2,1)S(1)}, u32[]{:S(2)}, u32[]{:S(2)}) collective-permute-start(bf16[192,1536]{1,0:T(8,128)(2,1)S(1)} %get-tuple-element.155.refs_2_), channel_id=1, source_target_pairs={{0,4},{1,3},{2,6},{3,1},{4,0},{5,7},{6,2},{7,5},{8,12},{9,11},{10,... | collective-permute-start | bytes 1769480 | tf_op jit(solution)/shard_map/ppermute | solution.py:776
  99.2 8.8 %collective-permute-start.15 = (bf16[48,1536]{1,0:T(8,128)(2,1)S(1)}, bf16[48,1536]{1,0:T(8,128)(2,1)S(1)}, u32[]{:S(2)}, u32[]{:S(2)}) collective-permute-start(bf16[48,1536]{1,0:T(8,128)(2,1)S(1)} %get-tuple-element.156.refs_11_), channel_id=1, source_target_pairs={{0,16},{1,17},{2,18},{3,19},{4,20},{5,21},{6,22},{7,23},{8,24},{9,... | collective-permute-start | bytes 442376 | tf_op jit(solution)/shard_map/ppermute | solution.py:776
  100.9 10.0 %copy-start.9 = (bf16[1024,1536]{1,0:T(8,128)(2,1)S(1)}, bf16[1024,1536]{1,0:T(8,128)(2,1)}, u32[]{:S(2)}) copy-start(bf16[1024,1536]{1,0:T(8,128)(2,1)} %get-tuple-element.103.refs_1_) | copy-start | bytes 9437188
  105.3 4.5 %collective-permute-start.13 = (f32[16,768]{1,0:T(8,128)S(1)}, f32[16,768]{1,0:T(8,128)S(1)}, u32[]{:S(2)}, u32[]{:S(2)}) collective-permute-start(f32[16,768]{1,0:T(8,128)S(1)} %get-tuple-element.157.refs_2_.refs_0_), channel_id=1, source_target_pairs={{0,2},{2,0},{4,6},{6,4},{8,10},{10,8},{12,14},{14,12},{16,18},{18,... | collective-permute-start | bytes 147464 | tf_op jit(solution)/shard_map/ppermute | solution.py:763
  106.7 7.8 %collective-permute-start.19 = (bf16[96,1536]{1,0:T(8,128)(2,1)S(1)}, bf16[96,1536]{1,0:T(8,128)(2,1)S(1)}, u32[]{:S(2)}, u32[]{:S(2)}) collective-permute-start(bf16[96,1536]{1,0:T(8,128)(2,1)S(1)} %get-tuple-element.161.refs_4_), channel_id=1, source_target_pairs={{0,8},{1,9},{2,10},{3,11},{4,12},{5,13},{6,14},{7,15},{8,0},{9,1},... | collective-permute-start | bytes 884744 | tf_op jit(solution)/shard_map/ppermute | solution.py:776
  109.9 7.1 %collective-permute-start.18 = (f32[16,768]{1,0:T(8,128)S(1)}, f32[16,768]{1,0:T(8,128)S(1)}, u32[]{:S(2)}, u32[]{:S(2)}) collective-permute-start(f32[16,768]{1,0:T(8,128)S(1)} %add.63.refs_2_.refs_0_), channel_id=1, source_target_pairs={{0,4},{2,6},{4,0},{6,2},{8,12},{10,14},{12,8},{14,10},{16,20},{18,... | collective-permute-start | bytes 147464 | tf_op jit(solution)/shard_map/ppermute | solution.py:763
  114.1 4.7 %collective-permute-start.17 = (bf16[1024,768]{1,0:T(8,128)(2,1)S(1)}, bf16[1024,768]{1,0:T(8,128)(2,1)S(1)}, u32[]{:S(2)}, u32[]{:S(2)}) collective-permute-start(bf16[1024,768]{1,0:T(8,128)(2,1)S(1)} %down.1.refs_2_.refs_5_), channel_id=1, source_target_pairs={{0,1},{1,0},{2,3},{3,2},{4,5},{5,4},{6,7},{7,6},{8,9},{9,8},{10,11... | collective-permute-start | bytes 4718600 | tf_op jit(solution)/shard_map/ppermute | solution.py:763
  115.3 10.0 %collective-permute-start.22 = (bf16[48,1536]{1,0:T(8,128)(2,1)S(1)}, bf16[48,1536]{1,0:T(8,128)(2,1)S(1)}, u32[]{:S(2)}, u32[]{:S(2)}) collective-permute-start(bf16[48,1536]{1,0:T(8,128)(2,1)S(1)} %get-tuple-element.164.refs_2_), channel_id=1, source_target_pairs={{0,16},{1,17},{2,18},{3,19},{4,20},{5,21},{6,22},{7,23},{8,24},{9,... | collective-permute-start | bytes 442376 | tf_op jit(solution)/shard_map/ppermute | solution.py:776
  117.0 5.7 %collective-permute-start.20 = (f32[16,768]{1,0:T(8,128)S(1)}, f32[16,768]{1,0:T(8,128)S(1)}, u32[]{:S(2)}, u32[]{:S(2)}) collective-permute-start(f32[16,768]{1,0:T(8,128)S(1)} %add.64.refs_7_.refs_0_), channel_id=1, source_target_pairs={{0,8},{2,10},{4,12},{6,14},{8,0},{10,2},{12,4},{14,6},{16,24},{18,... | collective-permute-start | bytes 147464 | tf_op jit(solution)/shard_map/ppermute | solution.py:763
  122.7 5.3 %collective-permute-start.21 = (f32[16,768]{1,0:T(8,128)S(1)}, f32[16,768]{1,0:T(8,128)S(1)}, u32[]{:S(2)}, u32[]{:S(2)}) collective-permute-start(f32[16,768]{1,0:T(8,128)S(1)} %add.65.refs_2_.refs_0_), channel_id=1, source_target_pairs={{0,16},{2,18},{4,20},{6,22},{8,24},{10,26},{12,28},{14,30},{16,0},... | collective-permute-start | bytes 147464 | tf_op jit(solution)/shard_map/ppermute | solution.py:763
  (19 other events, 93.0 us)

commit v4 on v3

--- a/solution.py
+++ b/solution.py
@@ -623,7 +623,7 @@
         value_total[...] += value_term
         grads.ref[span, :LANES] = (jnp.concatenate(turned_grads, axis=0).T * HEAD_DIM**-0.5).astype(bf16)
 
-    if pair == 0:
+    if pair % 2 == 0:
         half_of_queries(0)
         half_of_queries(1)
     else:

time: 129 us -> 128 us (level)
    ppermute x15, starting transfers between devices: 19.8 us -> 17.9 us  [exchange(): self.came = lax.ppermute(self.send, ('dp', 'mp'), pairs)]
  transfers between devices with their start and end apart: 23 -> 23, of which waited for: 7 -> 6; matrix products, arithmetic and copies ran while one was open for 0% -> 0% of each run, Pallas kernels for 49% -> 48%
where the time goes in v4:
time: 128 us
  Pallas kernels  93.6 us (73%)
  starting transfers between devices  25.5 us (20%)
  waiting for transfers between devices  5.68 us (4%)
  local copies, waits for them, and re-layouts  2.06 us (2%)
  between operations  1.34 us (1%)
    pallas_call x25, Pallas kernels, call(): pl.pallas_call(body, name=name, out_shape=tuple((pins[m.kind](m.shape, m....  93.6 us
    ppermute x15, starting transfers between devices, exchange(): self.came = lax.ppermute(self.send, ('dp', 'mp'), pairs)  17.9 us
    ppermute x8, starting transfers between devices, swap(): return lax.ppermute(values, axis, [(i, i ^ 1 << bit) for i in range(size)])  7.53 us
    ppermute x15, waiting for transfers between devices, exchange(): self.came = lax.ppermute(self.send, ('dp', 'mp'), pairs)  5.66 us
  transfers between devices with their start and end apart: 23, of which 6 were waited for; matrix products, arithmetic and copies ran while one was open for 0% of the time, Pallas kernels for 48%

profile of v4, /device:TPU:0, one launch (start us, length us, event | category | flops | bytes accessed | tf_op | source)
XLA Modules:
  0.0 128.1 jit_solution(6356550211593725510)
XLA Ops:
  1.3 17.8 %qkv_attention.1 = (bf16[1024,768]{1,0:T(8,128)(2,1)}, bf16[1024,384]{1,0:T(8,128)(2,1)}, bf16[1024,384]{1,0:T(8,128)(2,1)}, bf16[1024,384]{1,0:T(8,128)(2,1)}, ...) custom-call(s32[1,16]{1,0:T(1,128)S(1)} %copy-done.7, ...), custom_call_target="tpu_custom_call" | custom-call | flops 20000000000 | bytes 1 | tf_op jit(solution)/shard_map/qkv_attention/pallas_call | solution.py:182
  19.7 6.0 %grad_active.1 = (bf16[784,1024]{1,0:T(8,128)(2,1)S(1)}, f32[1024,1536]{1,0:T(8,128)S(1)}, f32[1,768]{1,0:T(1,128)S(1)}, bf16[1024,768]{1,0:T(8,128)(2,1)S(1)}, bf16[768,1536]{1,0:T(8,128)(2,1)S(1)}) custom-call(s32[1,16]{1,0:T(1,128)S(1)} %copy-done.8, s32[16]{0:T(128)S(1)} %get-tuple-element.179.refs_1_.refs_0_, bf16[1024,768]{1,0:T(8,128)(2,1)} %refs_7_.1, ...), custom_call_target="tpu_custom_call" | custom-call | flops 20000000000 | bytes 1 | tf_op jit(solution)/shard_map/grad_active/pallas_call | solution.py:182
  25.7 13.2 %mlp.1 = (bf16[1024,768]{1,0:T(8,128)(2,1)S(1)}, bf16[1024,768]{1,0:T(8,128)(2,1)}, f32[1024,128]{1,0:T(8,128)}, bf16[1024,1536]{1,0:T(8,128)(2,1)}, bf16[1024,1...) custom-call(f32[768]{0:T(1024)} %refs_0_.13, ...), custom_call_target="tpu_custom_call" | custom-call | flops 20000000000 | bytes 1 | tf_op jit(solution)/shard_map/mlp/pallas_call | solution.py:182
  38.9 2.6 %collective-permute-start.2 = (bf16[384,1536]{1,0:T(8,128)(2,1)S(1)}, bf16[384,1536]{1,0:T(8,128)(2,1)S(1)}, u32[]{:S(2)}, u32[]{:S(2)}) collective-permute-start(bf16[384,1536]{1,0:T(8,128)(2,1)S(1)} %get-tuple-element.123), channel_id=1, source_target_pairs={{0,2},{1,5},{2,0},{3,7},{4,6},{5,1},{6,4},{7,3},{8,10},{9,13},{10,... | collective-permute-start | bytes 3538952 | tf_op jit(solution)/shard_map/ppermute | solution.py:776
  41.8 4.0 %up_grad.1 = (bf16[384,1536]{1,0:T(8,128)(2,1)S(1)}, bf16[384,1536]{1,0:T(8,128)(2,1)S(1)}, f32[8,1536]{1,0:T(8,128)S(1)}) custom-call(s32[16]{0:T(128)S(1)} %get-tuple-element.178.refs_0_, bf16[1024,768]{1,0:T(8,128)(2,1)S(1)} %get-tuple-element.113.refs_1_, bf16[1024,1536]{1,0:T(8,128)(2,1)S(1)} %get-tuple-element.114.refs_2_, ...), custom_call_target="tpu_custom_call" | custom-call | flops 20000000000 | bytes 1 | tf_op jit(solution)/shard_map/up_grad/pallas_call | solution.py:182
  45.8 1.6 %collective-permute-start.5 = (bf16[384,1536]{1,0:T(8,128)(2,1)S(1)}, bf16[384,1536]{1,0:T(8,128)(2,1)S(1)}, u32[]{:S(2)}, u32[]{:S(2)}) collective-permute-start(bf16[384,1536]{1,0:T(8,128)(2,1)S(1)} %get-tuple-element.132), channel_id=1, source_target_pairs={{0,8},{1,9},{2,10},{3,11},{4,12},{5,13},{6,14},{7,15},{8,0},{9,1},... | collective-permute-start | bytes 3538952 | tf_op jit(solution)/shard_map/ppermute | solution.py:776
  47.6 8.3 %middle.1 = (f32[1024,768]{1,0:T(8,128)}, bf16[1024,384]{1,0:T(8,128)(2,1)S(1)}, bf16[1024,128]{1,0:T(8,128)(2,1)S(1)}, f32[8,768]{1,0:T(8,128)S(1)}, bf16[384,3...) custom-call(s32[1,16]{1,0:T(1,128)S(1)} %copy-done.8, s32[16]{0:T(128)S(1)} %get-tuple-element.179.refs_1_.refs_0_, ...), custom_call_target="tpu_custom_call" | custom-call | flops 20000000000 | bytes 1 | tf_op jit(solution)/shard_map/middle/pallas_call | solution.py:182
  55.9 1.6 %collective-permute-start.3 = (bf16[384,384]{1,0:T(8,128)(2,1)S(1)}, bf16[384,384]{1,0:T(8,128)(2,1)S(1)}, u32[]{:S(2)}, u32[]{:S(2)}) collective-permute-start(bf16[384,384]{1,0:T(8,128)(2,1)S(1)} %get-tuple-element.125), channel_id=1, source_target_pairs={{0,2},{1,5},{2,0},{3,7},{4,6},{5,1},{6,4},{7,3},{8,10},{9,13},{10,... | collective-permute-start | bytes 884744 | tf_op jit(solution)/shard_map/ppermute | solution.py:776
  57.5 7.6 %attention_back0.1 = (bf16[1024,384]{1,0:T(8,128)(2,1)S(1)}, f32[8,384]{1,0:T(8,128)S(1)}, bf16[384,384]{1,0:T(8,128)(2,1)S(1)}, bf16[384,384]{1,0:T(8,128)(2,1)S(1)}, bf16[784,1024]{1,0:T(8,128)(2,1)}) custom-call(s32[16]{0:T(128)S(1)} %get-tuple-element.179.refs_1_.refs_0_, bf16[1024,384]{1,0:T(8,128)(2,1)S(1)} %copy-done.17, ...), custom_call_target="tpu_custom_call" | custom-call | flops 20000000000 | bytes 1 | tf_op jit(solution)/shard_map/attention_back0/pallas_call | solution.py:182
  66.0 1.4 %collective-permute-start.4 = (bf16[192,1536]{1,0:T(8,128)(2,1)S(1)}, bf16[192,1536]{1,0:T(8,128)(2,1)S(1)}, u32[]{:S(2)}, u32[]{:S(2)}) collective-permute-start(bf16[192,1536]{1,0:T(8,128)(2,1)S(1)} %get-tuple-element.130), channel_id=1, source_target_pairs={{0,4},{1,3},{2,6},{3,1},{4,0},{5,7},{6,2},{7,5},{8,12},{9,11},{10,... | collective-permute-start | bytes 1769480 | tf_op jit(solution)/shard_map/ppermute | solution.py:776
  67.4 8.0 %attention_back1.1 = (bf16[1024,384]{1,0:T(8,128)(2,1)S(1)}, f32[8,384]{1,0:T(8,128)S(1)}, bf16[384,384]{1,0:T(8,128)(2,1)S(1)}, bf16[384,384]{1,0:T(8,128)(2,1)S(1)}) custom-call(s32[16]{0:T(128)S(1)} %get-tuple-element.179.refs_1_.refs_0_, bf16[1024,384]{1,0:T(8,128)(2,1)S(1)} %copy-done.17, bf16[1024,384]{1,0:T(8,128)(2,1)S(1)} %copy-done.16, ...), custom_call_target="tpu_custom_call" | custom-call | flops 20000000000 | bytes 1 | tf_op jit(solution)/shard_map/attention_back1/pallas_call | solution.py:182
  75.4 1.3 %collective-permute-start.9 = (bf16[384,384]{1,0:T(8,128)(2,1)S(1)}, bf16[384,384]{1,0:T(8,128)(2,1)S(1)}, u32[]{:S(2)}, u32[]{:S(2)}) collective-permute-start(bf16[384,384]{1,0:T(8,128)(2,1)S(1)} %get-tuple-element.143), channel_id=1, source_target_pairs={{0,2},{1,5},{2,0},{3,7},{4,6},{5,1},{6,4},{7,3},{8,10},{9,13},{10,... | collective-permute-start | bytes 884744 | tf_op jit(solution)/shard_map/ppermute | solution.py:776
  78.4 7.0 %attention_back2.1 = (bf16[1024,384]{1,0:T(8,128)(2,1)S(1)}, f32[8,384]{1,0:T(8,128)S(1)}, bf16[384,384]{1,0:T(8,128)(2,1)S(1)}, bf16[384,384]{1,0:T(8,128)(2,1)S(1)}) custom-call(s32[16]{0:T(128)S(1)} %get-tuple-element.179.refs_1_.refs_0_, bf16[1024,384]{1,0:T(8,128)(2,1)S(1)} %copy-done.17, bf16[1024,384]{1,0:T(8,128)(2,1)S(1)} %copy-done.16, ...), custom_call_target="tpu_custom_call" | custom-call | flops 20000000000 | bytes 1 | tf_op jit(solution)/shard_map/attention_back2/pallas_call | solution.py:182
  85.4 1.6 %collective-permute-start.12 = (bf16[384,384]{1,0:T(8,128)(2,1)S(1)}, bf16[384,384]{1,0:T(8,128)(2,1)S(1)}, u32[]{:S(2)}, u32[]{:S(2)}) collective-permute-start(bf16[384,384]{1,0:T(8,128)(2,1)S(1)} %get-tuple-element.154), channel_id=1, source_target_pairs={{0,2},{1,5},{2,0},{3,7},{4,6},{5,1},{6,4},{7,3},{8,10},{9,13},{10,... | collective-permute-start | bytes 884744 | tf_op jit(solution)/shard_map/ppermute | solution.py:776
  87.0 1.5 %collective-permute-done.8.refs_3_ = bf16[192,1536]{1,0:T(8,128)(2,1)S(1)} collective-permute-done((bf16[192,1536]{1,0:T(8,128)(2,1)S(1)}, bf16[192,1536]{1,0:T(8,128)(2,1)S(1)}, u32[]{:S(2)}, u32[]{:S(2)}) %collective-permute-start.8) | collective-permute-done | bytes 589856 | tf_op jit(solution)/shard_map/ppermute | solution.py:776
  88.5 0.8 fold.9
  89.3 2.7 %collective-permute-start.14 = (bf16[48,1536]{1,0:T(8,128)(2,1)S(1)}, bf16[48,1536]{1,0:T(8,128)(2,1)S(1)}, u32[]{:S(2)}, u32[]{:S(2)}) collective-permute-start(bf16[48,1536]{1,0:T(8,128)(2,1)S(1)} %get-tuple-element.145.refs_4_), channel_id=1, source_target_pairs={{0,16},{1,17},{2,18},{3,19},{4,20},{5,21},{6,22},{7,23},{8,24},{9,... | collective-permute-start | bytes 442376 | tf_op jit(solution)/shard_map/ppermute | solution.py:776
  92.0 1.0 collective-permute-start.11
  93.0 2.8 %first.1.refs_8_.refs_2_ = bf16[1024,768]{1,0:T(8,128)(2,1)S(1)} custom-call(bf16[1024,384]{1,0:T(8,128)(2,1)S(1)} %get-tuple-element.120.refs_0_, bf16[1024,384]{1,0:T(8,128)(2,1)S(1)} %get-tuple-element.128.refs_1_, bf16[1024,384]{1,0:T(8,128)(2,1)S(1)} %get-tuple-element.137.refs_2_, bf16[3,768,384]{2,1,0:T(8,128)(2,1)S(1)} %bitcast.5, ...), custom_call_target="tpu_custom_call" | custom-call | flops 20000000000 | bytes 1 | tf_op jit(solution)/shard_map/first/pallas_call | solution.py:182
  96.1 1.1 collective-permute-start.16
  97.2 1.5 %collective-permute-done.11.refs_1_ = bf16[96,1536]{1,0:T(8,128)(2,1)S(1)} collective-permute-done((bf16[96,1536]{1,0:T(8,128)(2,1)S(1)}, bf16[96,1536]{1,0:T(8,128)(2,1)S(1)}, u32[]{:S(2)}, u32[]{:S(2)}) %collective-permute-start.11) | collective-permute-done | bytes 294944 | tf_op jit(solution)/shard_map/ppermute | solution.py:776
  100.2 1.0 copy-done.10
  101.2 4.4 %last.1 = (f32[1024,768]{1,0:T(8,128)}, f32[16,768]{1,0:T(8,128)S(1)}) custom-call(f32[768]{0:T(1024)} %refs_0_.11, bf16[1024,768]{1,0:T(8,128)(2,1)S(1)} %copy-done.3, bf16[1024,768]{1,0:T(8,128)(2,1)S(1)} %first.1.refs_8_.refs_2_, bf16[1024,768]{1,0:T(8,128)(2,1)S(1)} %collective-permute-done.10.refs_3_, f32[1024,768]{1,0:T(8,128)S(1)} %copy-done.10, ...), custom_call_target="tpu_custom_call" | custom-call | flops 20000000000 | bytes 1 | tf_op jit(solution)/shard_map/last/pallas_call | solution.py:182
  105.6 1.3 %collective-permute-start.13 = (f32[16,768]{1,0:T(8,128)S(1)}, f32[16,768]{1,0:T(8,128)S(1)}, u32[]{:S(2)}, u32[]{:S(2)}) collective-permute-start(f32[16,768]{1,0:T(8,128)S(1)} %get-tuple-element.157.refs_2_.refs_0_), channel_id=1, source_target_pairs={{0,2},{2,0},{4,6},{6,4},{8,10},{10,8},{12,14},{14,12},{16,18},{18,... | collective-permute-start | bytes 147464 | tf_op jit(solution)/shard_map/ppermute | solution.py:763
  108.1 1.8 %final.2 = (f32[48,1536]{1,0:T(8,128)}, f32[48,1536]{1,0:T(8,128)}) custom-call(f32[48,1536]{1,0:T(8,128)} %get-tuple-element.158.refs_0_, bf16[48,1536]{1,0:T(8,128)(2,1)S(1)} %collective-permute-done.14.refs_1_, f32[48,1536]{1,0:T(8,128)} %get-tuple-element.159.refs_2_, bf16[48,1536]{1,0:T(8,128)(2,1)S(1)} %collective-permute-done.15.refs_3_, ...), custom_call_target="tpu_custom_call" | custom-call | bytes 1 | tf_op jit(solution)/shard_map/final/pallas_call | solution.py:182
  110.0 1.1 collective-permute-start.18
  111.1 3.1 %down.1.refs_2_.refs_5_ = bf16[1024,768]{1,0:T(8,128)(2,1)S(1)} custom-call(bf16[1536,768]{1,0:T(8,128)(2,1)S(1)} %copy-done, bf16[1024,1536]{1,0:T(8,128)(2,1)S(1)} %copy-done.9, f32[16,768]{1,0:T(8,128)S(1)} %add.63.refs_2_.refs_0_), custom_call_target="tpu_custom_call" | custom-call | flops 20000000000 | bytes 1 | tf_op jit(solution)/shard_map/down/pallas_call | solution.py:182
  116.2 1.5 %collective-permute-start.20 = (f32[16,768]{1,0:T(8,128)S(1)}, f32[16,768]{1,0:T(8,128)S(1)}, u32[]{:S(2)}, u32[]{:S(2)}) collective-permute-start(f32[16,768]{1,0:T(8,128)S(1)} %add.64.refs_7_.refs_0_), channel_id=1, source_target_pairs={{0,8},{2,10},{4,12},{6,14},{8,0},{10,2},{12,4},{14,6},{16,24},{18,... | collective-permute-start | bytes 147464 | tf_op jit(solution)/shard_map/ppermute | solution.py:763
  117.7 3.9 %output.1.refs_2_ = bf16[1024,768]{1,0:T(8,128)(2,1)} custom-call(f32[768]{0:T(1024)} %refs_0_.13, f32[768]{0:T(1024)} %refs_1_.7, bf16[1024,768]{1,0:T(8,128)(2,1)} %refs_2_.9, bf16[1024,768]{1,0:T(8,128)(2,1)} %copy-done.4, bf16[1024,768]{1,0:T(8,128)(2,1)} %copy-done.5, bf16[1024,768]{1,0:T(8,128)(2,1)S(1)} %down.1.refs_2_.refs_5_, ...), custom_call_target="tpu_custom_call" | custom-call | flops 20000000000 | bytes 1 | tf_op jit(solution)/shard_map/output/pallas_call | solution.py:182
  121.6 2.7 %collective-permute-start.21 = (f32[16,768]{1,0:T(8,128)S(1)}, f32[16,768]{1,0:T(8,128)S(1)}, u32[]{:S(2)}, u32[]{:S(2)}) collective-permute-start(f32[16,768]{1,0:T(8,128)S(1)} %add.65.refs_2_.refs_0_), channel_id=1, source_target_pairs={{0,16},{2,18},{4,20},{6,22},{8,24},{10,26},{12,28},{14,30},{16,0},... | collective-permute-start | bytes 147464 | tf_op jit(solution)/shard_map/ppermute | solution.py:763
  124.3 1.2 collective-permute-done.22.refs_1_
  125.5 1.7 %final.3 = (f32[3,48,384]{2,1,0:T(8,128)}, f32[48,384]{1,0:T(8,128)}) custom-call(f32[48,1536]{1,0:T(8,128)} %get-tuple-element.166.refs_0_, bf16[48,1536]{1,0:T(8,128)(2,1)S(1)} %collective-permute-done.22.refs_1_, f32[16,768]{1,0:T(8,128)S(1)} %add.65.refs_2_.refs_0_), custom_call_target="tpu_custom_call" | custom-call | flops 20000000000 | bytes 1 | tf_op jit(solution)/shard_map/final/pallas_call | solution.py:182
  (96 shorter events, 9.9 us)
Async XLA Ops:
  1.3 18.4 %copy-start.8 = (s32[1,16]{1,0:T(1,128)S(1)}, s32[1,16]{1,0:T(1,128)}, u32[]{:S(2)}) copy-start(s32[1,16]{1,0:T(1,128)} %refs_0_.10) | copy-start | bytes 196
  19.1 6.6 %collective-permute-start = (bf16[1024,768]{1,0:T(8,128)(2,1)S(1)}, bf16[1024,768]{1,0:T(8,128)(2,1)S(1)}, u32[]{:S(2)}, u32[]{:S(2)}) collective-permute-start(bf16[1024,768]{1,0:T(8,128)(2,1)S(1)} %get-tuple-element.96.refs_4_.refs_3_), channel_id=1, source_target_pairs={{0,1},{1,0},{2,3},{3,2},{4,5},{5,4},{6,7},{7,6},{8,9},{9,8},{10,11... | collective-permute-start | bytes 4718600 | tf_op jit(solution)/shard_map/ppermute | solution.py:763
  25.7 13.2 %copy-start.26 = (f32[1,768]{1,0:T(1,128)}, f32[1,768]{1,0:T(1,128)S(1)}, u32[]{:S(2)}) copy-start(f32[1,768]{1,0:T(1,128)S(1)} %get-tuple-element.102.refs_10_.refs_6_) | copy-start | bytes 9220
  25.7 13.2 %copy-start.5 = (bf16[1024,768]{1,0:T(8,128)(2,1)}, bf16[1024,768]{1,0:T(8,128)(2,1)S(1)}, u32[]{:S(2)}) copy-start(bf16[1024,768]{1,0:T(8,128)(2,1)S(1)} %collective-permute-done.refs_5_.refs_4_) | copy-start | bytes 4718596
  38.9 26.8 %collective-permute-start.2 = (bf16[384,1536]{1,0:T(8,128)(2,1)S(1)}, bf16[384,1536]{1,0:T(8,128)(2,1)S(1)}, u32[]{:S(2)}, u32[]{:S(2)}) collective-permute-start(bf16[384,1536]{1,0:T(8,128)(2,1)S(1)} %get-tuple-element.123), channel_id=1, source_target_pairs={{0,2},{1,5},{2,0},{3,7},{4,6},{5,1},{6,4},{7,3},{8,10},{9,13},{10,... | collective-permute-start | bytes 3538952 | tf_op jit(solution)/shard_map/ppermute | solution.py:776
  41.5 6.0 %collective-permute-start.1 = (bf16[1024,768]{1,0:T(8,128)(2,1)S(1)}, bf16[1024,768]{1,0:T(8,128)(2,1)S(1)}, u32[]{:S(2)}, u32[]{:S(2)}) collective-permute-start(bf16[1024,768]{1,0:T(8,128)(2,1)S(1)} %get-tuple-element.108.refs_3_), channel_id=1, source_target_pairs={{0,1},{1,0},{2,3},{3,2},{4,5},{5,4},{6,7},{7,6},{8,9},{9,8},{10,11... | collective-permute-start | bytes 4718600 | tf_op jit(solution)/shard_map/ppermute | solution.py:763
  45.8 10.1 %copy-start.22 = (f32[8,1536]{1,0:T(8,128)}, f32[8,1536]{1,0:T(8,128)S(1)}, u32[]{:S(2)}) copy-start(f32[8,1536]{1,0:T(8,128)S(1)} %get-tuple-element.115.refs_11_.refs_7_) | copy-start | bytes 147460
  45.8 30.8 %collective-permute-start.5 = (bf16[384,1536]{1,0:T(8,128)(2,1)S(1)}, bf16[384,1536]{1,0:T(8,128)(2,1)S(1)}, u32[]{:S(2)}, u32[]{:S(2)}) collective-permute-start(bf16[384,1536]{1,0:T(8,128)(2,1)S(1)} %get-tuple-element.132), channel_id=1, source_target_pairs={{0,8},{1,9},{2,10},{3,11},{4,12},{5,13},{6,14},{7,15},{8,0},{9,1},... | collective-permute-start | bytes 3538952 | tf_op jit(solution)/shard_map/ppermute | solution.py:776
  47.5 9.9 %copy-start.14 = (bf16[1024,768]{1,0:T(8,128)(2,1)S(1)}, bf16[1024,768]{1,0:T(8,128)(2,1)}, u32[]{:S(2)}) copy-start(bf16[1024,768]{1,0:T(8,128)(2,1)} %get-tuple-element.118.refs_8_) | copy-start | bytes 4718596
  47.6 9.9 %copy-start.16 = (bf16[1024,384]{1,0:T(8,128)(2,1)S(1)}, bf16[1024,384]{1,0:T(8,128)(2,1)}, u32[]{:S(2)}) copy-start(bf16[1024,384]{1,0:T(8,128)(2,1)} %get-tuple-element.105.refs_2_) | copy-start | bytes 2359300
  47.6 9.9 %copy-start.17 = (bf16[1024,384]{1,0:T(8,128)(2,1)S(1)}, bf16[1024,384]{1,0:T(8,128)(2,1)}, u32[]{:S(2)}) copy-start(bf16[1024,384]{1,0:T(8,128)(2,1)} %get-tuple-element.104.refs_1_) | copy-start | bytes 2359300
  47.6 9.9 %copy-start.18 = (bf16[1024,384]{1,0:T(8,128)(2,1)S(1)}, bf16[1024,384]{1,0:T(8,128)(2,1)}, u32[]{:S(2)}) copy-start(bf16[1024,384]{1,0:T(8,128)(2,1)} %get-tuple-element.106.refs_3_) | copy-start | bytes 2359300
  55.9 9.8 %collective-permute-start.3 = (bf16[384,384]{1,0:T(8,128)(2,1)S(1)}, bf16[384,384]{1,0:T(8,128)(2,1)S(1)}, u32[]{:S(2)}, u32[]{:S(2)}) collective-permute-start(bf16[384,384]{1,0:T(8,128)(2,1)S(1)} %get-tuple-element.125), channel_id=1, source_target_pairs={{0,2},{1,5},{2,0},{3,7},{4,6},{5,1},{6,4},{7,3},{8,10},{9,13},{10,... | collective-permute-start | bytes 884744 | tf_op jit(solution)/shard_map/ppermute | solution.py:776
  65.1 11.6 %collective-permute-start.6 = (bf16[384,384]{1,0:T(8,128)(2,1)S(1)}, bf16[384,384]{1,0:T(8,128)(2,1)S(1)}, u32[]{:S(2)}, u32[]{:S(2)}) collective-permute-start(bf16[384,384]{1,0:T(8,128)(2,1)S(1)} %get-tuple-element.134), channel_id=1, source_target_pairs={{0,2},{1,5},{2,0},{3,7},{4,6},{5,1},{6,4},{7,3},{8,10},{9,13},{10,... | collective-permute-start | bytes 884744 | tf_op jit(solution)/shard_map/ppermute | solution.py:776
  66.0 10.9 %collective-permute-start.4 = (bf16[192,1536]{1,0:T(8,128)(2,1)S(1)}, bf16[192,1536]{1,0:T(8,128)(2,1)S(1)}, u32[]{:S(2)}, u32[]{:S(2)}) collective-permute-start(bf16[192,1536]{1,0:T(8,128)(2,1)S(1)} %get-tuple-element.130), channel_id=1, source_target_pairs={{0,4},{1,3},{2,6},{3,1},{4,0},{5,7},{6,2},{7,5},{8,12},{9,11},{10,... | collective-permute-start | bytes 1769480 | tf_op jit(solution)/shard_map/ppermute | solution.py:776
  75.4 11.6 %collective-permute-start.9 = (bf16[384,384]{1,0:T(8,128)(2,1)S(1)}, bf16[384,384]{1,0:T(8,128)(2,1)S(1)}, u32[]{:S(2)}, u32[]{:S(2)}) collective-permute-start(bf16[384,384]{1,0:T(8,128)(2,1)S(1)} %get-tuple-element.143), channel_id=1, source_target_pairs={{0,2},{1,5},{2,0},{3,7},{4,6},{5,1},{6,4},{7,3},{8,10},{9,13},{10,... | collective-permute-start | bytes 884744 | tf_op jit(solution)/shard_map/ppermute | solution.py:776
  77.4 9.6 %collective-permute-start.7 = (bf16[96,1536]{1,0:T(8,128)(2,1)S(1)}, bf16[96,1536]{1,0:T(8,128)(2,1)S(1)}, u32[]{:S(2)}, u32[]{:S(2)}) collective-permute-start(bf16[96,1536]{1,0:T(8,128)(2,1)S(1)} %get-tuple-element.139), channel_id=1, source_target_pairs={{0,8},{1,9},{2,10},{3,11},{4,12},{5,13},{6,14},{7,15},{8,0},{9,1},... | collective-permute-start | bytes 884744 | tf_op jit(solution)/shard_map/ppermute | solution.py:776
  77.9 10.6 %collective-permute-start.8 = (bf16[192,1536]{1,0:T(8,128)(2,1)S(1)}, bf16[192,1536]{1,0:T(8,128)(2,1)S(1)}, u32[]{:S(2)}, u32[]{:S(2)}) collective-permute-start(bf16[192,1536]{1,0:T(8,128)(2,1)S(1)} %get-tuple-element.141), channel_id=1, source_target_pairs={{0,2},{1,5},{2,0},{3,7},{4,6},{5,1},{6,4},{7,3},{8,10},{9,13},{10,... | collective-permute-start | bytes 1769480 | tf_op jit(solution)/shard_map/ppermute | solution.py:776
  85.4 10.6 %collective-permute-start.12 = (bf16[384,384]{1,0:T(8,128)(2,1)S(1)}, bf16[384,384]{1,0:T(8,128)(2,1)S(1)}, u32[]{:S(2)}, u32[]{:S(2)}) collective-permute-start(bf16[384,384]{1,0:T(8,128)(2,1)S(1)} %get-tuple-element.154), channel_id=1, source_target_pairs={{0,2},{1,5},{2,0},{3,7},{4,6},{5,1},{6,4},{7,3},{8,10},{9,13},{10,... | collective-permute-start | bytes 884744 | tf_op jit(solution)/shard_map/ppermute | solution.py:776
  89.3 18.1 %collective-permute-start.14 = (bf16[48,1536]{1,0:T(8,128)(2,1)S(1)}, bf16[48,1536]{1,0:T(8,128)(2,1)S(1)}, u32[]{:S(2)}, u32[]{:S(2)}) collective-permute-start(bf16[48,1536]{1,0:T(8,128)(2,1)S(1)} %get-tuple-element.145.refs_4_), channel_id=1, source_target_pairs={{0,16},{1,17},{2,18},{3,19},{4,20},{5,21},{6,22},{7,23},{8,24},{9,... | collective-permute-start | bytes 442376 | tf_op jit(solution)/shard_map/ppermute | solution.py:776
  92.0 6.7 %collective-permute-start.11 = (bf16[96,1536]{1,0:T(8,128)(2,1)S(1)}, bf16[96,1536]{1,0:T(8,128)(2,1)S(1)}, u32[]{:S(2)}, u32[]{:S(2)}) collective-permute-start(bf16[96,1536]{1,0:T(8,128)(2,1)S(1)} %get-tuple-element.148), channel_id=1, source_target_pairs={{0,4},{1,3},{2,6},{3,1},{4,0},{5,7},{6,2},{7,5},{8,12},{9,11},{10,... | collective-permute-start | bytes 884744 | tf_op jit(solution)/shard_map/ppermute | solution.py:776
  95.9 4.0 %collective-permute-start.10 = (bf16[1024,768]{1,0:T(8,128)(2,1)S(1)}, bf16[1024,768]{1,0:T(8,128)(2,1)S(1)}, u32[]{:S(2)}, u32[]{:S(2)}) collective-permute-start(bf16[1024,768]{1,0:T(8,128)(2,1)S(1)} %first.1.refs_8_.refs_2_), channel_id=1, source_target_pairs={{0,1},{1,0},{2,3},{3,2},{4,5},{5,4},{6,7},{7,6},{8,9},{9,8},{10,11... | collective-permute-start | bytes 4718600 | tf_op jit(solution)/shard_map/ppermute | solution.py:763
  96.1 10.7 %collective-permute-start.16 = (bf16[192,1536]{1,0:T(8,128)(2,1)S(1)}, bf16[192,1536]{1,0:T(8,128)(2,1)S(1)}, u32[]{:S(2)}, u32[]{:S(2)}) collective-permute-start(bf16[192,1536]{1,0:T(8,128)(2,1)S(1)} %get-tuple-element.155.refs_2_), channel_id=1, source_target_pairs={{0,4},{1,3},{2,6},{3,1},{4,0},{5,7},{6,2},{7,5},{8,12},{9,11},{10,... | collective-permute-start | bytes 1769480 | tf_op jit(solution)/shard_map/ppermute | solution.py:776
  99.5 8.7 %collective-permute-start.15 = (bf16[48,1536]{1,0:T(8,128)(2,1)S(1)}, bf16[48,1536]{1,0:T(8,128)(2,1)S(1)}, u32[]{:S(2)}, u32[]{:S(2)}) collective-permute-start(bf16[48,1536]{1,0:T(8,128)(2,1)S(1)} %get-tuple-element.156.refs_11_), channel_id=1, source_target_pairs={{0,16},{1,17},{2,18},{3,19},{4,20},{5,21},{6,22},{7,23},{8,24},{9,... | collective-permute-start | bytes 442376 | tf_op jit(solution)/shard_map/ppermute | solution.py:776
  101.2 9.9 %copy-start.9 = (bf16[1024,1536]{1,0:T(8,128)(2,1)S(1)}, bf16[1024,1536]{1,0:T(8,128)(2,1)}, u32[]{:S(2)}) copy-start(bf16[1024,1536]{1,0:T(8,128)(2,1)} %get-tuple-element.103.refs_1_) | copy-start | bytes 9437188
  105.6 4.4 %collective-permute-start.13 = (f32[16,768]{1,0:T(8,128)S(1)}, f32[16,768]{1,0:T(8,128)S(1)}, u32[]{:S(2)}, u32[]{:S(2)}) collective-permute-start(f32[16,768]{1,0:T(8,128)S(1)} %get-tuple-element.157.refs_2_.refs_0_), channel_id=1, source_target_pairs={{0,2},{2,0},{4,6},{6,4},{8,10},{10,8},{12,14},{14,12},{16,18},{18,... | collective-permute-start | bytes 147464 | tf_op jit(solution)/shard_map/ppermute | solution.py:763
  107.0 7.8 %collective-permute-start.19 = (bf16[96,1536]{1,0:T(8,128)(2,1)S(1)}, bf16[96,1536]{1,0:T(8,128)(2,1)S(1)}, u32[]{:S(2)}, u32[]{:S(2)}) collective-permute-start(bf16[96,1536]{1,0:T(8,128)(2,1)S(1)} %get-tuple-element.161.refs_4_), channel_id=1, source_target_pairs={{0,8},{1,9},{2,10},{3,11},{4,12},{5,13},{6,14},{7,15},{8,0},{9,1},... | collective-permute-start | bytes 884744 | tf_op jit(solution)/shard_map/ppermute | solution.py:776
  110.0 6.2 %collective-permute-start.18 = (f32[16,768]{1,0:T(8,128)S(1)}, f32[16,768]{1,0:T(8,128)S(1)}, u32[]{:S(2)}, u32[]{:S(2)}) collective-permute-start(f32[16,768]{1,0:T(8,128)S(1)} %add.63.refs_2_.refs_0_), channel_id=1, source_target_pairs={{0,4},{2,6},{4,0},{6,2},{8,12},{10,14},{12,8},{14,10},{16,20},{18,... | collective-permute-start | bytes 147464 | tf_op jit(solution)/shard_map/ppermute | solution.py:763
  114.2 3.5 %collective-permute-start.17 = (bf16[1024,768]{1,0:T(8,128)(2,1)S(1)}, bf16[1024,768]{1,0:T(8,128)(2,1)S(1)}, u32[]{:S(2)}, u32[]{:S(2)}) collective-permute-start(bf16[1024,768]{1,0:T(8,128)(2,1)S(1)} %down.1.refs_2_.refs_5_), channel_id=1, source_target_pairs={{0,1},{1,0},{2,3},{3,2},{4,5},{5,4},{6,7},{7,6},{8,9},{9,8},{10,11... | collective-permute-start | bytes 4718600 | tf_op jit(solution)/shard_map/ppermute | solution.py:763
  115.5 10.0 %collective-permute-start.22 = (bf16[48,1536]{1,0:T(8,128)(2,1)S(1)}, bf16[48,1536]{1,0:T(8,128)(2,1)S(1)}, u32[]{:S(2)}, u32[]{:S(2)}) collective-permute-start(bf16[48,1536]{1,0:T(8,128)(2,1)S(1)} %get-tuple-element.164.refs_2_), channel_id=1, source_target_pairs={{0,16},{1,17},{2,18},{3,19},{4,20},{5,21},{6,22},{7,23},{8,24},{9,... | collective-permute-start | bytes 442376 | tf_op jit(solution)/shard_map/ppermute | solution.py:776
  116.2 5.4 %collective-permute-start.20 = (f32[16,768]{1,0:T(8,128)S(1)}, f32[16,768]{1,0:T(8,128)S(1)}, u32[]{:S(2)}, u32[]{:S(2)}) collective-permute-start(f32[16,768]{1,0:T(8,128)S(1)} %add.64.refs_7_.refs_0_), channel_id=1, source_target_pairs={{0,8},{2,10},{4,12},{6,14},{8,0},{10,2},{12,4},{14,6},{16,24},{18,... | collective-permute-start | bytes 147464 | tf_op jit(solution)/shard_map/ppermute | solution.py:763
  121.6 5.6 %collective-permute-start.21 = (f32[16,768]{1,0:T(8,128)S(1)}, f32[16,768]{1,0:T(8,128)S(1)}, u32[]{:S(2)}, u32[]{:S(2)}) collective-permute-start(f32[16,768]{1,0:T(8,128)S(1)} %add.65.refs_2_.refs_0_), channel_id=1, source_target_pairs={{0,16},{2,18},{4,20},{6,22},{8,24},{10,26},{12,28},{14,30},{16,0},... | collective-permute-start | bytes 147464 | tf_op jit(solution)/shard_map/ppermute | solution.py:763
  (19 other events, 92.6 us)
